TPU v7x, 32 devices: a whole 2x2x4 slice. The times are simulated.
32 devices in a mesh: grp: 4 (over y, x), dp: 8 (over z, core).
Axes of the slice: x: 2, y: 2, z: 4, core: 2. Of those that a mesh axis runs over, the one named last changes fastest.
Arguments:
- pixels: bfloat16 [4, 64, 256, 1024], P('grp', 'dp'), may hold values from -6 to 6
- keep_index: int32 [4, 64, 64], P('grp', 'dp'), may hold values from 0 to 255, as said below
- band_group: int32 [4, 64, 256], P('grp', 'dp'), may hold values from 0 to 3, as said below
- gsd_index: int32 [4, 64, 256], P('grp', 'dp'), may hold values from 0 to 511
- gsd_table: float32 [4, 512, 1536], P('grp'), may hold values from -4 to 4
- group_items: int32 [4], P('grp'), may hold values from 32 to 64, as said below
- step_count: int32 [1], replicated, may hold values from 2 to 20
- enc_cols: float32 [1024, 8192], P('dp'), may hold values from -0.1875 to 0.1875
- enc_rows: float32 [8192, 1024], P('dp'), may hold values from -0.09375 to 0.09375
- dec_cols: float32 [512, 4096], P('dp'), may hold values from -0.25 to 0.25
- dec_rows: float32 [4096, 512], P('dp'), may hold values from -0.1875 to 0.1875
- enc_gains: float32 [6, 1024], replicated
- dec_gains: float32 [7, 512], replicated
- moment_ecols: float32 [1024, 8192], P('dp'), may hold values from -1.5258789e-05 to 1.5258789e-05
- moment_erows: float32 [8192, 1024], P('dp'), may hold values from -1.5258789e-05 to 1.5258789e-05
- moment_dcols: float32 [512, 4096], P('dp'), may hold values from -1.5258789e-05 to 1.5258789e-05
- moment_drows: float32 [4096, 512], P('dp'), may hold values from -1.5258789e-05 to 1.5258789e-05
- moment_egains: float32 [6, 1024], replicated, may hold values from -3.0517578e-05 to 3.0517578e-05
- moment_dgains: float32 [7, 512], replicated, may hold values from -3.0517578e-05 to 3.0517578e-05
- square_ecols: float32 [1024, 8192], P('dp'), may hold values from 1.1915401e-12 to 4.7661606e-12
- square_erows: float32 [8192, 1024], P('dp'), may hold values from 1.1915401e-12 to 4.7661606e-12
- square_dcols: float32 [512, 4096], P('dp'), may hold values from 1.1915401e-12 to 4.7661606e-12
- square_drows: float32 [4096, 512], P('dp'), may hold values from 1.1915401e-12 to 4.7661606e-12
- square_egains: float32 [6, 1024], replicated, may hold values from 2.3830803e-12 to 9.532321e-12
- square_dgains: float32 [7, 512], replicated, may hold values from 2.3830803e-12 to 9.532321e-12
Outputs:
- clipped_ecols: float32 [1024, 8192], P('dp')
- squares_ecols: float32 [1024, 8192], P('dp')
- updated_ecols: float32 [1024, 8192], P('dp')
- clipped_erows: float32 [8192, 1024], P('dp')
- squares_erows: float32 [8192, 1024], P('dp')
- updated_erows: float32 [8192, 1024], P('dp')
- clipped_dcols: float32 [512, 4096], P('dp')
- squares_dcols: float32 [512, 4096], P('dp')
- updated_dcols: float32 [512, 4096], P('dp')
- clipped_drows: float32 [4096, 512], P('dp')
- squares_drows: float32 [4096, 512], P('dp')
- updated_drows: float32 [4096, 512], P('dp')
- clipped_egains: float32 [6, 1024], replicated
- squares_egains: float32 [6, 1024], replicated
- updated_egains: float32 [6, 1024], replicated
- clipped_dgains: float32 [7, 512], replicated
- squares_dgains: float32 [7, 512], replicated
- updated_dgains: float32 [7, 512], replicated
- loss: float32 [], replicated
- grad_norm: float32 [], replicated
Inputs may be any that keep to these rules, and one draw needn't show every extreme that they name: `keep_index`: each item's 64 entries are distinct patch positions. `band_group`: in groups of odd index every entry is 3. `group_items`: one group uses all 64 slots and another group 64 // 2.
All inputs are finite; a program needn't handle non-finite values.
Results may differ from a plain program's by a relative error of at most 0.017.
Values may be sent and summed in bfloat16 or wider, within the bound.
A program may use at most 384 MiB of HBM per device.

v0:
```python
import jax
import jax.numpy as jnp
from jax import lax
from jax.sharding import PartitionSpec as P

D = 1024
HEADS = 16
FF = 4096
DHEADS = 16
DFF = 2048
PIX = 1024
NBG = 4
L = 256
K = 64


norm_eps = 1e-06
clip_level = 0.005
learn_rate = 0.02
gain_rate = 0.25
weight_decay = 0.05
adam_eps = 1e-08
beta_first = 0.5
beta_second = 0.5


def to_low(value):
    return value.astype(jnp.bfloat16)


def project(inputs, matrix):
    return jnp.einsum("...n,nm->...m", inputs, matrix, preferred_element_type=jnp.float32)


def project_back(grads, matrix):
    return jnp.einsum("...m,nm->...n", grads, matrix, preferred_element_type=jnp.float32)


def weight_grad(inputs, grads):
    flat_in = inputs.reshape(-1, inputs.shape[-1])
    flat_grad = grads.reshape(-1, grads.shape[-1])
    return lax.dot_general(
        flat_in, flat_grad, (((0,), (0,)), ((), ())), preferred_element_type=jnp.float32
    )


def norm_forward(values, gain, shift):
    centred = values - jnp.mean(values, -1, keepdims=True)
    scaled = lax.rsqrt(jnp.mean(centred * centred, -1, keepdims=True) + norm_eps)
    normed = centred * scaled
    return (normed * gain + shift, normed, scaled)


def norm_backward(grads, normed, scaled, gain):
    inner = grads * gain
    back = scaled * (
        inner
        - jnp.mean(inner, -1, keepdims=True)
        - normed * jnp.mean(inner * normed, -1, keepdims=True)
    )
    flat_grad = grads.reshape(-1, grads.shape[-1])
    flat_norm = normed.reshape(-1, normed.shape[-1])
    return (back, jnp.sum(flat_grad * flat_norm, 0), jnp.sum(flat_grad, 0))


def gelu_parts(hidden):
    cumul = 0.5 * (1.0 + jax.scipy.special.erf(hidden * 0.7071067811865476))
    return (hidden * cumul, cumul + hidden * jnp.exp(-0.5 * hidden * hidden) * 0.3989422804014327)


def split_heads(packed, width, heads):
    shape = (packed.shape[0], packed.shape[1], heads, width // heads)
    return (
        packed[..., :width].reshape(shape),
        packed[..., width : 2 * width].reshape(shape),
        packed[..., 2 * width :].reshape(shape),
    )


def head_scores(queries, key_part, scale):
    return (
        jnp.einsum("bqhe,bkhe->bhqk", queries, key_part, preferred_element_type=jnp.float32) * scale
    )


def block_forward(inputs, columns, down_rows, gains, heads):
    width = inputs.shape[-1]
    scale = (width // heads) ** (-0.5)
    normed_one, hat_one, scale_one = norm_forward(inputs, gains[0], gains[1])
    first_in = to_low(normed_one)
    packed = to_low(project(first_in, columns[:, : 3 * width]))
    queries, key_part, val_part = split_heads(packed, width, heads)
    scores = head_scores(queries, key_part, scale)
    log_total = jax.nn.logsumexp(scores, -1, keepdims=True)
    attn_prob = to_low(jnp.exp(scores - log_total))
    mixed = jnp.einsum("bhqk,bkhe->bqhe", attn_prob, val_part, preferred_element_type=jnp.float32)
    mixed = to_low(mixed.reshape(inputs.shape))
    middle = inputs + project(mixed, columns[:, 3 * width : 4 * width])
    normed_two, hat_two, scale_two = norm_forward(middle, gains[2], gains[3])
    second_in = to_low(normed_two)
    hidden = project(second_in, columns[:, 4 * width :])
    activated = to_low(gelu_parts(hidden)[0])
    output = middle + project(activated, down_rows)
    saved = (
        hat_one,
        scale_one,
        first_in,
        packed,
        log_total,
        mixed,
        hat_two,
        scale_two,
        second_in,
        hidden,
        activated,
    )
    return (output, saved)


def block_backward(grad_out, columns, down_rows, gains, heads, saved):
    (
        hat_one,
        scale_one,
        first_in,
        packed,
        log_total,
        mixed,
        hat_two,
        scale_two,
        second_in,
        hidden,
        activated,
    ) = saved
    width = grad_out.shape[-1]
    scale = (width // heads) ** (-0.5)
    grad_low = to_low(grad_out)
    grad_down = weight_grad(activated, grad_low)
    grad_hidden = to_low(project_back(grad_low, down_rows) * gelu_parts(hidden)[1])
    grad_up = weight_grad(second_in, grad_hidden)
    back_two, gain_two, shift_two = norm_backward(
        project_back(grad_hidden, columns[:, 4 * width :]), hat_two, scale_two, gains[2]
    )
    grad_middle = grad_out + back_two
    middle_low = to_low(grad_middle)
    grad_proj = weight_grad(mixed, middle_low)
    head_shape = packed.shape[:2] + (heads, width // heads)
    grad_mixed = to_low(
        project_back(middle_low, columns[:, 3 * width : 4 * width]).reshape(head_shape)
    )
    queries, key_part, val_part = split_heads(packed, width, heads)
    attn_prob = jnp.exp(head_scores(queries, key_part, scale) - log_total)
    grad_prob = jnp.einsum(
        "bqhe,bkhe->bhqk", grad_mixed, val_part, preferred_element_type=jnp.float32
    )
    grad_val = jnp.einsum(
        "bhqk,bqhe->bkhe", to_low(attn_prob), grad_mixed, preferred_element_type=jnp.float32
    )
    grad_score = to_low(attn_prob * (grad_prob - jnp.sum(grad_prob * attn_prob, -1, keepdims=True)))
    grad_query = (
        jnp.einsum("bhqk,bkhe->bqhe", grad_score, key_part, preferred_element_type=jnp.float32)
        * scale
    )
    grad_key = (
        jnp.einsum("bhqk,bqhe->bkhe", grad_score, queries, preferred_element_type=jnp.float32)
        * scale
    )
    flat_shape = packed.shape[:2] + (width,)
    grad_packed = to_low(
        jnp.concatenate(
            [
                grad_query.reshape(flat_shape),
                grad_key.reshape(flat_shape),
                grad_val.reshape(flat_shape),
            ],
            -1,
        )
    )
    grad_qkv = weight_grad(first_in, grad_packed)
    back_one, gain_one, shift_one = norm_backward(
        project_back(grad_packed, columns[:, : 3 * width]), hat_one, scale_one, gains[0]
    )
    grad_in = grad_middle + back_one
    grad_cols = jnp.concatenate([grad_qkv, grad_proj, grad_up], 1)
    grad_gains = jnp.stack([gain_one, shift_one, gain_two, shift_two])
    return (grad_in, grad_cols, grad_down, grad_gains)


def adam_step(master, moment, square, grad, factor, fix_one, fix_two, decay, rate):
    clipped = grad * factor
    moment_new = beta_first * moment + (1.0 - beta_first) * clipped
    square_new = beta_second * square + (1.0 - beta_second) * clipped * clipped
    direction = moment_new / fix_one / (jnp.sqrt(square_new / fix_two) + adam_eps) + decay * master
    return (clipped, square_new, master - rate * direction)


def body(
    pixels,
    keep_index,
    band_group,
    gsd_index,
    gsd_table,
    group_items,
    step_count,
    enc_cols,
    enc_rows,
    dec_cols,
    dec_rows,
    enc_gains,
    dec_gains,
    moment_ecols,
    moment_erows,
    moment_dcols,
    moment_drows,
    moment_egains,
    moment_dgains,
    square_ecols,
    square_erows,
    square_dcols,
    square_drows,
    square_egains,
    square_dgains,
):
    total_count = lax.psum(jnp.sum(group_items.astype(jnp.float32)), "grp")
    masked = total_count * (L - K)
    copies = (
        lax.all_gather(to_low(enc_cols), "dp", axis=0, tiled=True),
        lax.all_gather(to_low(enc_rows), "dp", axis=0, tiled=True),
        lax.all_gather(to_low(dec_cols), "dp", axis=0, tiled=True),
        lax.all_gather(to_low(dec_rows), "dp", axis=0, tiled=True),
    )
    enc_copy = copies[0]
    enc_down = copies[1][:FF]
    embed_w = copies[1][FF:]
    dec_copy = copies[2]
    dec_down = copies[3][:DFF]
    dec_embed = copies[3][DFF : DFF + D]
    head_rows = copies[3][DFF + D :]
    pixel_rows = pixels[0]
    keep_rows = keep_index[0]
    batch = pixel_rows.shape[0]
    kept_pixels = jnp.take_along_axis(pixel_rows, keep_rows[..., None], 1)
    kept_bands = jnp.take_along_axis(band_group[0], keep_rows, 1)
    onehot = (kept_bands[..., None] == jnp.arange(NBG, dtype=jnp.int32)).astype(jnp.bfloat16)
    spread = (onehot[..., None] * kept_pixels[:, :, None, :]).reshape(batch, K, NBG * PIX)
    position = jnp.take(gsd_table[0], gsd_index[0], axis=0)
    enc_input = project(spread, embed_w) + jnp.take_along_axis(
        position[..., :D], keep_rows[..., None], 1
    )
    enc_out, enc_saved = block_forward(enc_input, enc_copy, enc_down, enc_gains, HEADS)
    enc_final, enc_hat, enc_scale = norm_forward(enc_out, enc_gains[4], enc_gains[5])
    enc_low = to_low(enc_final)
    latent = project(enc_low, dec_embed)
    item_rows = jnp.arange(batch)[:, None]
    hidden_mask = jnp.ones((batch, L), jnp.float32).at[item_rows, keep_rows].set(0.0)
    dec_input = hidden_mask[..., None] * dec_gains[6] + position[..., D:]
    dec_input = dec_input.at[item_rows, keep_rows].add(latent)
    dec_out, dec_saved = block_forward(dec_input, dec_copy, dec_down, dec_gains, DHEADS)
    dec_final, dec_hat, dec_scale = norm_forward(dec_out, dec_gains[4], dec_gains[5])
    dec_low = to_low(dec_final)
    predicted = project_back(dec_low, head_rows)
    pixel_float = pixel_rows.astype(jnp.float32)
    centred = pixel_float - jnp.mean(pixel_float, -1, keepdims=True)
    target = centred * lax.rsqrt(jnp.mean(centred * centred, -1, keepdims=True) + norm_eps)
    first_item = lax.axis_index("dp") * batch
    valid = (first_item + jnp.arange(batch, dtype=jnp.int32) < group_items[0]).astype(jnp.float32)
    token_weight = hidden_mask * valid[:, None]
    error = predicted - target
    loss_local = jnp.sum(token_weight * jnp.mean(error * error, -1))
    grad_pred = to_low(token_weight[..., None] * error * (2.0 / PIX) / masked)
    grad_head = weight_grad(grad_pred, dec_low)
    back_dec, gain_df, shift_df = norm_backward(
        project(grad_pred, head_rows), dec_hat, dec_scale, dec_gains[4]
    )
    grad_dec_in, grad_dcols, grad_ddown, dec_block_gains = block_backward(
        back_dec, dec_copy, dec_down, dec_gains, DHEADS, dec_saved
    )
    grad_token = jnp.sum(grad_dec_in * hidden_mask[..., None], (0, 1))
    grad_latent = to_low(jnp.take_along_axis(grad_dec_in, keep_rows[..., None], 1))
    grad_dembed = weight_grad(enc_low, grad_latent)
    back_enc, gain_ef, shift_ef = norm_backward(
        project_back(grad_latent, dec_embed), enc_hat, enc_scale, enc_gains[4]
    )
    grad_enc_in, grad_ecols, grad_edown, enc_block_gains = block_backward(
        back_enc, enc_copy, enc_down, enc_gains, HEADS, enc_saved
    )
    grad_embed = weight_grad(spread, to_low(grad_enc_in))
    grads = (
        grad_ecols,
        jnp.concatenate([grad_edown, grad_embed], 0),
        grad_dcols,
        jnp.concatenate([grad_ddown, grad_dembed, grad_head], 0),
    )
    grad_egains = jnp.concatenate([enc_block_gains, jnp.stack([gain_ef, shift_ef])], 0)
    grad_dgains = jnp.concatenate([dec_block_gains, jnp.stack([gain_df, shift_df, grad_token])], 0)
    shards = (
        lax.psum_scatter(grads[0], "dp", scatter_dimension=0, tiled=True),
        lax.psum_scatter(grads[1], "dp", scatter_dimension=0, tiled=True),
        lax.psum_scatter(grads[2], "dp", scatter_dimension=0, tiled=True),
        lax.psum_scatter(grads[3], "dp", scatter_dimension=0, tiled=True),
    )
    shards = (
        lax.psum(shards[0].astype(jnp.bfloat16), "grp").astype(jnp.float32),
        lax.psum(shards[1].astype(jnp.bfloat16), "grp").astype(jnp.float32),
        lax.psum(shards[2].astype(jnp.bfloat16), "grp").astype(jnp.float32),
        lax.psum(shards[3].astype(jnp.bfloat16), "grp").astype(jnp.float32),
    )
    enc_sum, dec_sum, loss_sum = lax.psum((grad_egains, grad_dgains, loss_local), ("grp", "dp"))
    shard_squares = lax.psum(sum((jnp.sum(piece * piece) for piece in shards)), "dp")
    loss = loss_sum / masked
    grad_norm = jnp.sqrt(shard_squares + jnp.sum(enc_sum * enc_sum) + jnp.sum(dec_sum * dec_sum))
    factor = clip_level / jnp.maximum(grad_norm, clip_level)
    count_steps = step_count[0].astype(jnp.float32)
    fix_one = 1.0 - beta_first**count_steps
    fix_two = 1.0 - beta_second**count_steps
    clipped_ecols, squares_ecols, updated_ecols = adam_step(
        enc_cols,
        moment_ecols,
        square_ecols,
        shards[0],
        factor,
        fix_one,
        fix_two,
        weight_decay,
        learn_rate,
    )
    clipped_erows, squares_erows, updated_erows = adam_step(
        enc_rows,
        moment_erows,
        square_erows,
        shards[1],
        factor,
        fix_one,
        fix_two,
        weight_decay,
        learn_rate,
    )
    clipped_dcols, squares_dcols, updated_dcols = adam_step(
        dec_cols,
        moment_dcols,
        square_dcols,
        shards[2],
        factor,
        fix_one,
        fix_two,
        weight_decay,
        learn_rate,
    )
    clipped_drows, squares_drows, updated_drows = adam_step(
        dec_rows,
        moment_drows,
        square_drows,
        shards[3],
        factor,
        fix_one,
        fix_two,
        weight_decay,
        learn_rate,
    )
    clipped_egains, squares_egains, updated_egains = adam_step(
        enc_gains, moment_egains, square_egains, enc_sum, factor, fix_one, fix_two, 0.0, gain_rate
    )
    clipped_dgains, squares_dgains, updated_dgains = adam_step(
        dec_gains, moment_dgains, square_dgains, dec_sum, factor, fix_one, fix_two, 0.0, gain_rate
    )
    return (
        clipped_ecols,
        squares_ecols,
        updated_ecols,
        clipped_erows,
        squares_erows,
        updated_erows,
        clipped_dcols,
        squares_dcols,
        updated_dcols,
        clipped_drows,
        squares_drows,
        updated_drows,
        clipped_egains,
        squares_egains,
        updated_egains,
        clipped_dgains,
        squares_dgains,
        updated_dgains,
        loss,
        grad_norm,
    )


def solution(mesh):
    return jax.shard_map(
        body,
        mesh=mesh,
        in_specs=(
            P("grp", "dp", None, None),
            P("grp", "dp", None),
            P("grp", "dp", None),
            P("grp", "dp", None),
            P("grp", None, None),
            P("grp"),
            P(),
            P("dp", None),
            P("dp", None),
            P("dp", None),
            P("dp", None),
            P(),
            P(),
            P("dp", None),
            P("dp", None),
            P("dp", None),
            P("dp", None),
            P(),
            P(),
            P("dp", None),
            P("dp", None),
            P("dp", None),
            P("dp", None),
            P(),
            P(),
        ),
        out_specs=(
            P("dp", None),
            P("dp", None),
            P("dp", None),
            P("dp", None),
            P("dp", None),
            P("dp", None),
            P("dp", None),
            P("dp", None),
            P("dp", None),
            P("dp", None),
            P("dp", None),
            P("dp", None),
            P(),
            P(),
            P(),
            P(),
            P(),
            P(),
            P(),
            P(),
        ),
        check_vma=False,
    )
```

profile of v0, /device:TPU:0, one launch (start us, length us, event | category | flops | bytes accessed | tf_op | source)
XLA Modules:
  0.0 1718.9 jit_solution(14711521115183976709)
XLA Ops:
  20.2 12.5 psum.63
  43.0 10.9 gather_fusion.2
  59.1 7.8 mul.696
  66.9 11.0 gather_fusion
  77.9 10.1 broadcast_select_fusion
  88.0 8.4 slice.161
  96.4 10.5 gather_fusion.3
  108.0 24.3 %scatter_fusion = f32[8,256]{1,0:T(8,128)S(1)} fusion(f32[8,256]{1,0:T(8,128)S(1)} %broadcast_in_dim.52, s32[512]{0:T(512)S(1)} %reshape.496, f32[512]{0:T(512)S(1)} %broadcast.507), kind=kCustom, calls=%fused_computation.5 | custom fusion | bytes 10240 | tf_op jit(solution)/shard_map/scatter | solution.py:254
  137.0 28.3 %all-gather.5.cloned.1.call-done = bf16[8192,1024]{1,0:T(8,128)(2,1)} async-done(((bf16[1024,1024]{1,0:T(8,128)(2,1)}), bf16[8192,1024]{1,0:T(8,128)(2,1)}) %all-gather.5.cloned.1.call-update) | async-done | bytes 16777232 | tf_op jit(solution)/shard_map/all_gather | solution.py:227
  165.2 9.7 fusion.120
  175.4 141.4 %all-gather.7.cloned.1.call-done = bf16[1024,8192]{1,0:T(8,128)(2,1)} async-done(((bf16[128,8192]{1,0:T(8,128)(2,1)}), bf16[1024,8192]{1,0:T(8,128)(2,1)}) %all-gather.7.cloned.1.call-update) | async-done | bytes 16777232 | tf_op jit(solution)/shard_map/all_gather | solution.py:226
  316.8 6.6 fusion.23
  346.2 10.8 multiply_convert_fusion.2
  366.3 64.8 %scatter_fusion.1 = f32[8,256,512]{2,1,0:T(8,128)} fusion(f32[8,256,512]{2,1,0:T(8,128)} %slice_add_fusion, s32[512]{0:T(512)S(1)} %reshape.496, f32[512,512]{1,0:T(8,128)S(1)} %bitcast.272), kind=kCustom, calls=%fused_computation.6 | custom fusion | flops 262144 | bytes 3149824 | tf_op jit(solution)/shard_map/scatter-add | solution.py:256
  437.2 6.3 convolution_convert_fusion
  455.9 14.4 multiply_reduce_fusion.1
  470.3 13.8 exponential_reduce_fusion
  484.2 15.7 fusion.42
  506.6 9.3 multiply_convert_fusion.1
  528.5 6.9 divide_convert_fusion
  535.4 6.6 multiply_reduce_fusion.4
  544.2 13.8 fusion.6
  558.1 7.1 convolution_bitcast_fusion.5
  565.2 6.7 multiply_reduce_fusion.5
  582.5 15.9 fusion.45
  598.5 23.3 %multiply_reduce_fusion = (f32[8,16,256]{2,1,0:T(8,128)S(1)}, f32[8,16,256,256]{2,3,1,0:T(8,128)}) fusion(f32[8,16,256,256]{2,3,1,0:T(8,128)} %get-tuple-element.107, f32[8,16,256]{2,1,0:T(8,128)S(1)} %log_add_fusion, bf16[8,256,16,32]{1,3,2,0:T(8,128)(2,1)} %bitcast.251, bf16[8,256,16,32]{1,3,2,0:T(8,128)(2,1)S(1)} %bitcast.249), kind=kOutput, calls=%fused_computation.10 | convolution fusion | flops 570392576 | bytes 71565312 | tf_op jit(solution)/shard_map/bqhe,bkhe->bhqk/dot_general | solution.py:152
  621.7 28.0 %multiply_convert_fusion = bf16[8,16,256,256]{2,3,1,0:T(8,128)(2,1)} fusion(f32[8,16,256,256]{2,3,1,0:T(8,128)} %get-tuple-element.119, f32[8,16,256,256]{2,3,1,0:T(8,128)} %get-tuple-element.107, f32[8,16,256]{2,1,0:T(8,128)S(1)} %get-tuple-element.118, f32[8,16,256]{2,1,0:T(8,128)S(1)} %log_add_fusion), kind=kLoop, calls=%fused_computation.9 | loop fusion | flops 41943040 | bytes 84148224 | tf_op jit(solution)/shard_map/convert_element_type | solution.py:28
  649.8 12.0 multiply_convert_fusion.6
  661.8 10.5 multiply_convert_fusion.7
  682.9 7.8 convolution_bitcast_fusion.3
  695.9 8.2 multiply_reduce_fusion.6
  732.7 11.0 fusion.16
  743.7 9.7 multiply_reduce_fusion.19
  760.2 5.5 convolution_convert_fusion.1
  788.7 6.1 convolution_bitcast_fusion.6
  794.9 7.0 convolution_bitcast_fusion.2
  801.9 8.6 convolution_bitcast_fusion.1
  810.6 22.9 %pad_maximum_fusion = f32[1024,8192]{1,0:T(8,128)} fusion(f32[1024,4096]{1,0:T(8,128)} %convolution_bitcast_fusion.1, f32[1024,1024]{1,0:T(8,128)} %convolution_bitcast_fusion.6, f32[1024,3072]{1,0:T(8,128)} %convolution_bitcast_fusion.2), kind=kLoop, calls=%fused_computation.7 | loop fusion | flops 16777216 | bytes 67108864 | tf_op jit(solution)/shard_map/concatenate | solution.py:183
  838.4 6.9 multiply_reduce_fusion.20
  850.8 8.8 convolution_bitcast_fusion
  859.6 18.8 %pad_maximum_fusion.1 = f32[8192,1024]{1,0:T(8,128)} fusion(f32[4096,1024]{1,0:T(8,128)S(1)} %fusion.125, f32[4096,1024]{1,0:T(8,128)} %convolution_bitcast_fusion), kind=kLoop, calls=%fused_computation.8 | loop fusion | flops 8388608 | bytes 67108864 | tf_op jit(solution)/shard_map/concatenate | solution.py:289
  882.7 316.6 %reduce-scatter.5.cloned.1.call-done = f32[128,8192]{1,0:T(8,128)} async-done(((f32[1024,8192]{1,0:T(8,128)}), f32[128,8192]{1,0:T(8,128)}) %reduce-scatter.5.cloned.1.call-update) | async-done | bytes 4194320 | tf_op jit(solution)/shard_map/reduce_scatter | solution.py:296
  1203.1 322.6 %reduce-scatter.7.cloned.1.call-done = f32[1024,1024]{1,0:T(8,128)} async-done(((f32[8192,1024]{1,0:T(8,128)}), f32[1024,1024]{1,0:T(8,128)}) %reduce-scatter.7.cloned.1.call-update) | async-done | bytes 4194320 | tf_op jit(solution)/shard_map/reduce_scatter | solution.py:297
  1530.7 38.8 %all-reduce = (f32[6,1024]{1,0:T(8,128)S(1)}, f32[7,512]{1,0:T(8,128)S(1)}, f32[]{:T(128)}) all-reduce(f32[6,1024]{1,0:T(8,128)S(1)} %concatenate.37, f32[7,512]{1,0:T(8,128)S(1)} %concatenate.38, f32[]{:T(128)} %get-tuple-element.69), channel_id=1, replica_groups=mesh['grp'=4,'dp'=8] {'grp','dp'}, use_global_device_ids=true, to_apply=%region_54.55 | all-reduce | flops 9729 | bytes 77832 | tf_op jit(solution)/shard_map/psum | solution.py:307
  1570.7 81.2 %all-reduce.4.cloned.1.call-done = (bf16[128,8192]{1,0:T(8,128)(2,1)}, bf16[1024,1024]{1,0:T(8,128)(2,1)}, bf16[64,4096]{1,0:T(8,128)(2,1)}, bf16[512,512]{1,0:T(8,128)(2,1)}) async-done(((bf16[128,8192]{1,0:T(8,128)(2,1)}, bf16[1024,1024]{1,0:T(8,128)(2,1)}, bf16[64,4096]{1,0:T(8,128)(2,1)}, bf16[512,512]{1,0:T(8,128)(2,1)}), (bf16[128,8192]{1,0:T(8,128)(2,1)}, bf16[1024,1024]{1,0:T(8,128)(2,1)}, ...) | async-done | bytes 5242896 | tf_op jit(solution)/shard_map/psum | solution.py:302
  1664.1 17.0 psum.68
  1693.5 8.9 fusion.35
  1704.3 5.6 fusion.30
  (435 shorter events, 233.8 us)
Async XLA Ops:
  7.2 59.7 %copy-start = (f32[1,512,1536]{2,1,0:T(8,128)S(1)}, f32[1,512,1536]{2,1,0:T(8,128)}, u32[]{:S(2)}) copy-start(f32[1,512,1536]{2,1,0:T(8,128)} %param.29) | copy-start | bytes 9437188
  7.2 158.0 %all-gather.5.cloned.1.call-start = ((), (), s32[]{:S(2)}) async-start(), calls=%async_computation.4 | async-start | bytes 18874368 | tf_op jit(solution)/shard_map/all_gather | solution.py:227
  11.3 305.5 %all-gather.7.cloned.1.call-start = ((), (), s32[]{:S(2)}) async-start(), calls=%async_computation.5 | async-start | bytes 18874368 | tf_op jit(solution)/shard_map/all_gather | solution.py:226
  15.1 349.2 %all-gather.9.cloned.1.call-start = ((), (), s32[]{:S(2)}) async-start(), calls=%async_computation.6 | async-start | bytes 4718592 | tf_op jit(solution)/shard_map/all_gather | solution.py:229
  17.3 419.3 %all-gather.11.cloned.1.call-start = ((), (), s32[]{:S(2)}) async-start(), calls=%async_computation.7 | async-start | bytes 4718592 | tf_op jit(solution)/shard_map/all_gather | solution.py:228
  19.4 859.1 %reduce-scatter.9.cloned.1.call-start = ((), (), s32[]{:S(2)}) async-start(), calls=%async_computation.10 | async-start | bytes 9437184 | tf_op jit(solution)/shard_map/reduce_scatter | solution.py:298
  38.4 57.9 %copy-start.6 = (s32[512]{0:T(512)}, s32[512]{0:T(512)S(1)}, u32[]{:S(2)}) copy-start(s32[512]{0:T(512)S(1)} %reshape.472) | copy-start | bytes 6148
  42.1 123.1 %copy-start.108 = (pred[8,64]{1,0:T(8,128)(4,1)}, pred[8,64]{1,0:T(8,128)(4,1)S(1)}, u32[]{:S(2)}) copy-start(pred[8,64]{1,0:T(8,128)(4,1)S(1)} %get-tuple-element.74) | copy-start | bytes 1540
  42.7 393.9 %copy-start.105 = (f32[1,512]{1,0:T(1,128)}, f32[1,512]{1,0:T(1,128)S(1)}, u32[]{:S(2)}) copy-start(f32[1,512]{1,0:T(1,128)S(1)} %get-tuple-element.91) | copy-start | bytes 6148
  42.7 393.9 %copy-start.120 = (f32[1,512]{1,0:T(1,128)}, f32[1,512]{1,0:T(1,128)S(1)}, u32[]{:S(2)}) copy-start(f32[1,512]{1,0:T(1,128)S(1)} %get-tuple-element.90) | copy-start | bytes 6148
  42.8 274.0 %copy-start.61 = (f32[1,1024]{1,0:T(1,128)}, f32[1,1024]{1,0:T(1,128)S(1)}, u32[]{:S(2)}) copy-start(f32[1,1024]{1,0:T(1,128)S(1)} %get-tuple-element.85) | copy-start | bytes 12292
  42.8 274.0 %copy-start.65 = (f32[1,1024]{1,0:T(1,128)}, f32[1,1024]{1,0:T(1,128)S(1)}, u32[]{:S(2)}) copy-start(f32[1,1024]{1,0:T(1,128)S(1)} %get-tuple-element.84) | copy-start | bytes 12292
  42.8 303.4 %copy-start.92 = (f32[1,1024]{1,0:T(1,128)}, f32[1,1024]{1,0:T(1,128)S(1)}, u32[]{:S(2)}) copy-start(f32[1,1024]{1,0:T(1,128)S(1)} %get-tuple-element.83) | copy-start | bytes 12292
  42.8 303.4 %copy-start.114 = (f32[1,1024]{1,0:T(1,128)}, f32[1,1024]{1,0:T(1,128)S(1)}, u32[]{:S(2)}) copy-start(f32[1,1024]{1,0:T(1,128)S(1)} %get-tuple-element.82) | copy-start | bytes 12292
  42.8 321.5 %copy-start.99 = (f32[1,1024]{1,0:T(1,128)}, f32[1,1024]{1,0:T(1,128)S(1)}, u32[]{:S(2)}) copy-start(f32[1,1024]{1,0:T(1,128)S(1)} %get-tuple-element.81) | copy-start | bytes 12292
  42.8 321.5 %copy-start.116 = (f32[1,1024]{1,0:T(1,128)}, f32[1,1024]{1,0:T(1,128)S(1)}, u32[]{:S(2)}) copy-start(f32[1,1024]{1,0:T(1,128)S(1)} %get-tuple-element.86) | copy-start | bytes 12292
  175.0 167.1 %copy-start.17 = (f32[8,64,1024]{2,1,0:T(8,128)}, f32[8,64,1024]{2,1,0:T(8,128)S(1)}, u32[]{:S(2)}) copy-start(f32[8,64,1024]{2,1,0:T(8,128)S(1)} %get-tuple-element.97) | copy-start | bytes 6291460
  175.0 148.4 %copy-start.59 = (f32[8,64]{1,0:T(8,128)}, f32[8,64]{1,0:T(8,128)S(1)}, u32[]{:S(2)}) copy-start(f32[8,64]{1,0:T(8,128)S(1)} %broadcast_multiply_fusion.22) | copy-start | bytes 6148
  175.4 148.0 %copy-start.63 = (f32[8,64]{1,0:T(8,128)}, f32[8,64]{1,0:T(8,128)S(1)}, u32[]{:S(2)}) copy-start(f32[8,64]{1,0:T(8,128)S(1)} %add_rsqrt_fusion.6) | copy-start | bytes 6148
  345.8 11.3 copy-start.23
  345.8 11.3 copy-start.78
  345.8 11.3 slice-start
  346.2 11.8 slice-start.3
  362.6 68.5 %copy-start.37 = (f32[8,64,1024]{2,1,0:T(8,128)}, f32[8,64,1024]{2,1,0:T(8,128)S(1)}, u32[]{:S(2)}) copy-start(f32[8,64,1024]{2,1,0:T(8,128)S(1)} %get-tuple-element.105) | copy-start | bytes 6291460
  362.6 68.5 %copy-start.80 = (f32[8,64]{1,0:T(8,128)}, f32[8,64]{1,0:T(8,128)S(1)}, u32[]{:S(2)}) copy-start(f32[8,64]{1,0:T(8,128)S(1)} %broadcast_multiply_fusion.20) | copy-start | bytes 6148
  363.0 68.1 %copy-start.101 = (f32[8,64]{1,0:T(8,128)}, f32[8,64]{1,0:T(8,128)S(1)}, u32[]{:S(2)}) copy-start(f32[8,64]{1,0:T(8,128)S(1)} %add_rsqrt_fusion.4) | copy-start | bytes 6148
  451.4 18.9 %copy-start.13 = (bf16[8,256,512]{1,2,0:T(8,128)(2,1)}, bf16[8,256,512]{1,2,0:T(8,128)(2,1)S(1)}, u32[]{:S(2)}) copy-start(bf16[8,256,512]{1,2,0:T(8,128)(2,1)S(1)} %copy.92) | copy-start | bytes 6291460
  470.3 13.9 copy-start.19
  520.6 21.4 %copy-start.28 = (f32[8,256,512]{2,1,0:T(8,128)}, f32[8,256,512]{2,1,0:T(8,128)S(1)}, u32[]{:S(2)}) copy-start(f32[8,256,512]{2,1,0:T(8,128)S(1)} %get-tuple-element.113) | copy-start | bytes 12582916
  520.7 21.4 %copy-start.74 = (f32[8,256]{1,0:T(8,128)}, f32[8,256]{1,0:T(8,128)S(1)}, u32[]{:S(2)}) copy-start(f32[8,256]{1,0:T(8,128)S(1)} %broadcast_multiply_fusion.11) | copy-start | bytes 24580
  521.5 20.6 %copy-start.88 = (f32[8,256]{1,0:T(8,128)}, f32[8,256]{1,0:T(8,128)S(1)}, u32[]{:S(2)}) copy-start(f32[8,256]{1,0:T(8,128)S(1)} %add_rsqrt_fusion.1) | copy-start | bytes 24580
  543.6 28.3 %copy-start.26 = (f32[8,256,512]{2,1,0:T(8,128)}, f32[8,256,512]{2,1,0:T(8,128)S(1)}, u32[]{:S(2)}) copy-start(f32[8,256,512]{2,1,0:T(8,128)S(1)} %subtract_multiply_fusion) | copy-start | bytes 12582916
  621.7 28.0 %copy-start.14 = (bf16[8,256,512]{1,2,0:T(8,128)(2,1)S(1)}, bf16[8,256,512]{1,2,0:T(8,128)(2,1)}, u32[]{:S(2)}) copy-start(bf16[8,256,512]{1,2,0:T(8,128)(2,1)} %copy-done.13) | copy-start | bytes 6291460
  694.4 186.3 %reduce-scatter.11.cloned.1.call-start = ((), (), s32[]{:S(2)}) async-start(), calls=%async_computation.11 | async-start | bytes 9437184 | tf_op jit(solution)/shard_map/reduce_scatter | solution.py:299
  727.4 471.9 %reduce-scatter.5.cloned.1.call-start = ((), (), s32[]{:S(2)}) async-start(), calls=%async_computation.8 | async-start | bytes 37748736 | tf_op jit(solution)/shard_map/reduce_scatter | solution.py:296
  732.6 20.9 %copy-start.40 = (f32[8,64,1024]{2,1,0:T(8,128)}, f32[8,64,1024]{2,1,0:T(8,128)S(1)}, u32[]{:S(2)}) copy-start(f32[8,64,1024]{2,1,0:T(8,128)S(1)} %subtract_multiply_fusion.4) | copy-start | bytes 6291460
  732.6 11.1 copy-start.24
  732.6 11.1 copy-start.79
  732.6 11.1 copy-start.93
  833.5 692.2 %reduce-scatter.7.cloned.1.call-start = ((), (), s32[]{:S(2)}) async-start(), calls=%async_computation.9 | async-start | bytes 37748736 | tf_op jit(solution)/shard_map/reduce_scatter | solution.py:297
  878.4 773.5 %all-reduce.4.cloned.1.call-start = ((), (), s32[]{:S(2)}) async-start(), calls=%async_computation.12 | async-start | bytes 10485760 | tf_op jit(solution)/shard_map/psum | solution.py:302
  1529.6 153.5 %copy-start.77 = (f32[7,512]{1,0:T(8,128)S(1)}, f32[7,512]{1,0:T(8,128)}, u32[]{:S(2)}) copy-start(f32[7,512]{1,0:T(8,128)} %param.37) | copy-start | bytes 43012
  1529.6 153.5 %copy-start.96 = (f32[7,512]{1,0:T(8,128)S(1)}, f32[7,512]{1,0:T(8,128)}, u32[]{:S(2)}) copy-start(f32[7,512]{1,0:T(8,128)} %param.43) | copy-start | bytes 43012
  1529.6 153.5 %copy-start.97 = (f32[7,512]{1,0:T(8,128)S(1)}, f32[7,512]{1,0:T(8,128)}, u32[]{:S(2)}) copy-start(f32[7,512]{1,0:T(8,128)} %param.49) | copy-start | bytes 43012
  1529.6 154.2 %copy-start.69 = (f32[6,1024]{1,0:T(8,128)S(1)}, f32[6,1024]{1,0:T(8,128)}, u32[]{:S(2)}) copy-start(f32[6,1024]{1,0:T(8,128)} %param.36) | copy-start | bytes 73732
  1529.7 154.2 %copy-start.85 = (f32[6,1024]{1,0:T(8,128)S(1)}, f32[6,1024]{1,0:T(8,128)}, u32[]{:S(2)}) copy-start(f32[6,1024]{1,0:T(8,128)} %param.42) | copy-start | bytes 73732
  1529.7 154.1 %copy-start.86 = (f32[6,1024]{1,0:T(8,128)S(1)}, f32[6,1024]{1,0:T(8,128)}, u32[]{:S(2)}) copy-start(f32[6,1024]{1,0:T(8,128)} %param.48) | copy-start | bytes 73732
  1529.7 154.8 %copy-start.49 = (f32[512,512]{1,0:T(8,128)S(1)}, f32[512,512]{1,0:T(8,128)}, u32[]{:S(2)}) copy-start(f32[512,512]{1,0:T(8,128)} %param.35) | copy-start | bytes 3145732
  (103 other events, 499.5 us)
Sparse Core Ops, SparseCore 0:
  11.4 153.7 all-gather.4
  167.4 149.3 all-gather.6
  318.9 45.3 all-gather.8
  366.4 45.8 all-gather.10
  694.5 88.3 reduce-scatter.8
  785.0 87.9 reduce-scatter.10
  875.4 323.8 reduce-scatter.4
  1201.8 323.8 reduce-scatter.6
  1530.6 121.2 all-reduce.3
where the time goes:
time: 1730 us; the launch traced here: 1720 us
  waiting for transfers between devices  892 us (52%)
  matrix products  310 us (18%)
  other arithmetic  265 us (15%)
  local copies, waits for them, and re-layouts  157 us (9%)
  blocking collectives  68.3 us (4%)
  between operations  25.6 us (1%)
    reduce_scatter x1, waiting for transfers between devices, body(): lax.psum_scatter(grads[1], 'dp', scatter_dimension=0, tiled=True)  323 us
    reduce_scatter x1, waiting for transfers between devices, body(): lax.psum_scatter(grads[0], 'dp', scatter_dimension=0, tiled=True)  317 us
    all_gather x1, waiting for transfers between devices, body(): lax.all_gather(to_low(enc_cols), 'dp', axis=0, tiled=True)  141 us
    psum x1, waiting for transfers between devices, body(): lax.psum(shards[0].astype(jnp.bfloat16), 'grp').astype(jnp.float32)  81.2 us
    dot_general x11, matrix products, project(): jnp.einsum('...n,nm->...m', inputs, matrix, preferred_element_type=jnp.fl...  68.6 us
    dot_general x10, matrix products, project_back(): jnp.einsum('...m,nm->...n', grads, matrix, preferred_element_type=jnp.flo...  68.4 us
    scatter-add x1, other arithmetic, body(): dec_input = dec_input.at[item_rows, keep_rows].add(latent)  64.8 us
    dot_general x11, matrix products, weight_grad(): lax.dot_general(flat_in, flat_grad, (((0,), (0,)), ((), ())), preferred_e...  62.3 us
  transfers between devices with their start and end apart: 9, of which 6 were waited for; matrix products, arithmetic and copies ran while one was open for 24% of the time, Pallas kernels for 0%

commit v1 on v0

--- a/solution.py
+++ b/solution.py
@@ -1,6 +1,10 @@
+import functools
+
 import jax
 import jax.numpy as jnp
 from jax import lax
+from jax.experimental import pallas as pl
+from jax.experimental.pallas import tpu as pltpu
 from jax.sharding import PartitionSpec as P
 
 D = 1024
@@ -180,9 +184,697 @@
         project_back(grad_packed, columns[:, : 3 * width]), hat_one, scale_one, gains[0]
     )
     grad_in = grad_middle + back_one
-    grad_cols = jnp.concatenate([grad_qkv, grad_proj, grad_up], 1)
+    grad_cols = (grad_qkv, grad_proj, grad_up)
     grad_gains = jnp.stack([gain_one, shift_one, gain_two, shift_two])
     return (grad_in, grad_cols, grad_down, grad_gains)
+
+
+def dot_nn(a, b):
+    return lax.dot_general(a, b, (((1,), (0,)), ((), ())), preferred_element_type=jnp.float32)
+
+
+def dot_nt(a, b):
+    return lax.dot_general(a, b, (((1,), (1,)), ((), ())), preferred_element_type=jnp.float32)
+
+
+def dot_tn(a, b):
+    return lax.dot_general(a, b, (((0,), (0,)), ((), ())), preferred_element_type=jnp.float32)
+
+
+def unit_rows(values):
+    centred = values - jnp.mean(values, -1, keepdims=True)
+    scaled = lax.rsqrt(jnp.mean(centred * centred, -1, keepdims=True) + norm_eps)
+    return centred * scaled, scaled
+
+
+def unit_back(grads, hat, scaled, gain):
+    inner = grads * gain
+    return scaled * (
+        inner
+        - jnp.mean(inner, -1, keepdims=True)
+        - hat * jnp.mean(inner * hat, -1, keepdims=True)
+    )
+
+
+def decoder_kernel(
+    items, heads, scal_ref, z_ref, pos_ref, pix_ref, cols_ref, down_ref, head_ref, gains_ref,
+    dz_ref, gcols_out, gdown_out, ghead_out, ggains_ref, loss_ref,
+    x_s, h1_s, qkv_s, p_s, o_s, x1_s, h2_s, a_s, gp_s, x2_s, hd_s, dx_s, dy_s, acc_s, dqkv_s,
+    gcols, gdown, ghead,
+):
+    low = jnp.bfloat16
+    step = pl.program_id(0)
+    width = x_s.shape[1]
+    tokens = pos_ref.shape[1]
+    hide = tokens - K
+    rows = items * tokens
+    tile = 512
+    grp_heads = 4
+    lanes = 128
+    ee = width // heads
+    scale = ee ** (-0.5)
+    expo = scale * 1.4426950408889634
+
+    @pl.when(step == 0)
+    def _():
+        gcols[...] = jnp.zeros_like(gcols)
+        gdown[...] = jnp.zeros_like(gdown)
+        ghead[...] = jnp.zeros_like(ghead)
+        ggains_ref[...] = jnp.zeros_like(ggains_ref)
+        loss_ref[...] = jnp.zeros_like(loss_ref)
+
+    def gain(i):
+        return gains_ref[i : i + 1, :]
+
+    for i in range(items):
+        base = i * tokens
+        x_s[base : base + K, :] = pos_ref[i, :K, :] + z_ref[i]
+        x_s[base + K : base + tokens, :] = pos_ref[i, K:, :] + gain(6)
+    hat, _ = unit_rows(x_s[...])
+    h1_s[...] = (hat * gain(0) + gain(1)).astype(low)
+
+    @pl.loop(0, 3)
+    def _(t):
+        at = pl.ds(pl.multiple_of(t * width, width), width)
+        qkv_s[:, at] = dot_nn(h1_s[...], cols_ref[:, at]).astype(low)
+
+    lane = lax.broadcasted_iota(jnp.int32, (1, lanes), 1) // ee
+    groups = width // lanes
+
+    def masked(value, h):
+        return jnp.where(lane == h, value, jnp.zeros_like(value))
+
+    @pl.loop(0, items * groups)
+    def _(n):
+        item = n // groups
+        g = n % groups
+        rs = pl.ds(pl.multiple_of(item * tokens, tokens), tokens)
+        q = qkv_s[rs, pl.ds(pl.multiple_of(g * lanes, lanes), lanes)]
+        k = qkv_s[rs, pl.ds(pl.multiple_of(width + g * lanes, lanes), lanes)]
+        v = qkv_s[rs, pl.ds(pl.multiple_of(2 * width + g * lanes, lanes), lanes)]
+        out = jnp.zeros((tokens, lanes), jnp.float32)
+        for h in range(grp_heads):
+            s = dot_nt(masked(q, h), k)
+            top = jnp.max(s, -1, keepdims=True)
+            e = jnp.exp2((s - top) * expo)
+            p = (e * (1.0 / jnp.sum(e, -1, keepdims=True))).astype(low)
+            p_s[n * grp_heads + h] = p
+            out = out + dot_nn(p, masked(v, h))
+        o_s[rs, pl.ds(pl.multiple_of(g * lanes, lanes), lanes)] = out.astype(low)
+
+    x1_s[...] = x_s[...] + dot_nn(o_s[...], cols_ref[:, 3 * width : 4 * width])
+    hat, _ = unit_rows(x1_s[...])
+    h2_s[...] = (hat * gain(2) + gain(3)).astype(low)
+    x2_s[...] = x1_s[...]
+
+    @pl.loop(0, down_ref.shape[0] // tile)
+    def _(t):
+        at = pl.ds(pl.multiple_of(t * tile, tile), tile)
+        up = pl.ds(pl.multiple_of(4 * width + t * tile, tile), tile)
+        u = dot_nn(h2_s[...], cols_ref[:, up])
+        cumul = 0.5 * (1.0 + lax.erf(u * 0.7071067811865476))
+        act = (u * cumul).astype(low)
+        a_s[:, at] = act
+        gp_s[:, at] = (cumul + u * jnp.exp(-0.5 * u * u) * 0.3989422804014327).astype(gp_s.dtype)
+        x2_s[...] += dot_nn(act, down_ref[at, :])
+
+    hat, _ = unit_rows(x2_s[...])
+    hd_s[...] = (hat * gain(4) + gain(5)).astype(low)
+
+    pixel_count = head_ref.shape[0]
+    for i in range(items):
+        base = i * tokens
+        weight = scal_ref[0, step * items + i]
+        coef = scal_ref[1, step * items + i]
+        pixel = pix_ref[i].astype(jnp.float32)
+        target, _ = unit_rows(pixel)
+        hd = hd_s[base + K : base + tokens, :]
+        back = jnp.zeros((hide, width), jnp.float32)
+        for t in range(pixel_count // tile):
+            at = slice(t * tile, (t + 1) * tile)
+            err = dot_nt(hd, head_ref[at, :]) - target[:, at]
+            loss_ref[...] += weight * jnp.sum(err * err, keepdims=True).reshape(1, 1)
+            dpred = (err * coef).astype(low)
+            ghead[at, :] += dot_tn(dpred, hd)
+            back = back + dot_nn(dpred, head_ref[at, :])
+        hat, scaled = unit_rows(x2_s[base + K : base + tokens, :])
+        ggains_ref[4:5, :] += jnp.sum(back * hat, 0, keepdims=True)
+        ggains_ref[5:6, :] += jnp.sum(back, 0, keepdims=True)
+        dx = unit_back(back, hat, scaled, gain(4))
+        dx_s[base : base + K, :] = jnp.zeros((K, width), jnp.float32)
+        dx_s[base + K : base + tokens, :] = dx
+        dy_s[base : base + K, :] = jnp.zeros((K, width), low)
+        dy_s[base + K : base + tokens, :] = dx.astype(low)
+
+    acc_s[...] = jnp.zeros_like(acc_s)
+
+    @pl.loop(0, down_ref.shape[0] // tile)
+    def _(t):
+        at = pl.ds(pl.multiple_of(t * tile, tile), tile)
+        up = pl.ds(pl.multiple_of(4 * width + t * tile, tile), tile)
+        gdown[at, :] += dot_tn(a_s[:, at], dy_s[...])
+        du = (dot_nt(dy_s[...], down_ref[at, :]) * gp_s[:, at].astype(jnp.float32)).astype(low)
+        gcols[:, up] += dot_tn(h2_s[...], du)
+        acc_s[...] += dot_nt(du, cols_ref[:, up])
+
+    hat, scaled = unit_rows(x1_s[...])
+    grads = acc_s[...]
+    ggains_ref[2:3, :] += jnp.sum(grads * hat, 0, keepdims=True)
+    ggains_ref[3:4, :] += jnp.sum(grads, 0, keepdims=True)
+    dx_s[...] += unit_back(grads, hat, scaled, gain(2))
+    dy_s[...] = dx_s[...].astype(low)
+    gcols[:, 3 * width : 4 * width] += dot_tn(o_s[...], dy_s[...])
+    o_s[...] = dot_nt(dy_s[...], cols_ref[:, 3 * width : 4 * width]).astype(low)
+
+    @pl.loop(0, items * groups)
+    def _(n):
+        item = n // groups
+        g = n % groups
+        rs = pl.ds(pl.multiple_of(item * tokens, tokens), tokens)
+        qa = pl.ds(pl.multiple_of(g * lanes, lanes), lanes)
+        ka = pl.ds(pl.multiple_of(width + g * lanes, lanes), lanes)
+        va = pl.ds(pl.multiple_of(2 * width + g * lanes, lanes), lanes)
+        q = qkv_s[rs, qa]
+        k = qkv_s[rs, ka]
+        v = qkv_s[rs, va]
+        do = o_s[rs, qa]
+        dq = jnp.zeros((tokens, lanes), jnp.float32)
+        dk = jnp.zeros((tokens, lanes), jnp.float32)
+        dv = jnp.zeros((tokens, lanes), jnp.float32)
+        for h in range(grp_heads):
+            p = p_s[n * grp_heads + h]
+            dom = masked(do, h)
+            dp = dot_nt(dom, v)
+            pf = p.astype(jnp.float32)
+            ds = (pf * (dp - jnp.sum(dp * pf, -1, keepdims=True))).astype(low)
+            dv = dv + dot_tn(p, dom)
+            dq = dq + dot_nn(ds, masked(k, h))
+            dk = dk + dot_tn(ds, masked(q, h))
+        dqkv_s[rs, qa] = (dq * scale).astype(low)
+        dqkv_s[rs, ka] = (dk * scale).astype(low)
+        dqkv_s[rs, va] = dv.astype(low)
+
+    acc_s[...] = jnp.zeros_like(acc_s)
+
+    @pl.loop(0, 3)
+    def _(t):
+        at = pl.ds(pl.multiple_of(t * width, width), width)
+        gcols[:, at] += dot_tn(h1_s[...], dqkv_s[:, at])
+        acc_s[...] += dot_nt(dqkv_s[:, at], cols_ref[:, at])
+
+    hat, scaled = unit_rows(x_s[...])
+    grads = acc_s[...]
+    ggains_ref[0:1, :] += jnp.sum(grads * hat, 0, keepdims=True)
+    ggains_ref[1:2, :] += jnp.sum(grads, 0, keepdims=True)
+    dx_s[...] += unit_back(grads, hat, scaled, gain(0))
+    for i in range(items):
+        base = i * tokens
+        dz_ref[i] = dx_s[base : base + K, :].astype(low)
+        ggains_ref[6:7, :] += jnp.sum(dx_s[base + K : base + tokens, :], 0, keepdims=True)
+
+    @pl.when(step == pl.num_programs(0) - 1)
+    def _():
+        gcols_out[...] = gcols[...].astype(low)
+        gdown_out[...] = gdown[...].astype(low)
+        ghead_out[...] = ghead[...].astype(low)
+
+
+def decoder_call(scal, latent, position, pixel_rows, cols, down, head, gains, heads):
+    batch, tokens, width = position.shape
+    pixel_count = head.shape[0]
+    items = 2
+    rows = items * tokens
+    hide = tokens - K
+    low = jnp.bfloat16
+    full = pl.Buffered(1)
+
+    def whole(array):
+        return pl.BlockSpec(array.shape, lambda s: (0,) * array.ndim, pipeline_mode=full)
+
+    def by_item(shape):
+        return pl.BlockSpec((items,) + shape, lambda s: (s, 0, 0))
+
+    outs = (
+        jax.ShapeDtypeStruct((batch, K, width), low),
+        jax.ShapeDtypeStruct(cols.shape, low),
+        jax.ShapeDtypeStruct(down.shape, low),
+        jax.ShapeDtypeStruct(head.shape, low),
+        jax.ShapeDtypeStruct((8, width), jnp.float32),
+        jax.ShapeDtypeStruct((1, 1), jnp.float32),
+    )
+    vmem = pltpu.VMEM
+    f32 = jnp.float32
+    return pl.pallas_call(
+        functools.partial(decoder_kernel, items, heads),
+        grid=(batch // items,),
+        in_specs=[
+            pl.BlockSpec(memory_space=pltpu.SMEM),
+            by_item((K, width)),
+            by_item((tokens, width)),
+            by_item((hide, pixel_count)),
+            whole(cols),
+            whole(down),
+            whole(head),
+            whole(gains),
+        ],
+        out_specs=(by_item((K, width)),) + tuple(whole(out) for out in outs[1:]),
+        out_shape=outs,
+        scratch_shapes=[
+            vmem((rows, width), f32),
+            vmem((rows, width), low),
+            vmem((rows, 3 * width), low),
+            vmem((items * heads, tokens, tokens), low),
+            vmem((rows, width), low),
+            vmem((rows, width), f32),
+            vmem((rows, width), low),
+            vmem((rows, down.shape[0]), low),
+            vmem((rows, down.shape[0]), f32),
+            vmem((rows, width), f32),
+            vmem((rows, width), low),
+            vmem((rows, width), f32),
+            vmem((rows, width), low),
+            vmem((rows, width), f32),
+            vmem((rows, 3 * width), low),
+            vmem(cols.shape, f32),
+            vmem(down.shape, f32),
+            vmem(head.shape, f32),
+        ],
+        compiler_params=pltpu.CompilerParams(
+            dimension_semantics=("arbitrary",), vmem_limit_bytes=60 * 1024 * 1024
+        ),
+        cost_estimate=pl.CostEstimate(
+            flops=70_000_000_000, bytes_accessed=40_000_000, transcendentals=20_000_000
+        ),
+    )(scal, latent, position, pixel_rows, cols, down, head, gains)
+
+
+MESH_ID = pl.DeviceIdType.MESH
+
+
+def place():
+    g = lax.axis_index("grp")
+    d = lax.axis_index("dp")
+    z, c = d // 2, d % 2
+    xn = g + 1 - 2 * (g % 2)
+    yn = (g + 2) % 4
+    return g, z, c, xn, yn
+
+
+def pieces(shape, parts):
+    rows, columns = shape
+    if rows // parts >= 32:
+        n = rows // parts
+        cut = [(slice(i * n, (i + 1) * n), slice(0, columns)) for i in range(parts)]
+    else:
+        n = columns // parts
+        cut = [(slice(0, rows), slice(i * n, (i + 1) * n)) for i in range(parts)]
+    return cut
+
+
+def halves(cut):
+    rows, columns = cut
+    mid = (columns.start + columns.stop) // 2
+    return (rows, slice(columns.start, mid)), (rows, slice(mid, columns.stop))
+
+
+def greet(peers):
+    barrier = pltpu.get_barrier_semaphore()
+    for peer in peers:
+        pl.semaphore_signal(barrier, inc=1, device_id=peer, device_id_type=MESH_ID)
+    pl.semaphore_wait(barrier, len(peers))
+
+
+def gather_kernel(count, chunks, ahead, *refs):
+    ins, outs = refs[:count], refs[count : 2 * count]
+    zs, zr, xs, xr, ys, yr, fs, fr, gs, gr, cs, os, cr, ls = refs[2 * count :]
+    g, z, c, xn, yn = place()
+    dg = (xn + 2) % 4
+    here = 2 * z + c
+    sib = (g, 2 * z + 1 - c)
+    zpeer = [(g, 2 * ((z + j) % 4) + c) for j in (1, 2, 3)]
+    zfrom = [(z + 4 - j) % 4 for j in (1, 2, 3)]
+    greet([sib, (xn, here), (yn, here)] + zpeer)
+
+    def send(src, dst, send_sem, recv_sem, peer):
+        return pltpu.make_async_remote_copy(
+            src_ref=src, dst_ref=dst, send_sem=send_sem, recv_sem=recv_sem,
+            device_id=peer, device_id_type=MESH_ID,
+        )
+
+    def block(array, z_at, q, cut, core=None):
+        return outs[array].at[z_at, c if core is None else core, q, cut[0], cut[1]]
+
+    work = []
+    for array in range(count):
+        for cut in pieces(ins[array].shape[1:], chunks[array]):
+            work.append((array, cut))
+    steps = len(work)
+    sent = []
+
+    def go(copy):
+        copy.start()
+        sent.append(copy)
+
+    def zcopy(k, j):
+        array, cut = work[k]
+        return send(
+            ins[array].at[g, cut[0], cut[1]], block(array, z, g, cut), zs.at[k, j], zr.at[k, j], zpeer[j]
+        )
+
+    def relay(k, j, q, cut, ssem, rsem, peer):
+        at = block(work[k][0], zfrom[j], q, cut)
+        return send(at, at, ssem, rsem, peer)
+
+    local = []
+    for array in range(count):
+        copy = pltpu.make_async_copy(ins[array], outs[array].at[z, c], ls.at[array])
+        copy.start()
+        local.append(copy)
+    for k in range(min(ahead, steps)):
+        for j in range(3):
+            go(zcopy(k, j))
+    for array in range(count):
+        go(send(ins[array], outs[array].at[z, c], os.at[array], cr.at[array], sib))
+
+    for t in range(steps + 2):
+        if t < steps:
+            array, cut = work[t]
+            for j in range(3):
+                zcopy(t, j).wait_recv()
+                go(relay(t, j, g, cut, xs.at[t, j], xr.at[t, j], (xn, here)))
+                go(relay(t, j, g, cut, ys.at[t, j], yr.at[t, j], (yn, here)))
+                go(relay(t, j, g, cut, cs.at[t, j, 0], cr.at[array], sib))
+            if t + ahead < steps:
+                for j in range(3):
+                    go(zcopy(t + ahead, j))
+        if 1 <= t <= steps:
+            k = t - 1
+            array, cut = work[k]
+            left, right = halves(cut)
+            for j in range(3):
+                relay(k, j, xn, cut, xs.at[k, j], xr.at[k, j], (xn, here)).wait_recv()
+                go(relay(k, j, xn, left, fs.at[k, j], fr.at[k, j], (yn, here)))
+                go(relay(k, j, xn, cut, cs.at[k, j, 1], cr.at[array], sib))
+                relay(k, j, yn, cut, ys.at[k, j], yr.at[k, j], (yn, here)).wait_recv()
+                go(relay(k, j, yn, right, gs.at[k, j], gr.at[k, j], (xn, here)))
+                go(relay(k, j, yn, cut, cs.at[k, j, 2], cr.at[array], sib))
+        if 2 <= t:
+            k = t - 2
+            array, cut = work[k]
+            left, right = halves(cut)
+            for j in range(3):
+                relay(k, j, dg, left, fs.at[k, j], fr.at[k, j], (yn, here)).wait_recv()
+                relay(k, j, dg, right, gs.at[k, j], gr.at[k, j], (xn, here)).wait_recv()
+                go(relay(k, j, dg, cut, cs.at[k, j, 3], cr.at[array], sib))
+    for copy in sent:
+        copy.wait_send()
+    for array in range(count):
+        whole = outs[array].at[:, 1 - c]
+        send(whole, whole, os.at[array], cr.at[array], sib).wait_recv()
+        local[array].wait()
+
+
+def gather_call(shards, chunks, ahead=2, collective_id=0):
+    count = len(shards)
+    steps = sum(chunks)
+    views = [s.reshape(4, s.shape[0] // 4, s.shape[1]) for s in shards]
+    dma = pltpu.SemaphoreType.DMA
+    hbm = pl.BlockSpec(memory_space=pl.ANY)
+    outs = pl.pallas_call(
+        functools.partial(gather_kernel, count, chunks, ahead),
+        out_shape=tuple(jax.ShapeDtypeStruct((4, 2) + v.shape, v.dtype) for v in views),
+        in_specs=[hbm] * count,
+        out_specs=tuple([hbm] * count),
+        scratch_shapes=[dma((steps, 3))] * 10
+        + [dma((steps, 3, 4)), dma((count,)), dma((count,)), dma((count,))],
+        compiler_params=pltpu.CompilerParams(collective_id=collective_id, has_side_effects=True),
+    )(*views)
+    return [o.reshape(-1, o.shape[-1]) for o in outs]
+
+
+def reduce_kernel(n_in, n_out, work, ahead, *refs):
+    ins = refs[:n_in]
+    small_ref = refs[n_in]
+    outs = refs[n_in + 1 : n_in + 1 + n_out]
+    small_out = refs[n_in + 1 + n_out]
+    (s, own, xa, yb, xb, ya, zb, fin, sm,
+     cs, cr, os, x1s, x1r, x2s, x2r, z_s, z_r, ags, agr, ls, sms, smr) = refs[n_in + n_out + 2 :]
+    g, z, c, xn, yn = place()
+    dg = (xn + 2) % 4
+    here = 2 * z + c
+    sib = (g, 2 * z + 1 - c)
+    right, up = (xn, here), (yn, here)
+    zto = [(z + j) % 4 for j in (1, 2, 3)]
+    zpeer = [(g, 2 * t + c) for t in zto]
+    greet([sib, right, up] + zpeer)
+    steps = len(work)
+    rows, columns = s.shape[3:]
+    half = columns // 2
+    left_half, right_half = pl.ds(0, half), pl.ds(half, half)
+    sent = []
+    f32 = jnp.float32
+
+    def send(src, dst, send_sem, recv_sem, peer):
+        return pltpu.make_async_remote_copy(
+            src_ref=src, dst_ref=dst, send_sem=send_sem, recv_sem=recv_sem,
+            device_id=peer, device_id_type=MESH_ID,
+        )
+
+    def go(copy):
+        copy.start()
+        sent.append(copy)
+
+    def c_copies(k):
+        return [
+            send(
+                ins[array].at[:, 1 - c, :, cut[0], cut[1]], s.at[k, pl.ds(z0, nz)],
+                cs.at[k, i], cr.at[k, i], sib,
+            )
+            for i, (array, z0, nz, cut) in enumerate(work[k][0])
+        ]
+
+    def own_copies(k):
+        slot = k % own.shape[0]
+        return [
+            pltpu.make_async_copy(
+                ins[array].at[:, c, :, cut[0], cut[1]], own.at[slot, pl.ds(z0, nz)], os.at[slot, i]
+            )
+            for i, (array, z0, nz, cut) in enumerate(work[k][0])
+        ]
+
+    def begin(k):
+        for copy in c_copies(k):
+            go(copy)
+        for copy in own_copies(k):
+            copy.start()
+
+    def x1_copies(k):
+        return [
+            send(s.at[k, :, xn, :, left_half], xa.at[k, 0], x1s.at[k, 0], x1r.at[k, 0], right),
+            send(s.at[k, :, dg, :, left_half], xa.at[k, 1], x1s.at[k, 1], x1r.at[k, 1], right),
+            send(s.at[k, :, yn, :, right_half], yb.at[k, 0], x1s.at[k, 2], x1r.at[k, 2], up),
+            send(s.at[k, :, dg, :, right_half], yb.at[k, 1], x1s.at[k, 3], x1r.at[k, 3], up),
+        ]
+
+    def x2_copies(k):
+        return [
+            send(s.at[k, :, yn, :, left_half], ya.at[k], x2s.at[k, 0], x2r.at[k, 0], up),
+            send(s.at[k, :, xn, :, right_half], xb.at[k], x2s.at[k, 1], x2r.at[k, 1], right),
+        ]
+
+    def z_copies(k):
+        return [
+            send(s.at[k, zto[j], g], zb.at[k, j], z_s.at[k, j], z_r.at[k, j], zpeer[j]) for j in range(3)
+        ]
+
+    def out_at(k, q, part=None):
+        _, index, cut = work[k]
+        if part is not None:
+            cut = halves(cut)[part]
+        return outs[index].at[q, cut[0], cut[1]]
+
+    def ag_copies(k):
+        return [
+            send(fin.at[k], out_at(k, g), ags.at[k, 0], agr.at[k, 0], right),
+            send(fin.at[k], out_at(k, g), ags.at[k, 1], agr.at[k, 1], up),
+        ]
+
+    def fwd_copies(k, of_x, of_y):
+        return [
+            send(out_at(k, of_x, 0), out_at(k, of_x, 0), ags.at[k, 2], agr.at[k, 2], up),
+            send(out_at(k, of_y, 1), out_at(k, of_y, 1), ags.at[k, 3], agr.at[k, 3], right),
+        ]
+
+    def small_copy(i, j, slot, peer):
+        return send(sm.at[slot], sm.at[4 + i], sms.at[j], smr.at[j], peer)
+
+    def stage1(k):
+        slot = k % own.shape[0]
+        for copy in c_copies(k):
+            copy.wait_recv()
+        for copy in own_copies(k):
+            copy.wait()
+
+        @pl.loop(0, 4)
+        def _(i):
+            for q in range(4):
+                s[k, i, q] = (s[k, i, q].astype(f32) + own[slot, i, q].astype(f32)).astype(s.dtype)
+
+        for copy in x1_copies(k):
+            go(copy)
+
+    def add_half(k, q, part, other):
+        @pl.loop(0, 4)
+        def _(i):
+            s[k, i, q, :, part] = (
+                s[k, i, q, :, part].astype(f32) + other[i].astype(f32)
+            ).astype(s.dtype)
+
+    def stage2(k):
+        for copy in x1_copies(k):
+            copy.wait_recv()
+        add_half(k, yn, left_half, xa.at[k, 1])
+        add_half(k, xn, right_half, yb.at[k, 1])
+        for copy in x2_copies(k):
+            go(copy)
+        add_half(k, g, left_half, xa.at[k, 0])
+        add_half(k, g, right_half, yb.at[k, 0])
+
+    def stage3(k):
+        for copy in x2_copies(k):
+            copy.wait_recv()
+        add_half(k, g, left_half, ya.at[k])
+        add_half(k, g, right_half, xb.at[k])
+        for copy in z_copies(k):
+            go(copy)
+
+    def stage4(k):
+        for copy in z_copies(k):
+            copy.wait_recv()
+        total = s[k, z, g].astype(f32)
+        for j in range(3):
+            total = total + zb[k, j].astype(f32)
+        fin[k] = total.astype(fin.dtype)
+        for copy in ag_copies(k):
+            go(copy)
+        pltpu.make_async_copy(fin.at[k], out_at(k, g), ls.at[k]).start()
+
+    def stage5(k):
+        for copy in ag_copies(k):
+            copy.wait_recv()
+        for copy in fwd_copies(k, xn, yn):
+            go(copy)
+
+    def stage6(k):
+        for copy in fwd_copies(k, dg, dg):
+            copy.wait_recv()
+
+    stages = [stage1, stage2, stage3, stage4, stage5, stage6]
+    sm[0] = small_ref[...]
+    go(small_copy(0, 0, 0, sib))
+    for k in range(min(ahead, steps)):
+        begin(k)
+    for t in range(steps + len(stages) - 1):
+        for i, stage in enumerate(stages):
+            k = t - i
+            if 0 <= k < steps:
+                stage(k)
+                if i == 0 and k + ahead < steps:
+                    begin(k + ahead)
+        if t == 0:
+            small_copy(0, 0, 0, sib).wait_recv()
+            sm[1] = sm[0] + sm[4]
+            go(small_copy(1, 1, 1, right))
+        if t == 1:
+            small_copy(1, 1, 1, right).wait_recv()
+            sm[2] = sm[1] + sm[5]
+            go(small_copy(2, 2, 2, up))
+        if t == 2:
+            small_copy(2, 2, 2, up).wait_recv()
+            sm[3] = sm[2] + sm[6]
+            for j in range(3):
+                go(small_copy(3 + j, 3 + j, 3, zpeer[j]))
+        if t == 3:
+            for j in range(3):
+                small_copy(3 + j, 3 + j, 3, zpeer[j]).wait_recv()
+            total = None
+            for t_z in range(4):
+                term = jnp.where(z == t_z, sm[3], jnp.zeros_like(sm[3]))
+                for j in range(3):
+                    came = (z + 3 - j) % 4
+                    term = term + jnp.where(came == t_z, sm[7 + j], jnp.zeros_like(sm[3]))
+                total = term if total is None else total + term
+            small_out[...] = total
+    for copy in sent:
+        copy.wait_send()
+    for k in range(steps):
+        pltpu.make_async_copy(fin.at[k], out_at(k, g), ls.at[k]).wait()
+
+
+def reduce_call(grads, small, work, block, out_shapes, ahead=2, collective_id=1):
+    steps = len(work)
+    rows, columns = block
+    half = columns // 2
+    low = jnp.bfloat16
+    dma = pltpu.SemaphoreType.DMA
+    hbm = pl.BlockSpec(memory_space=pl.ANY)
+    vm = pl.BlockSpec(memory_space=pltpu.VMEM)
+    vmem = pltpu.VMEM
+    return pl.pallas_call(
+        functools.partial(reduce_kernel, len(grads), len(out_shapes), work, ahead),
+        out_shape=tuple(jax.ShapeDtypeStruct(shape, low) for shape in out_shapes)
+        + (jax.ShapeDtypeStruct(small.shape, jnp.float32),),
+        in_specs=[hbm] * len(grads) + [vm],
+        out_specs=tuple([hbm] * len(out_shapes) + [vm]),
+        scratch_shapes=[
+            vmem((steps, 4, 4, rows, columns), low),
+            vmem((ahead + 1, 4, 4, rows, columns), low),
+            vmem((steps, 2, 4, rows, half), low),
+            vmem((steps, 2, 4, rows, half), low),
+            vmem((steps, 4, rows, half), low),
+            vmem((steps, 4, rows, half), low),
+            vmem((steps, 3, rows, columns), low),
+            vmem((steps, rows, columns), low),
+            vmem((10,) + small.shape, jnp.float32),
+            dma((steps, 2)), dma((steps, 2)), dma((ahead + 1, 2)),
+            dma((steps, 4)), dma((steps, 4)),
+            dma((steps, 2)), dma((steps, 2)),
+            dma((steps, 3)), dma((steps, 3)),
+            dma((steps, 4)), dma((steps, 4)),
+            dma((steps,)), dma((6,)), dma((6,)),
+        ],
+        compiler_params=pltpu.CompilerParams(
+            collective_id=collective_id, has_side_effects=True, vmem_limit_bytes=60 * 1024 * 1024
+        ),
+    )(*grads, small)
+
+
+def reduce_encoder(edown, embed, qkv, proj, up, small, ahead=2, collective_id=1):
+    width = edown.shape[1]
+    rows = qkv.shape[0] // 32
+    tall = edown.shape[0] // 16
+
+    def cut_rows(k):
+        return (slice(k * rows, (k + 1) * rows), slice(0, width))
+
+    def cut_columns(k):
+        return (slice(0, rows), slice(k * width, (k + 1) * width))
+
+    work = []
+    for k in range(tall // rows):
+        work.append((((0, 0, 2, cut_rows(k)), (1, 2, 2, cut_rows(k))), 0, cut_rows(k)))
+    grads = [edown.reshape(2, 2, 4, tall, width), embed.reshape(2, 2, 4, tall, width)]
+    at = 0
+    for index, part in enumerate((qkv, proj, up)):
+        grads.append(part.reshape(4, 2, 4, rows, part.shape[1]))
+        for k in range(part.shape[1] // width):
+            work.append((((2 + index, 0, 4, cut_columns(k)),), 1, cut_columns(at)))
+            at += 1
+    shapes = ((4, tall, width), (4, rows, at * width))
+    erows, ecols, total = reduce_call(
+        grads, small, tuple(work), (rows, width), shapes, ahead, collective_id
+    )
+    return ecols.reshape(4 * rows, -1), erows.reshape(4 * tall, width), total
 
 
 def adam_step(master, moment, square, grad, factor, fix_one, fix_two, decay, rate):
@@ -220,14 +912,25 @@
     square_egains,
     square_dgains,
 ):
+    n_grp = lax.axis_size("grp")
+    grp_at = lax.axis_index("grp")
+
+    def gather_rows(master):
+        rows = master.shape[0]
+        if rows % (16 * n_grp):
+            return lax.all_gather(to_low(master), "dp", axis=0, tiled=True)
+        part = rows // n_grp
+        mine = lax.dynamic_slice_in_dim(master, grp_at * part, part, 0)
+        return lax.all_gather(to_low(mine), ("dp", "grp"), axis=0, tiled=True)
+
     total_count = lax.psum(jnp.sum(group_items.astype(jnp.float32)), "grp")
     masked = total_count * (L - K)
-    copies = (
-        lax.all_gather(to_low(enc_cols), "dp", axis=0, tiled=True),
-        lax.all_gather(to_low(enc_rows), "dp", axis=0, tiled=True),
-        lax.all_gather(to_low(dec_cols), "dp", axis=0, tiled=True),
-        lax.all_gather(to_low(dec_rows), "dp", axis=0, tiled=True),
-    )
+    direct = (n_grp, lax.axis_size("dp")) == (4, 8)
+    if direct:
+        whole_rows, whole_cols = gather_call([to_low(enc_rows), to_low(enc_cols)], (4, 4), 2, 0)
+    else:
+        whole_rows, whole_cols = gather_rows(enc_rows), gather_rows(enc_cols)
+    copies = (whole_cols, whole_rows, gather_rows(dec_cols), gather_rows(dec_rows))
     enc_copy = copies[0]
     enc_down = copies[1][:FF]
     embed_w = copies[1][FF:]
@@ -235,47 +938,54 @@
     dec_down = copies[3][:DFF]
     dec_embed = copies[3][DFF : DFF + D]
     head_rows = copies[3][DFF + D :]
-    pixel_rows = pixels[0]
     keep_rows = keep_index[0]
-    batch = pixel_rows.shape[0]
-    kept_pixels = jnp.take_along_axis(pixel_rows, keep_rows[..., None], 1)
-    kept_bands = jnp.take_along_axis(band_group[0], keep_rows, 1)
+    batch = keep_rows.shape[0]
+    places = jnp.arange(L, dtype=jnp.int32)
+    keep_hot = keep_rows[..., None] == places
+    shown = jnp.any(keep_hot, 1)
+    earlier = (places[:, None] <= places[None, :]).astype(jnp.bfloat16)
+    rank = jnp.dot(
+        1.0 - shown.astype(jnp.bfloat16), earlier, preferred_element_type=jnp.float32
+    ).astype(jnp.int32)
+    hide_hot = (rank[:, None, :] - 1 == jnp.arange(L - K, dtype=jnp.int32)[:, None]) & ~shown[:, None]
+    order_hot = jnp.concatenate([keep_hot, hide_hot], 1)
+    order_low = order_hot.astype(jnp.bfloat16)
+    pixel_rows = jnp.einsum("bsl,blp->bsp", order_low, pixels[0])
+    order_gsd = jnp.sum(jnp.where(order_hot, gsd_index[0][:, None, :], 0), -1)
+    kept_bands = jnp.sum(jnp.where(keep_hot, band_group[0][:, None, :], 0), -1)
+    kept_pixels = pixel_rows[:, :K]
     onehot = (kept_bands[..., None] == jnp.arange(NBG, dtype=jnp.int32)).astype(jnp.bfloat16)
     spread = (onehot[..., None] * kept_pixels[:, :, None, :]).reshape(batch, K, NBG * PIX)
-    position = jnp.take(gsd_table[0], gsd_index[0], axis=0)
-    enc_input = project(spread, embed_w) + jnp.take_along_axis(
-        position[..., :D], keep_rows[..., None], 1
+    gsd_hot = (
+        order_gsd[..., None] == jnp.arange(gsd_table.shape[1], dtype=jnp.int32)
+    ).astype(jnp.bfloat16)
+    table_high = to_low(gsd_table[0])
+    table_low = to_low(gsd_table[0] - table_high.astype(jnp.float32))
+    enc_input = (
+        project(spread, embed_w)
+        + project(gsd_hot[:, :K], table_high[:, :D])
+        + project(gsd_hot[:, :K], table_low[:, :D])
     )
     enc_out, enc_saved = block_forward(enc_input, enc_copy, enc_down, enc_gains, HEADS)
     enc_final, enc_hat, enc_scale = norm_forward(enc_out, enc_gains[4], enc_gains[5])
     enc_low = to_low(enc_final)
     latent = project(enc_low, dec_embed)
-    item_rows = jnp.arange(batch)[:, None]
-    hidden_mask = jnp.ones((batch, L), jnp.float32).at[item_rows, keep_rows].set(0.0)
-    dec_input = hidden_mask[..., None] * dec_gains[6] + position[..., D:]
-    dec_input = dec_input.at[item_rows, keep_rows].add(latent)
-    dec_out, dec_saved = block_forward(dec_input, dec_copy, dec_down, dec_gains, DHEADS)
-    dec_final, dec_hat, dec_scale = norm_forward(dec_out, dec_gains[4], dec_gains[5])
-    dec_low = to_low(dec_final)
-    predicted = project_back(dec_low, head_rows)
-    pixel_float = pixel_rows.astype(jnp.float32)
-    centred = pixel_float - jnp.mean(pixel_float, -1, keepdims=True)
-    target = centred * lax.rsqrt(jnp.mean(centred * centred, -1, keepdims=True) + norm_eps)
+    dec_position = project(gsd_hot, table_high[:, D:]) + project(gsd_hot, table_low[:, D:])
     first_item = lax.axis_index("dp") * batch
     valid = (first_item + jnp.arange(batch, dtype=jnp.int32) < group_items[0]).astype(jnp.float32)
-    token_weight = hidden_mask * valid[:, None]
-    error = predicted - target
-    loss_local = jnp.sum(token_weight * jnp.mean(error * error, -1))
-    grad_pred = to_low(token_weight[..., None] * error * (2.0 / PIX) / masked)
-    grad_head = weight_grad(grad_pred, dec_low)
-    back_dec, gain_df, shift_df = norm_backward(
-        project(grad_pred, head_rows), dec_hat, dec_scale, dec_gains[4]
-    )
-    grad_dec_in, grad_dcols, grad_ddown, dec_block_gains = block_backward(
-        back_dec, dec_copy, dec_down, dec_gains, DHEADS, dec_saved
-    )
-    grad_token = jnp.sum(grad_dec_in * hidden_mask[..., None], (0, 1))
-    grad_latent = to_low(jnp.take_along_axis(grad_dec_in, keep_rows[..., None], 1))
+    scal = jnp.stack([valid / PIX, valid * (2.0 / PIX) / masked])
+    grad_latent, grad_dcols, grad_ddown, grad_head, dec_sums, loss_local = decoder_call(
+        scal,
+        latent,
+        dec_position,
+        pixel_rows[:, K:],
+        dec_copy,
+        dec_down,
+        head_rows,
+        dec_gains,
+        DHEADS,
+    )
+    loss_local = loss_local[0, 0]
     grad_dembed = weight_grad(enc_low, grad_latent)
     back_enc, gain_ef, shift_ef = norm_backward(
         project_back(grad_latent, dec_embed), enc_hat, enc_scale, enc_gains[4]
@@ -284,27 +994,34 @@
         back_enc, enc_copy, enc_down, enc_gains, HEADS, enc_saved
     )
     grad_embed = weight_grad(spread, to_low(grad_enc_in))
-    grads = (
-        grad_ecols,
-        jnp.concatenate([grad_edown, grad_embed], 0),
-        grad_dcols,
-        jnp.concatenate([grad_ddown, grad_dembed, grad_head], 0),
-    )
+
+    def reduce_rows(pieces, axis):
+        whole = jnp.concatenate([to_low(piece) for piece in pieces], axis)
+        return lax.psum_scatter(whole, "dp", scatter_dimension=0, tiled=True)
+
+    dec_shards = (
+        reduce_rows((grad_dcols,), 1),
+        reduce_rows((grad_ddown, grad_dembed, grad_head), 0),
+    )
+    dec_shards = tuple(lax.psum(piece, "grp") for piece in dec_shards)
     grad_egains = jnp.concatenate([enc_block_gains, jnp.stack([gain_ef, shift_ef])], 0)
-    grad_dgains = jnp.concatenate([dec_block_gains, jnp.stack([gain_df, shift_df, grad_token])], 0)
-    shards = (
-        lax.psum_scatter(grads[0], "dp", scatter_dimension=0, tiled=True),
-        lax.psum_scatter(grads[1], "dp", scatter_dimension=0, tiled=True),
-        lax.psum_scatter(grads[2], "dp", scatter_dimension=0, tiled=True),
-        lax.psum_scatter(grads[3], "dp", scatter_dimension=0, tiled=True),
-    )
-    shards = (
-        lax.psum(shards[0].astype(jnp.bfloat16), "grp").astype(jnp.float32),
-        lax.psum(shards[1].astype(jnp.bfloat16), "grp").astype(jnp.float32),
-        lax.psum(shards[2].astype(jnp.bfloat16), "grp").astype(jnp.float32),
-        lax.psum(shards[3].astype(jnp.bfloat16), "grp").astype(jnp.float32),
-    )
-    enc_sum, dec_sum, loss_sum = lax.psum((grad_egains, grad_dgains, loss_local), ("grp", "dp"))
+    grad_dgains = dec_sums[:7]
+    if direct:
+        flat = jnp.concatenate([grad_egains.reshape(-1), grad_dgains.reshape(-1), loss_local[None]])
+        count_e, count_d = grad_egains.size, grad_dgains.size
+        small = jnp.pad(flat, (0, 16 * D - flat.shape[0])).reshape(16, D)
+        ecols_shard, erows_shard, small = reduce_encoder(
+            to_low(grad_edown), to_low(grad_embed), *[to_low(piece) for piece in grad_ecols], small
+        )
+        flat = small.reshape(-1)
+        enc_sum = flat[:count_e].reshape(grad_egains.shape)
+        dec_sum = flat[count_e : count_e + count_d].reshape(grad_dgains.shape)
+        loss_sum = flat[count_e + count_d]
+    else:
+        enc_sum, dec_sum, loss_sum = lax.psum((grad_egains, grad_dgains, loss_local), ("grp", "dp"))
+        ecols_shard = lax.psum(reduce_rows(grad_ecols, 1), "grp")
+        erows_shard = lax.psum(reduce_rows((grad_edown, grad_embed), 0), "grp")
+    shards = tuple(piece.astype(jnp.float32) for piece in (ecols_shard, erows_shard) + dec_shards)
     shard_squares = lax.psum(sum((jnp.sum(piece * piece) for piece in shards)), "dp")
     loss = loss_sum / masked
     grad_norm = jnp.sqrt(shard_squares + jnp.sum(enc_sum * enc_sum) + jnp.sum(dec_sum * dec_sum))

time: 1730 us -> 870 us (0.50)
  waiting for transfers between devices: 892 us -> 29.7 us
  Pallas kernels: 0 us -> 520 us
  other arithmetic: 265 us -> 52.5 us
  matrix products: 310 us -> 130 us
  local copies, waits for them, and re-layouts: 157 us -> 82.8 us
  blocking collectives: 68.3 us -> 26.1 us
    reduce_scatter x4 -> x2, waiting for transfers between devices: 639 us -> 29.6 us  [reduce_rows(): return lax.psum_scatter(whole, 'dp', scatter_dimension=0, tiled=True)]
    pallas_call x0 -> x3, Pallas kernels: none -> 520 us  [the longest x1 205 us: reduce_call(): pl.pallas_call(functools.partial(reduce_kernel, len(grads), len(out_shape...]
    all_gather x4 -> x2, waiting for transfers between devices: 171 us -> 0.01 us  [gather_rows(): return lax.all_gather(to_low(mine), ('dp', 'grp'), axis=0, tiled=True)]
    psum x1, waiting for transfers between devices: 81.2 us -> 0.01 us  [body(): dec_shards = tuple((lax.psum(piece, 'grp') for piece in dec_shards))]
    scatter-add x1 -> x0, other arithmetic: 64.8 us -> none  [body(): dec_input = dec_input.at[item_rows, keep_rows].add(latent)]
    concatenate x4 -> x2, other arithmetic: 49.2 us -> 2.82 us  [the longest x1 2.17 us: reduce_rows(): whole = jnp.concatenate([to_low(piece) for piece in pieces], axis)]
    gather x8 -> x0, local copies, waits for them, and re-layouts: 40.1 us -> none  [the longest x1 11 us: body(): position = jnp.take(gsd_table[0], gsd_index[0], axis=0)]
    psum x1 -> x0, blocking collectives: 38.8 us -> none  [body(): lax.psum((grad_egains, grad_dgains, loss_local), ('grp', 'dp'))]
  transfers between devices with their start and end apart: 9 -> 5, of which waited for: 6 -> 1; matrix products, arithmetic and copies ran while one was open for 24% -> 25% of each run, Pallas kernels for 0% -> 42%
where the time goes in v1:
time: 870 us; the launch traced here: 866 us
  Pallas kernels  520 us (60%)
  matrix products  130 us (15%)
  local copies, waits for them, and re-layouts  82.8 us (10%)
  other arithmetic  52.5 us (6%)
  waiting for transfers between devices  29.7 us (3%)
  blocking collectives  26.1 us (3%)
  between operations  24.7 us (3%)
    pallas_call x1, Pallas kernels, reduce_call(): pl.pallas_call(functools.partial(reduce_kernel, len(grads), len(out_shape...  205 us
    pallas_call x1, Pallas kernels, decoder_call(): pl.pallas_call(functools.partial(decoder_kernel, items, heads), grid=(bat...  161 us
    pallas_call x1, Pallas kernels, gather_call(): pl.pallas_call(functools.partial(gather_kernel, count, chunks, ahead), ou...  154 us
    dot_general x10, matrix products, project(): jnp.einsum('...n,nm->...m', inputs, matrix, preferred_element_type=jnp.fl...  41.2 us
    dot_general x5, matrix products, project_back(): jnp.einsum('...m,nm->...n', grads, matrix, preferred_element_type=jnp.flo...  33.8 us
    dot_general x6, matrix products, weight_grad(): lax.dot_general(flat_in, flat_grad, (((0,), (0,)), ((), ())), preferred_e...  33.7 us
    reduce_scatter x2, waiting for transfers between devices, reduce_rows(): return lax.psum_scatter(whole, 'dp', scatter_dimension=0, tiled=True)  29.6 us
    unnamed x152, local copies, waits for them, and re-layouts  24.3 us
  transfers between devices with their start and end apart: 5, of which 1 were waited for; matrix products, arithmetic and copies ran while one was open for 25% of the time, Pallas kernels for 42%

profile of v1, /device:TPU:0, one launch (start us, length us, event | category | flops | bytes accessed | tf_op | source)
XLA Modules:
  0.0 866.5 jit_solution(2964667816746304129)
XLA Ops:
  12.0 3.5 fusion.23
  18.1 4.1 broadcast_multiply_fusion
  22.1 7.8 mul.461
  29.9 4.0 convert_element_type.135
  35.5 154.2 %shard_map.392 = (bf16[4,2,4,256,1024]{4,3,2,1,0:T(8,128)(2,1)}, bf16[4,2,4,32,8192]{4,3,2,1,0:T(8,128)(2,1)}) custom-call(bf16[4,256,1024]{2,1,0:T(8,128)(2,1)} %bitcast.158, bf16[4,32,8192]{2,1,0:T(8,128)(2,1)} %bitcast.159), custom_call_target="tpu_custom_call" | custom-call | tf_op jit(solution)/shard_map/pallas_call | solution.py:603
  189.7 9.6 %fusion.92 = (bf16[2,2,4,256,1024]{4,3,2,1,0:T(8,128)(2,1)}, bf16[2,2,4,256,1024]{4,3,2,1,0:T(8,128)(2,1)S(1)}) fusion(bf16[4,2,4,256,1024]{4,3,2,1,0:T(8,128)(2,1)} %get-tuple-element.31), kind=kLoop, calls=%fused_computation.195 | loop fusion | bytes 33554432 | tf_op jit(solution)/shard_map/slice | solution.py:935
  200.9 2.9 copy-done.26
  203.7 4.6 fusion.98
  210.5 8.0 fusion.10
  219.1 11.1 %psum.28 = f32[]{:T(128)} all-reduce(f32[]{:T(128)} %bitcast.24), channel_id=1, replica_groups=mesh['grp'=4,'dp'=8] {'grp'}, use_global_device_ids=true, to_apply=%region_11.12 | all-reduce | flops 1 | bytes 8 | tf_op jit(solution)/shard_map/psum | solution.py:926
  230.2 4.0 slice.148.pix_ref
  236.0 2.8 copy.89
  238.7 2.7 copy.90
  241.5 2.4 reshape.293
  243.8 6.5 copy.92
  252.2 3.3 multiply_reduce_fusion.1
  259.9 3.7 fusion.96
  264.0 10.7 %multiply_convert_fusion = (bf16[8,64,4096]{2,1,0:T(8,128)(2,1)S(1)}, f32[8,64,4096]{2,1,0:T(8,128)}) fusion(bf16[1024,8192]{1,0:T(8,128)(2,1)} %bitcast.178, f32[8,64,1024]{2,1,0:T(8,128)S(1)} %get-tuple-element.92, f32[1024]{0:T(1024)S(1)} %bitcast.206, f32[1024]{0:T(1024)S(1)} %bitcast.183, f32[8,64]{1,0:T(8,128)S(1)} %add_rsqrt_fusion.1, ...), kind=kOutput, calls=%fused_computation.11 | convolution fusion | flops 4308074496 | bytes 23080960 | tf_op jit(solution)/shard_map/...n,nm->...m/dot_general | solution.py:36
  274.8 4.6 fusion.97
  279.8 2.3 fusion.27
  282.1 3.9 fusion.29.pos_ref
  286.0 3.2 slice.149.down_ref
  292.0 160.7 %shard_map.393 = (bf16[8,64,512]{2,1,0:T(8,128)(2,1)}, bf16[512,4096]{1,0:T(8,128)(2,1)}, bf16[2048,512]{1,0:T(8,128)(2,1)}, bf16[1024,512]{1,0:T(8,128)(2,1)}, f32[8,512]{1,0:T(8,128)}, /*index=5*/f32[1,1]{1,0:T(1,128)}) custom-call(f32[2,8]{1,0:T(2,128)} %pad_maximum_fusion.4.scal_ref, f32[8,64,512]{2,1,0:T(8,128)} %fusion.55.z_ref, ...), custom_call_target="tpu_custom_call" | custom-call | flops 70000001024 | bytes 40000000 | tf_op jit(solution)/shard_map/pallas_call | solution.py:427
  458.1 2.4 multiply_reduce_fusion.2
  461.1 10.9 %fusion.5 = bf16[8,64,4096]{2,1,0:T(8,128)(2,1)S(1)} fusion(f32[8,64,4096]{2,1,0:T(8,128)} %get-tuple-element.94, bf16[4096,1024,1]{1,0,2:T(8,128)(2,1)} %bitcast.161, f32[8,64,1024]{2,1,0:T(8,128)S(1)} %subtract_multiply_fusion), kind=kOutput, calls=%fused_computation.9 | convolution fusion | flops 4316463104 | bytes 23068672 | tf_op jit(solution)/shard_map/...m,nm->...n/dot_general | solution.py:40
  472.1 9.1 %multiply_reduce_fusion.3 = (f32[1024]{0:T(1024)S(1)}, f32[8,64]{1,0:T(8,128)S(1)}, f32[8,64]{1,0:T(8,128)S(1)}, f32[1024]{0:T(1024)S(1)}, f32[8,64,1024]{2,1,0:T(8,128)S(1)}) fusion(f32[8,64,1024]{2,1,0:T(8,128)S(1)} %copy-done.9, f32[8,64]{1,0:T(8,128)S(1)} %add_rsqrt_fusion.1, f32[8,64]{1,0:T(8,128)S(1)} %broadcast_multiply_fusion.8, ...), kind=kOutput, calls=%fused_computation.63 | convolution fusion | flops 4299682816 | bytes 16797696 | tf_op jit(solution)/shard_map/...m,nm->...n/dot_general | solution.py:40
  483.3 2.9 fusion.39
  488.3 4.6 multiply_reduce_fusion
  495.8 2.8 copy.72
  498.6 3.3 reshape.297
  501.8 2.8 fusion.36
  504.7 2.8 copy.76
  507.4 4.1 reshape.298
  511.5 4.8 convolution_convert_fusion.1
  516.3 2.9 copy.79
  519.2 8.5 multiply_reduce_fusion.4
  529.2 3.1 add_convert_fusion
  532.6 7.0 convolution_convert_fusion
  539.6 6.2 bitcast_convert_fusion.2
  545.8 7.2 bitcast_convert_fusion
  553.1 7.0 bitcast_convert_fusion.1
  560.1 29.6 %reduce-scatter.3.cloned.1.call-done = bf16[64,4096]{1,0:T(8,128)(2,1)} async-done(((bf16[512,4096]{1,0:T(8,128)(2,1)}), bf16[64,4096]{1,0:T(8,128)(2,1)}) %reduce-scatter.3.cloned.1.call-update) | async-done | bytes 524304 | tf_op jit(solution)/shard_map/reduce_scatter | solution.py:1000
  589.7 4.2 bitcast_convert_fusion.3
  593.9 205.4 %shard_map.394 = (bf16[4,256,1024]{2,1,0:T(8,128)(2,1)}, bf16[4,32,8192]{2,1,0:T(8,128)(2,1)}, f32[16,1024]{1,0:T(8,128)}) custom-call(bf16[2,2,4,256,1024]{4,3,2,1,0:T(8,128)(2,1)} %bitcast.167, bf16[2,2,4,256,1024]{4,3,2,1,0:T(8,128)(2,1)} %bitcast.165, bf16[4,2,4,32,3072]{4,3,2,1,0:T(8,128)(2,1)} %bitcast.171, bf16[4,2,4,32,1024]{4,3,2,1,0:T(8,128)(2,1)} %bitcast.173, ...), custom_call_target="tpu_custom_call" | custom-call | tf_op jit(solution)/shard_map/pallas_call | solution.py:823
  801.7 3.3 fusion.11
  815.0 15.0 %psum.31 = f32[]{:T(128)} all-reduce(f32[]{:T(128)S(6)} %add.262), channel_id=1, replica_groups=mesh['grp'=4,'dp'=8] {'dp'}, use_global_device_ids=true, to_apply=%region_33.34 | all-reduce | flops 1 | bytes 8 | tf_op jit(solution)/shard_map/psum | solution.py:1025
  845.7 5.2 fusion.22
  851.0 6.5 fusion.17
  (230 shorter events, 60.0 us)
Async XLA Ops:
  7.2 278.9 %all-gather.3.cloned.1.call-start = ((), (), s32[]{:S(2)}) async-start(), calls=%async_computation.2 | async-start | bytes 4325376 | tf_op jit(solution)/shard_map/all_gather | solution.py:924
  8.9 283.1 %all-gather.5.cloned.1.call-start = ((), (), s32[]{:S(2)}) async-start(), calls=%async_computation.3 | async-start | bytes 4325376 | tf_op jit(solution)/shard_map/all_gather | solution.py:924
  10.6 549.5 %reduce-scatter.5.cloned.1.call-start = ((), (), s32[]{:S(2)}) async-start(), calls=%async_computation.5 | async-start | bytes 4718592 | tf_op jit(solution)/shard_map/reduce_scatter | solution.py:1000
  12.0 5.6 copy-start.61
  12.0 5.6 copy-start.63
  189.6 9.6 %copy-start.62 = (s32[1,8,256]{2,1,0:T(8,128)S(1)}, s32[1,8,256]{2,1,0:T(8,128)}, u32[]{:S(2)}) copy-start(s32[1,8,256]{2,1,0:T(8,128)} %param.28) | copy-start | bytes 24580
  189.7 10.8 %copy-start.30 = (f32[1,512,1536]{2,1,0:T(8,128)S(1)}, f32[1,512,1536]{2,1,0:T(8,128)}, u32[]{:S(2)}) copy-start(f32[1,512,1536]{2,1,0:T(8,128)} %param.29) | copy-start | bytes 9437188
  200.9 7.5 copy-start.32
  200.9 8.2 copy-start.24
  210.0 49.9 %copy-start.2 = (f32[8,64,1024]{2,1,0:T(8,128)}, f32[8,64,1024]{2,1,0:T(8,128)S(1)}, u32[]{:S(2)}) copy-start(f32[8,64,1024]{2,1,0:T(8,128)S(1)} %get-tuple-element.88) | copy-start | bytes 6291460
  210.0 8.5 copy-start.49
  210.4 8.1 copy-start.55
  210.4 8.0 copy-start.53
  210.4 8.0 copy-start.66
  210.4 53.6 %copy-start.64 = (f32[1,1024]{1,0:T(1,128)}, f32[1,1024]{1,0:T(1,128)S(1)}, u32[]{:S(2)}) copy-start(f32[1,1024]{1,0:T(1,128)S(1)} %get-tuple-element.80) | copy-start | bytes 12292
  263.6 11.2 %copy-start.8 = (f32[8,64,1024]{2,1,0:T(8,128)}, f32[8,64,1024]{2,1,0:T(8,128)S(1)}, u32[]{:S(2)}) copy-start(f32[8,64,1024]{2,1,0:T(8,128)S(1)} %get-tuple-element.92) | copy-start | bytes 6291460
  263.6 11.1 %slice-start = ((s8[8388608]{0:T(1024)(128)(4,1)}), s8[4194304]{0:T(1024)(128)(4,1)S(1)}, s32[]{:S(2)}) async-start(s8[8388608]{0:T(1024)(128)(4,1)} %bitcast.162), calls=%async_computation.7 | async-start | bytes 8388608
  264.0 10.8 %slice-start.1 = ((s8[8388608]{0:T(1024)(128)(4,1)}), s8[4194304]{0:T(1024)(128)(4,1)S(1)}, s32[]{:S(2)}) async-start(s8[8388608]{0:T(1024)(128)(4,1)} %bitcast.162), calls=%async_computation.8 | async-start | bytes 8388608
  457.1 132.6 %reduce-scatter.3.cloned.1.call-start = ((), (), s32[]{:S(2)}) async-start(), calls=%async_computation.4 | async-start | bytes 4718592 | tf_op jit(solution)/shard_map/reduce_scatter | solution.py:1000
  461.1 20.2 %copy-start.22 = (f32[8,64,1024]{2,1,0:T(8,128)}, f32[8,64,1024]{2,1,0:T(8,128)S(1)}, u32[]{:S(2)}) copy-start(f32[8,64,1024]{2,1,0:T(8,128)S(1)} %subtract_multiply_fusion) | copy-start | bytes 6291460
  461.1 11.0 %copy-start.9 = (f32[8,64,1024]{2,1,0:T(8,128)S(1)}, f32[8,64,1024]{2,1,0:T(8,128)}, u32[]{:S(2)}) copy-start(f32[8,64,1024]{2,1,0:T(8,128)} %copy-done.8) | copy-start | bytes 6291460
  472.1 9.1 %copy-start.71 = (bf16[8,64,4096]{2,1,0:T(8,128)(2,1)}, bf16[8,64,4096]{2,1,0:T(8,128)(2,1)S(1)}, u32[]{:S(2)}) copy-start(bf16[8,64,4096]{2,1,0:T(8,128)(2,1)S(1)} %fusion.5) | copy-start | bytes 12582916
  504.7 6.9 copy-start.7
  519.2 8.6 copy-start.60
  529.1 280.1 %all-reduce.4.cloned.1.call-start = ((), (), s32[]{:S(2)}) async-start(), calls=%async_computation.6 | async-start | bytes 2097152 | tf_op jit(solution)/shard_map/psum | solution.py:1006
  532.6 7.0 copy-start.39
  532.6 7.0 copy-start.40
  532.6 7.0 copy-start.67
  539.6 6.2 copy-start.10
  539.6 6.2 copy-start.65
  539.6 6.2 copy-start.72
  545.8 7.3 copy-start.23
  545.8 7.3 copy-start.70
  553.1 36.6 %copy-start.20 = (f32[8,64,1024]{2,1,0:T(8,128)S(1)}, f32[8,64,1024]{2,1,0:T(8,128)}, u32[]{:S(2)}) copy-start(f32[8,64,1024]{2,1,0:T(8,128)} %copy-done.19) | copy-start | bytes 6291460
  799.3 5.7 copy-start.18
  799.4 9.2 %copy-start.46 = (f32[16,1024]{1,0:T(8,128)S(1)}, f32[16,1024]{1,0:T(8,128)}, u32[]{:S(2)}) copy-start(f32[16,1024]{1,0:T(8,128)} %get-tuple-element.41) | copy-start | bytes 196612
  833.6 8.8 %copy-start.15 = (f32[4,256,1024]{2,1,0:T(8,128)}, f32[4,256,1024]{2,1,0:T(8,128)S(1)}, u32[]{:S(2)}) copy-start(f32[4,256,1024]{2,1,0:T(8,128)S(1)} %convert_multiply_fusion) | copy-start | bytes 12582916
  833.7 4.6 copy-start.42
  833.7 6.7 copy-start.38
  833.7 6.7 copy-start.43
  833.7 6.7 copy-start.44
  834.2 16.8 %copy-start.16 = (f32[4,32,8192]{2,1,0:T(8,128)}, f32[4,32,8192]{2,1,0:T(8,128)S(1)}, u32[]{:S(2)}) copy-start(f32[4,32,8192]{2,1,0:T(8,128)S(1)} %convert_multiply_fusion.2) | copy-start | bytes 12582916
  834.9 5.5 copy-start.34
  838.3 4.7 copy-start.27
  838.3 6.3 copy-start.28
  840.4 5.3 copy-start.12
  845.7 5.3 copy-start.14
  845.7 5.3 copy-start.29
  (32 other events, 87.6 us)
Sparse Core Ops, SparseCore 0:
  11.5 86.1 all-gather.2
  101.2 79.1 all-gather.4
  457.2 60.0 reduce-scatter.4
  529.2 60.3 reduce-scatter.2
  592.5 66.1 all-reduce.3

commit v2 on v1

v2 whole, which is shorter than its diff:
```python
import functools

import jax
import jax.numpy as jnp
from jax import lax
from jax.experimental import pallas as pl
from jax.experimental.pallas import tpu as pltpu
from jax.sharding import PartitionSpec as P

D = 1024
HEADS = 16
FF = 4096
DHEADS = 16
DFF = 2048
PIX = 1024
NBG = 4
L = 256
K = 64


norm_eps = 1e-06
clip_level = 0.005
learn_rate = 0.02
gain_rate = 0.25
weight_decay = 0.05
adam_eps = 1e-08
beta_first = 0.5
beta_second = 0.5


def to_low(value):
    return value.astype(jnp.bfloat16)


def project(inputs, matrix):
    return jnp.einsum("...n,nm->...m", inputs, matrix, preferred_element_type=jnp.float32)


def dot_nn(a, b):
    return lax.dot_general(a, b, (((1,), (0,)), ((), ())), preferred_element_type=jnp.float32)


def dot_nt(a, b):
    return lax.dot_general(a, b, (((1,), (1,)), ((), ())), preferred_element_type=jnp.float32)


def dot_tn(a, b):
    return lax.dot_general(a, b, (((0,), (0,)), ((), ())), preferred_element_type=jnp.float32)


def unit_rows(values):
    centred = values - jnp.mean(values, -1, keepdims=True)
    scaled = lax.rsqrt(jnp.mean(centred * centred, -1, keepdims=True) + norm_eps)
    return centred * scaled, scaled


def unit_back(grads, hat, scaled, gain):
    inner = grads * gain
    return scaled * (
        inner
        - jnp.mean(inner, -1, keepdims=True)
        - hat * jnp.mean(inner * hat, -1, keepdims=True)
    )

LANES = 128


def stack_rows(value, ee):
    head = lax.broadcasted_iota(jnp.int32, value.shape, 1) // ee
    return jnp.concatenate(
        [jnp.where(head == h, value, jnp.zeros_like(value)) for h in range(LANES // ee)], 0
    )


def stack_lanes(value, ee):
    head = lax.broadcasted_iota(jnp.int32, value.shape, 0) // ee
    return jnp.concatenate(
        [jnp.where(head == h, value, jnp.zeros_like(value)) for h in range(LANES // ee)], 1
    )


def attend(n, groups, tokens, width, ee, expo, same, qkv_s, s_s, p_s, inv_s, oo_s, o_s):
    item = n // groups
    g = n % groups
    rs = pl.ds(pl.multiple_of(item * tokens, tokens), tokens)
    qa = pl.ds(pl.multiple_of(g * LANES, LANES), LANES)
    q = qkv_s[rs, qa]
    k = qkv_s[rs, pl.ds(pl.multiple_of(width + g * LANES, LANES), LANES)]
    v = qkv_s[rs, pl.ds(pl.multiple_of(2 * width + g * LANES, LANES), LANES)]
    s_s[...] = dot_nt(stack_rows(q, ee), k)
    for h in range(LANES // ee):
        at = slice(h * tokens, (h + 1) * tokens)
        s = s_s[at, :]
        if same is not None:
            s = jnp.where(same, s, -1e30)
        top = jnp.max(s, -1, keepdims=True)
        p_s[n, :, at] = jnp.exp2((s - top) * expo).astype(p_s.dtype)
    ones = jnp.ones_like(v)
    both = jnp.concatenate([stack_rows(v, ee), stack_rows(ones, ee)], 1)
    out = dot_nn(p_s[n], both)
    inv = 1.0 / out[:, LANES:]
    out = out[:, :LANES] * inv
    inv_s[n] = inv
    oo_s[n] = out
    o_s[rs, qa] = out.astype(o_s.dtype)


def attend_back(n, groups, tokens, width, ee, scale, qkv_s, s_s, ds_s, p_s, inv_s, oo_s, do_s, dqkv_s):
    low = dqkv_s.dtype
    item = n // groups
    g = n % groups
    rs = pl.ds(pl.multiple_of(item * tokens, tokens), tokens)
    qa = pl.ds(pl.multiple_of(g * LANES, LANES), LANES)
    ka = pl.ds(pl.multiple_of(width + g * LANES, LANES), LANES)
    va = pl.ds(pl.multiple_of(2 * width + g * LANES, LANES), LANES)
    heads = range(LANES // ee)
    do = do_s[rs, qa].astype(jnp.float32) * inv_s[n]
    rest = (-do * oo_s[n]).astype(low)
    do_t = do.T.astype(low)
    do = do.astype(low)
    v = qkv_s[rs, va]
    s_s[...] = dot_nt(
        jnp.concatenate([stack_rows(do, ee), stack_rows(rest, ee)], 1),
        jnp.concatenate([v, jnp.ones_like(v)], 1),
    )
    for h in heads:
        at = slice(h * tokens, (h + 1) * tokens)
        ds_s[:, at] = (p_s[n, :, at].astype(jnp.float32) * s_s[at, :]).astype(low)
    e_rows = jnp.concatenate([p_s[n, :, h * tokens : (h + 1) * tokens] for h in heads], 0)
    ds_rows = jnp.concatenate([ds_s[:, h * tokens : (h + 1) * tokens] for h in heads], 0)
    dv_t = dot_nn(stack_lanes(do_t, ee), e_rows)
    dk_t = dot_nn(stack_lanes(qkv_s[rs, qa].T, ee), ds_rows)
    dq = dot_nn(ds_s[...], stack_rows(qkv_s[rs, ka], ee))
    dqkv_s[rs, qa] = (dq * scale).astype(low)
    dqkv_s[rs, ka] = (dk_t.T * scale).astype(low)
    dqkv_s[rs, va] = dv_t.T.astype(low)


def one_hot(index, count):
    places = lax.broadcasted_iota(jnp.int32, (index.shape[0], count), 1)
    return jnp.where(places.astype(jnp.float32) == index.astype(jnp.float32), 1.0, 0.0)


def split_table(table_ref, high_s, low_s):
    high = table_ref[...].astype(high_s.dtype)
    high_s[...] = high
    low_s[...] = (table_ref[...] - high.astype(jnp.float32)).astype(low_s.dtype)


def look_up(hot, index_row, high_s, low_s):
    index = jnp.sum(hot * index_row, -1, keepdims=True)
    rows = one_hot(index, high_s.shape[0]).astype(high_s.dtype)
    return dot_nn(rows, high_s[...]) + dot_nn(rows, low_s[...])


def decoder_kernel(
    items, heads, scal_ref, z_ref, keep_ref, gsd_ref, table_ref, pix_ref, cols_ref, down_ref, head_ref, gains_ref,
    dz_ref, gcols_out, gdown_out, ghead_out, ggains_ref, loss_ref,
    x_s, h1_s, qkv_s, p_s, o_s, x1_s, h2_s, a_s, gp_s, x2_s, hd_s, dx_s, dy_s, acc_s, dqkv_s, inv_s, oo_s, s_s, ds_s,
    high_s, low_s, pixel_s, gcols, gdown, ghead,
):
    low = jnp.bfloat16
    step = pl.program_id(0)
    width = x_s.shape[1]
    tokens = pix_ref.shape[1]
    hide = tokens - K
    rows = items * tokens
    tile = 512
    ee = width // heads
    scale = ee ** (-0.5)
    expo = scale * 1.4426950408889634

    @pl.when(step == 0)
    def _():
        gcols[...] = jnp.zeros_like(gcols)
        gdown[...] = jnp.zeros_like(gdown)
        ghead[...] = jnp.zeros_like(ghead)
        ggains_ref[...] = jnp.zeros_like(ggains_ref)
        loss_ref[...] = jnp.zeros_like(loss_ref)
        split_table(table_ref, high_s, low_s)

    def gain(i):
        return gains_ref[i : i + 1, :]

    f32 = jnp.float32
    before = lax.broadcasted_iota(jnp.int32, (tokens, tokens), 0) <= lax.broadcasted_iota(
        jnp.int32, (tokens, tokens), 1
    )
    before = before.astype(f32).astype(low)
    for i in range(items):
        base = i * tokens
        keep_hot = one_hot(keep_ref[i], tokens)
        shown = jnp.max(keep_hot, 0, keepdims=True)
        rank = dot_nn(jnp.broadcast_to(1.0 - shown, (8, tokens)).astype(low), before)[:1]
        slot = lax.broadcasted_iota(jnp.int32, (hide, tokens), 0).astype(f32) + 1.0
        hide_hot = jnp.where(slot == rank, 1.0 - shown, 0.0)
        position = look_up(jnp.concatenate([keep_hot, hide_hot], 0), gsd_ref[i], high_s, low_s)
        x_s[base : base + K, :] = position[:K] + z_ref[i]
        x_s[base + K : base + tokens, :] = position[K:] + gain(6)
        pixel_s[i] = dot_nn(hide_hot.astype(low), pix_ref[i]).astype(low)
    hat, _ = unit_rows(x_s[...])
    h1_s[...] = (hat * gain(0) + gain(1)).astype(low)

    @pl.loop(0, 3)
    def _(t):
        at = pl.ds(pl.multiple_of(t * width, width), width)
        qkv_s[:, at] = dot_nn(h1_s[...], cols_ref[:, at]).astype(low)

    groups = width // LANES

    @pl.loop(0, items * groups)
    def _(n):
        attend(n, groups, tokens, width, ee, expo, None, qkv_s, s_s, p_s, inv_s, oo_s, o_s)

    x1_s[...] = x_s[...] + dot_nn(o_s[...], cols_ref[:, 3 * width : 4 * width])
    hat, _ = unit_rows(x1_s[...])
    h2_s[...] = (hat * gain(2) + gain(3)).astype(low)
    x2_s[...] = x1_s[...]

    @pl.loop(0, down_ref.shape[0] // tile)
    def _(t):
        at = pl.ds(pl.multiple_of(t * tile, tile), tile)
        up = pl.ds(pl.multiple_of(4 * width + t * tile, tile), tile)
        u = dot_nn(h2_s[...], cols_ref[:, up])
        cumul = 0.5 * (1.0 + lax.erf(u * 0.7071067811865476))
        act = (u * cumul).astype(low)
        a_s[:, at] = act
        gp_s[:, at] = (cumul + u * jnp.exp(-0.5 * u * u) * 0.3989422804014327).astype(gp_s.dtype)
        x2_s[...] += dot_nn(act, down_ref[at, :])

    hat, _ = unit_rows(x2_s[...])
    hd_s[...] = (hat * gain(4) + gain(5)).astype(low)

    pixel_count = head_ref.shape[0]
    for i in range(items):
        base = i * tokens
        weight = scal_ref[0, step * items + i]
        coef = scal_ref[1, step * items + i]
        target, _ = unit_rows(pixel_s[i].astype(f32))
        hd = hd_s[base + K : base + tokens, :]
        back = jnp.zeros((hide, width), jnp.float32)
        for t in range(pixel_count // tile):
            at = slice(t * tile, (t + 1) * tile)
            err = dot_nt(hd, head_ref[at, :]) - target[:, at]
            loss_ref[...] += weight * jnp.sum(err * err, keepdims=True).reshape(1, 1)
            dpred = (err * coef).astype(low)
            ghead[at, :] += dot_tn(dpred, hd)
            back = back + dot_nn(dpred, head_ref[at, :])
        hat, scaled = unit_rows(x2_s[base + K : base + tokens, :])
        ggains_ref[4:5, :] += jnp.sum(back * hat, 0, keepdims=True)
        ggains_ref[5:6, :] += jnp.sum(back, 0, keepdims=True)
        dx = unit_back(back, hat, scaled, gain(4))
        dx_s[base : base + K, :] = jnp.zeros((K, width), jnp.float32)
        dx_s[base + K : base + tokens, :] = dx
        dy_s[base : base + K, :] = jnp.zeros((K, width), low)
        dy_s[base + K : base + tokens, :] = dx.astype(low)

    acc_s[...] = jnp.zeros_like(acc_s)

    @pl.loop(0, down_ref.shape[0] // tile)
    def _(t):
        at = pl.ds(pl.multiple_of(t * tile, tile), tile)
        up = pl.ds(pl.multiple_of(4 * width + t * tile, tile), tile)
        gdown[at, :] += dot_tn(a_s[:, at], dy_s[...])
        du = (dot_nt(dy_s[...], down_ref[at, :]) * gp_s[:, at].astype(jnp.float32)).astype(low)
        gcols[:, up] += dot_tn(h2_s[...], du)
        acc_s[...] += dot_nt(du, cols_ref[:, up])

    hat, scaled = unit_rows(x1_s[...])
    grads = acc_s[...]
    ggains_ref[2:3, :] += jnp.sum(grads * hat, 0, keepdims=True)
    ggains_ref[3:4, :] += jnp.sum(grads, 0, keepdims=True)
    dx_s[...] += unit_back(grads, hat, scaled, gain(2))
    dy_s[...] = dx_s[...].astype(low)
    gcols[:, 3 * width : 4 * width] += dot_tn(o_s[...], dy_s[...])
    o_s[...] = dot_nt(dy_s[...], cols_ref[:, 3 * width : 4 * width]).astype(low)

    @pl.loop(0, items * groups)
    def _(n):
        attend_back(n, groups, tokens, width, ee, scale, qkv_s, s_s, ds_s, p_s, inv_s, oo_s, o_s, dqkv_s)

    acc_s[...] = jnp.zeros_like(acc_s)

    @pl.loop(0, 3)
    def _(t):
        at = pl.ds(pl.multiple_of(t * width, width), width)
        gcols[:, at] += dot_tn(h1_s[...], dqkv_s[:, at])
        acc_s[...] += dot_nt(dqkv_s[:, at], cols_ref[:, at])

    hat, scaled = unit_rows(x_s[...])
    grads = acc_s[...]
    ggains_ref[0:1, :] += jnp.sum(grads * hat, 0, keepdims=True)
    ggains_ref[1:2, :] += jnp.sum(grads, 0, keepdims=True)
    dx_s[...] += unit_back(grads, hat, scaled, gain(0))
    for i in range(items):
        base = i * tokens
        dz_ref[i] = dx_s[base : base + K, :].astype(low)
        ggains_ref[6:7, :] += jnp.sum(dx_s[base + K : base + tokens, :], 0, keepdims=True)

    @pl.when(step == pl.num_programs(0) - 1)
    def _():
        gcols_out[...] = gcols[...].astype(low)
        gdown_out[...] = gdown[...].astype(low)
        ghead_out[...] = ghead[...].astype(low)


def decoder_call(scal, latent, keep, gsd, table, pixels, cols, down, head, gains, heads):
    batch, tokens, pixel_count = pixels.shape
    width = cols.shape[0]
    items = 2
    rows = items * tokens
    hide = tokens - K
    low = jnp.bfloat16
    full = pl.Buffered(1)

    def whole(array):
        return pl.BlockSpec(array.shape, lambda s: (0,) * array.ndim, pipeline_mode=full)

    def by_item(shape):
        return pl.BlockSpec((items,) + shape, lambda s: (s, 0, 0))

    outs = (
        jax.ShapeDtypeStruct((batch, K, width), low),
        jax.ShapeDtypeStruct(cols.shape, low),
        jax.ShapeDtypeStruct(down.shape, low),
        jax.ShapeDtypeStruct(head.shape, low),
        jax.ShapeDtypeStruct((8, width), jnp.float32),
        jax.ShapeDtypeStruct((1, 1), jnp.float32),
    )
    vmem = pltpu.VMEM
    f32 = jnp.float32
    return pl.pallas_call(
        functools.partial(decoder_kernel, items, heads),
        grid=(batch // items,),
        in_specs=[
            pl.BlockSpec(memory_space=pltpu.SMEM),
            by_item((K, width)),
            by_item((K, 1)),
            by_item((1, tokens)),
            pl.BlockSpec((table.shape[0], width), lambda s: (0, table.shape[1] // width - 1), pipeline_mode=full),
            by_item((tokens, pixel_count)),
            whole(cols),
            whole(down),
            whole(head),
            whole(gains),
        ],
        out_specs=(by_item((K, width)),) + tuple(whole(out) for out in outs[1:]),
        out_shape=outs,
        scratch_shapes=[
            vmem((rows, width), f32),
            vmem((rows, width), low),
            vmem((rows, 3 * width), low),
            vmem((items * width // 128, tokens, 4 * tokens), low),
            vmem((rows, width), low),
            vmem((rows, width), f32),
            vmem((rows, width), low),
            vmem((rows, down.shape[0]), low),
            vmem((rows, down.shape[0]), low),
            vmem((rows, width), f32),
            vmem((rows, width), low),
            vmem((rows, width), f32),
            vmem((rows, width), low),
            vmem((rows, width), f32),
            vmem((rows, 3 * width), low),
            vmem((items * width // 128, tokens, 128), f32),
            vmem((items * width // 128, tokens, 128), f32),
            vmem((4 * tokens, tokens), f32),
            vmem((tokens, 4 * tokens), low),
            vmem((table.shape[0], width), low),
            vmem((table.shape[0], width), low),
            vmem((items, hide, pixel_count), low),
            vmem(cols.shape, f32),
            vmem(down.shape, f32),
            vmem(head.shape, f32),
        ],
        compiler_params=pltpu.CompilerParams(
            dimension_semantics=("arbitrary",), vmem_limit_bytes=62 * 1024 * 1024
        ),
        cost_estimate=pl.CostEstimate(
            flops=70_000_000_000, bytes_accessed=40_000_000, transcendentals=20_000_000
        ),
    )(scal, latent, keep, gsd, table, pixels, cols, down, head, gains)


RUN = 256


def same_item():
    row = lax.broadcasted_iota(jnp.int32, (RUN, RUN), 0) // K
    column = lax.broadcasted_iota(jnp.int32, (RUN, RUN), 1) // K
    return row == column


def encoder_kernel(
    heads, pixels_ref, keep_ref, bands_ref, gsd_ref, table_ref, rows_ref, cols_ref, de_ref, gains_ref,
    z_ref, pix_ref, band_ref, x_ref, qkv_ref, p_ref, inv_ref, oo_ref, x1_ref, a_ref, gp_ref, x2_ref,
    h_s, s_s, o_s, high_s, low_s,
):
    low = jnp.bfloat16
    step = pl.program_id(0)
    width = x_ref.shape[1]
    ee = width // heads
    groups = width // LANES
    expo = ee ** (-0.5) * 1.4426950408889634

    def gain(i):
        return gains_ref[i : i + 1, :]

    @pl.when(step == 0)
    def _():
        split_table(table_ref, high_s, low_s)

        @pl.loop(0, pixels_ref.shape[0])
        def _(i):
            at = pl.ds(pl.multiple_of(i * K, K), K)
            hot = one_hot(keep_ref[i], pixels_ref.shape[1])
            pix_ref[at, :] = dot_nn(hot.astype(low), pixels_ref[i]).astype(low)
            band_ref[at, :] = jnp.sum(hot * bands_ref[i], -1, keepdims=True).astype(jnp.int32)
            x_ref[at, :] = look_up(hot, gsd_ref[i], high_s, low_s)

    @pl.when(step < 4)
    def _():
        pixel = pix_ref[...]
        x_ref[...] += dot_nn(jnp.where(band_ref[...] == step, pixel, jnp.zeros_like(pixel)), rows_ref[...])

    @pl.when(step == 4)
    def _():
        hat, _ = unit_rows(x_ref[...])
        h_s[...] = (hat * gain(0) + gain(1)).astype(low)

    @pl.when((step >= 4) & (step < 7))
    def _():
        at = pl.ds(pl.multiple_of((step - 4) * width, width), width)
        qkv_ref[:, at] = dot_nn(h_s[...], cols_ref[...]).astype(low)

    @pl.when(step == 7)
    def _():
        same = same_item()

        @pl.loop(0, x_ref.shape[0] // RUN * groups)
        def _(n):
            attend(n, groups, RUN, width, ee, expo, same, qkv_ref, s_s, p_ref, inv_ref, oo_ref, o_s)

        x1_ref[...] = x_ref[...] + dot_nn(o_s[...], cols_ref[...])
        hat, _ = unit_rows(x1_ref[...])
        h_s[...] = (hat * gain(2) + gain(3)).astype(low)
        x2_ref[...] = x1_ref[...]

    @pl.when(step >= 8)
    def _():
        @pl.loop(0, 2)
        def _(t):
            half = width // 2
            at = pl.ds(pl.multiple_of(t * half, half), half)
            u = dot_nn(h_s[...], cols_ref[:, at])
            cumul = 0.5 * (1.0 + lax.erf(u * 0.7071067811865476))
            a_ref[:, at] = (u * cumul).astype(low)
            gp_ref[:, at] = (cumul + u * jnp.exp(-0.5 * u * u) * 0.3989422804014327).astype(low)

        x2_ref[...] += dot_nn(a_ref[...], rows_ref[...])

    @pl.when(step == 11)
    def _():
        hat, _ = unit_rows(x2_ref[...])
        h_s[...] = (hat * gain(4) + gain(5)).astype(low)
        z_ref[...] = dot_nn(h_s[...], de_ref[...])


def encoder_call(pixels, keep, bands, gsd, table, rows, cols, de, gains, heads):
    width = cols.shape[0]
    tokens = keep.shape[0] * K
    low, f32 = jnp.bfloat16, jnp.float32
    runs = tokens // RUN * (width // LANES)
    wide = LANES // (width // heads) * RUN
    one = pl.Buffered(1)

    def whole(shape):
        return pl.BlockSpec(shape, lambda s: (0,) * len(shape), pipeline_mode=one)

    def row_block(s):
        return (jnp.where(s < 4, s + 4, jnp.where(s < 8, 0, s - 8)), 0)

    def column_block(s):
        return (0, jnp.where(s < 4, 0, s - 4))

    def hidden_block(s):
        return (0, jnp.where(s < 8, 0, s - 8))

    def hold(shape, dtype=f32):
        return jax.ShapeDtypeStruct(shape, dtype), whole(shape)

    ff = (tokens, 4 * width)
    outs = [
        hold((tokens, de.shape[1])),
        hold((tokens, pixels.shape[2]), low),
        hold((tokens, 1), jnp.int32),
        hold((tokens, width)),
        hold((tokens, 3 * width), low),
        hold((runs, RUN, wide), low),
        hold((runs, RUN, LANES)),
        hold((runs, RUN, LANES)),
        hold((tokens, width)),
        (jax.ShapeDtypeStruct(ff, low), pl.BlockSpec((tokens, width), hidden_block)),
        (jax.ShapeDtypeStruct(ff, low), pl.BlockSpec((tokens, width), hidden_block)),
        hold((tokens, width)),
    ]
    return pl.pallas_call(
        functools.partial(encoder_kernel, heads),
        grid=(12,),
        in_specs=[
            whole(pixels.shape),
            whole(keep.shape),
            whole(bands.shape),
            whole(gsd.shape),
            pl.BlockSpec((table.shape[0], width), lambda s: (0, 0), pipeline_mode=one),
            pl.BlockSpec((width, width), row_block),
            pl.BlockSpec((width, width), column_block),
            whole(de.shape),
            whole(gains.shape),
        ],
        out_specs=tuple(o[1] for o in outs),
        out_shape=tuple(o[0] for o in outs),
        scratch_shapes=[
            pltpu.VMEM((tokens, width), low),
            pltpu.VMEM((wide, RUN), f32),
            pltpu.VMEM((tokens, width), low),
            pltpu.VMEM((table.shape[0], width), low),
            pltpu.VMEM((table.shape[0], width), low),
        ],
        compiler_params=pltpu.CompilerParams(
            dimension_semantics=("arbitrary",), vmem_limit_bytes=60 * 1024 * 1024
        ),
        cost_estimate=pl.CostEstimate(
            flops=20_000_000_000, bytes_accessed=70_000_000, transcendentals=8_000_000
        ),
    )(pixels, keep, bands, gsd, table, rows, cols, de, gains)


def encoder_back_kernel(
    heads, dz_ref, pix_ref, band_ref, x_ref, qkv_ref, p_ref, inv_ref, oo_ref, x1_ref, a_ref, gp_ref, x2_ref,
    rows_ref, cols_ref, de_ref, gains_ref,
    grows_ref, gcols_ref, gde_ref, ggains_ref,
    h_s, dx_s, dy_s, acc_s, do_s, dqkv_s, s_s, ds_s,
):
    low, f32 = jnp.bfloat16, jnp.float32
    step = pl.program_id(0)
    width = x_ref.shape[1]
    ee = width // heads
    groups = width // LANES
    runs = x_ref.shape[0] // RUN

    def gain(i):
        return gains_ref[i : i + 1, :]

    def back(x, grads, at):
        hat, scaled = unit_rows(x)
        ggains_ref[at : at + 1, :] = jnp.sum(grads * hat, 0, keepdims=True)
        ggains_ref[at + 1 : at + 2, :] = jnp.sum(grads, 0, keepdims=True)
        return unit_back(grads, hat, scaled, gain(at))

    def normed(x, at):
        hat, _ = unit_rows(x)
        h_s[...] = (hat * gain(at) + gain(at + 1)).astype(low)

    @pl.when(step == 0)
    def _():
        ggains_ref[...] = jnp.zeros_like(ggains_ref)
        normed(x2_ref[...], 4)
        gde_ref[...] = dot_tn(h_s[...], dz_ref[...]).astype(low)
        dx_s[...] = back(x2_ref[...], dot_nt(dz_ref[...], de_ref[...]), 4)
        dy_s[...] = dx_s[...].astype(low)
        normed(x1_ref[...], 2)
        acc_s[...] = jnp.zeros_like(acc_s)

    @pl.when(step < 4)
    def _():
        grows_ref[...] = dot_tn(a_ref[...], dy_s[...]).astype(low)
        du = (dot_nt(dy_s[...], rows_ref[...]) * gp_ref[...].astype(f32)).astype(low)
        do_s[...] = du
        gcols_ref[...] = dot_tn(h_s[...], du).astype(low)
        acc_s[...] += dot_nt(do_s[...], cols_ref[...])

    @pl.when(step == 4)
    def _():
        dx_s[...] += back(x1_ref[...], acc_s[...], 2)
        dy_s[...] = dx_s[...].astype(low)
        for run in range(runs):
            for g in range(groups):
                h_s[run * RUN : (run + 1) * RUN, g * LANES : (g + 1) * LANES] = oo_ref[
                    run * groups + g
                ].astype(low)
        gcols_ref[...] = dot_tn(h_s[...], dy_s[...]).astype(low)
        do_s[...] = dot_nt(dy_s[...], cols_ref[...]).astype(low)

        @pl.loop(0, runs * groups)
        def _(n):
            attend_back(
                n, groups, RUN, width, ee, ee ** (-0.5), qkv_ref, s_s, ds_s, p_ref, inv_ref, oo_ref, do_s,
                dqkv_s,
            )

        normed(x_ref[...], 0)
        acc_s[...] = jnp.zeros_like(acc_s)

    @pl.when((step >= 5) & (step < 8))
    def _():
        at = pl.ds(pl.multiple_of((step - 5) * width, width), width)
        gcols_ref[...] = dot_tn(h_s[...], dqkv_s[:, at]).astype(low)
        acc_s[...] += dot_nt(dqkv_s[:, at], cols_ref[...])

    @pl.when(step == 8)
    def _():
        dx_s[...] += back(x_ref[...], acc_s[...], 0)
        dy_s[...] = dx_s[...].astype(low)

    @pl.when(step >= 8)
    def _():
        pixel = pix_ref[...]
        h_s[...] = jnp.where(band_ref[...] == step - 8, pixel, jnp.zeros_like(pixel))
        grows_ref[...] = dot_tn(h_s[...], dy_s[...]).astype(low)


def encoder_back_call(dz, pixel, band, saved, rows, cols, de, gains, heads):
    x, qkv, p, inv, oo, x1, a, gp, x2 = saved
    tokens, width = x.shape
    low, f32 = jnp.bfloat16, jnp.float32
    wide = p.shape[2]
    one = pl.Buffered(1)

    def whole(array):
        return pl.BlockSpec(array.shape, lambda s: (0,) * len(array.shape), pipeline_mode=one)

    def row_block(s):
        return (jnp.minimum(s, 3), 0)

    def column_block(s):
        return (0, jnp.where(s < 4, s + 4, jnp.where(s == 4, 3, jnp.minimum(s - 5, 2))))

    def hidden_block(s):
        return (0, jnp.minimum(s, 3))

    def grow_block(s):
        return (jnp.where(s < 4, s, jnp.where(s < 8, 3, s - 4)), 0)

    hidden = pl.BlockSpec((tokens, width), hidden_block)
    square = (width, width)
    outs = (
        jax.ShapeDtypeStruct(rows.shape, low),
        jax.ShapeDtypeStruct(cols.shape, low),
        jax.ShapeDtypeStruct(de.shape, low),
        jax.ShapeDtypeStruct((8, width), f32),
    )
    vmem = pltpu.VMEM
    return pl.pallas_call(
        functools.partial(encoder_back_kernel, heads),
        grid=(12,),
        in_specs=[
            whole(dz), whole(pixel), whole(band), whole(x), whole(qkv), whole(p), whole(inv), whole(oo),
            whole(x1), hidden, hidden, whole(x2),
            pl.BlockSpec(square, row_block), pl.BlockSpec(square, column_block),
            whole(de), whole(gains),
        ],
        out_specs=(
            pl.BlockSpec(square, grow_block),
            pl.BlockSpec(square, column_block),
            whole(outs[2]),
            whole(outs[3]),
        ),
        out_shape=outs,
        scratch_shapes=[
            vmem((tokens, width), low),
            vmem((tokens, width), f32),
            vmem((tokens, width), low),
            vmem((tokens, width), f32),
            vmem((tokens, width), low),
            vmem((tokens, 3 * width), low),
            vmem((wide, RUN), f32),
            vmem((RUN, wide), low),
        ],
        compiler_params=pltpu.CompilerParams(
            dimension_semantics=("arbitrary",), vmem_limit_bytes=60 * 1024 * 1024
        ),
        cost_estimate=pl.CostEstimate(
            flops=40_000_000_000, bytes_accessed=110_000_000, transcendentals=1_000_000
        ),
    )(dz, pixel, band, x, qkv, p, inv, oo, x1, a, gp, x2, rows, cols, de, gains)


MESH_ID = pl.DeviceIdType.MESH


def place():
    g = lax.axis_index("grp")
    d = lax.axis_index("dp")
    z, c = d // 2, d % 2
    xn = g + 1 - 2 * (g % 2)
    yn = (g + 2) % 4
    return g, z, c, xn, yn


def pieces(shape, parts):
    rows, columns = shape
    if rows // parts >= 32:
        n = rows // parts
        cut = [(slice(i * n, (i + 1) * n), slice(0, columns)) for i in range(parts)]
    else:
        n = columns // parts
        cut = [(slice(0, rows), slice(i * n, (i + 1) * n)) for i in range(parts)]
    return cut


def halves(cut):
    rows, columns = cut
    mid = (columns.start + columns.stop) // 2
    return (rows, slice(columns.start, mid)), (rows, slice(mid, columns.stop))


def greet(peers):
    barrier = pltpu.get_barrier_semaphore()
    for peer in peers:
        pl.semaphore_signal(barrier, inc=1, device_id=peer, device_id_type=MESH_ID)
    pl.semaphore_wait(barrier, len(peers))


def gather_kernel(count, chunks, ahead, *refs):
    ins, items_ref = refs[:count], refs[count]
    outs, items_out = refs[count + 1 : 2 * count + 1], refs[2 * count + 1]
    (zs, zr, xs, xr, ys, yr, fs, fr, gs, gr, cs, os, cr, ls, it, its, itr) = refs[2 * count + 2 :]
    g, z, c, xn, yn = place()
    dg = (xn + 2) % 4
    here = 2 * z + c
    sib = (g, 2 * z + 1 - c)
    zpeer = [(g, 2 * ((z + j) % 4) + c) for j in (1, 2, 3)]
    zfrom = [(z + 4 - j) % 4 for j in (1, 2, 3)]
    greet([sib, (xn, here), (yn, here)] + zpeer)

    def send(src, dst, send_sem, recv_sem, peer):
        return pltpu.make_async_remote_copy(
            src_ref=src, dst_ref=dst, send_sem=send_sem, recv_sem=recv_sem,
            device_id=peer, device_id_type=MESH_ID,
        )

    def block(array, z_at, q, cut, core=None):
        return outs[array].at[z_at, c if core is None else core, q, cut[0], cut[1]]

    work = []
    for array in range(count):
        for cut in pieces(ins[array].shape[1:], chunks[array]):
            work.append((array, cut))
    steps = len(work)
    sent = []

    def go(copy):
        copy.start()
        sent.append(copy)

    def items_copy(i, peer):
        return send(it.at[2 * i], it.at[2 * i + 1], its.at[i], itr.at[i], peer)

    def zcopy(k, j):
        array, cut = work[k]
        return send(
            ins[array].at[g, cut[0], cut[1]], block(array, z, g, cut), zs.at[k, j], zr.at[k, j], zpeer[j]
        )

    def relay(k, j, q, cut, ssem, rsem, peer):
        at = block(work[k][0], zfrom[j], q, cut)
        return send(at, at, ssem, rsem, peer)

    it[0] = items_ref[...]
    go(items_copy(0, (xn, here)))
    local = []
    for array in range(count):
        copy = pltpu.make_async_copy(ins[array], outs[array].at[z, c], ls.at[array])
        copy.start()
        local.append(copy)
    for k in range(min(ahead, steps)):
        for j in range(3):
            go(zcopy(k, j))
    for array in range(count):
        go(send(ins[array], outs[array].at[z, c], os.at[array], cr.at[array], sib))

    for t in range(steps + 2):
        if t < steps:
            array, cut = work[t]
            for j in range(3):
                zcopy(t, j).wait_recv()
                go(relay(t, j, g, cut, xs.at[t, j], xr.at[t, j], (xn, here)))
                go(relay(t, j, g, cut, ys.at[t, j], yr.at[t, j], (yn, here)))
                go(relay(t, j, g, cut, cs.at[t, j, 0], cr.at[array], sib))
            if t + ahead < steps:
                for j in range(3):
                    go(zcopy(t + ahead, j))
        if t == 0:
            items_copy(0, (xn, here)).wait_recv()
            it[2] = it[0] + it[1]
            go(items_copy(1, (yn, here)))
        if t == 1:
            items_copy(1, (yn, here)).wait_recv()
            items_out[...] = it[2] + it[3]
        if 1 <= t <= steps:
            k = t - 1
            array, cut = work[k]
            left, right = halves(cut)
            for j in range(3):
                relay(k, j, xn, cut, xs.at[k, j], xr.at[k, j], (xn, here)).wait_recv()
                go(relay(k, j, xn, left, fs.at[k, j], fr.at[k, j], (yn, here)))
                go(relay(k, j, xn, cut, cs.at[k, j, 1], cr.at[array], sib))
                relay(k, j, yn, cut, ys.at[k, j], yr.at[k, j], (yn, here)).wait_recv()
                go(relay(k, j, yn, right, gs.at[k, j], gr.at[k, j], (xn, here)))
                go(relay(k, j, yn, cut, cs.at[k, j, 2], cr.at[array], sib))
        if 2 <= t:
            k = t - 2
            array, cut = work[k]
            left, right = halves(cut)
            for j in range(3):
                relay(k, j, dg, left, fs.at[k, j], fr.at[k, j], (yn, here)).wait_recv()
                relay(k, j, dg, right, gs.at[k, j], gr.at[k, j], (xn, here)).wait_recv()
                go(relay(k, j, dg, cut, cs.at[k, j, 3], cr.at[array], sib))
    for copy in sent:
        copy.wait_send()
    for array in range(count):
        whole = outs[array].at[:, 1 - c]
        send(whole, whole, os.at[array], cr.at[array], sib).wait_recv()
        local[array].wait()


def gather_call(shards, items, chunks, ahead=2, collective_id=0):
    count = len(shards)
    steps = sum(chunks)
    views = [s.reshape(4, s.shape[0] // 4, s.shape[1]) for s in shards]
    dma = pltpu.SemaphoreType.DMA
    hbm = pl.BlockSpec(memory_space=pl.ANY)
    vm = pl.BlockSpec(memory_space=pltpu.VMEM)
    *outs, total = pl.pallas_call(
        functools.partial(gather_kernel, count, chunks, ahead),
        out_shape=tuple(jax.ShapeDtypeStruct((4, 2) + v.shape, v.dtype) for v in views)
        + (jax.ShapeDtypeStruct((8, 128), jnp.float32),),
        in_specs=[hbm] * count + [vm],
        out_specs=tuple([hbm] * count + [vm]),
        scratch_shapes=[dma((steps, 3))] * 10
        + [dma((steps, 3, 4)), dma((count,)), dma((count,)), dma((count,))]
        + [pltpu.VMEM((4, 8, 128), jnp.float32), dma((2,)), dma((2,))],
        compiler_params=pltpu.CompilerParams(collective_id=collective_id, has_side_effects=True),
    )(*views, jnp.broadcast_to(items, (8, 128)))
    return [o.reshape(-1, o.shape[-1]) for o in outs], total[0, 0]


def reduce_kernel(n_in, n_out, kinds, work, ahead, offsets, z_offsets, newest_last, *refs):
    ins = refs[:n_in]
    small_ref = refs[n_in]
    outs = refs[n_in + 1 : n_in + 1 + n_out]
    small_out, ss_out = refs[n_in + 1 + n_out : n_in + 3 + n_out]
    rest = refs[n_in + 3 + n_out :]
    bufs = [rest[9 * i : 9 * i + 9] for i in range(len(kinds))]
    (sm, ss, ssx, cs, cr, os, x1s, x1r, x2s, x2r, z_s, z_r, ags, agr, ls, sms, smr, sss, ssr) = rest[
        9 * len(kinds) :
    ]
    g, z, c, xn, yn = place()
    dg = (xn + 2) % 4
    here = 2 * z + c
    sib = (g, 2 * z + 1 - c)
    right, up = (xn, here), (yn, here)
    zto = [(z + j) % 4 for j in (1, 2, 3)]
    zpeer = [(g, 2 * t + c) for t in zto]
    greet([sib, right, up] + zpeer)
    steps = len(work)
    sent = []
    f32 = jnp.float32
    slots = ahead + 1

    def send(src, dst, send_sem, recv_sem, peer):
        return pltpu.make_async_remote_copy(
            src_ref=src, dst_ref=dst, send_sem=send_sem, recv_sem=recv_sem,
            device_id=peer, device_id_type=MESH_ID,
        )

    def go(copies):
        for copy in copies:
            copy.start()
            sent.append(copy)

    def got(copies):
        for copy in copies:
            copy.wait_recv()

    def buffers(k):
        kind, at = work[k][:2]
        return bufs[kind], at, kinds[kind][1] // 2

    def c_copies(k):
        (s, *_), at, _ = buffers(k)
        return [
            send(
                ins[array].at[:, 1 - c, :, cut[0], cut[1]], s.at[at, pl.ds(z0, nz)],
                cs.at[k, i], cr.at[k, i], sib,
            )
            for i, (array, z0, nz, cut) in enumerate(work[k][3])
        ]

    def own_copies(k):
        (_, own, *_), at, _ = buffers(k)
        return [
            pltpu.make_async_copy(
                ins[array].at[:, c, :, cut[0], cut[1]], own.at[at % slots, pl.ds(z0, nz)], os.at[k, i]
            )
            for i, (array, z0, nz, cut) in enumerate(work[k][3])
        ]

    def begin(k):
        go(c_copies(k))
        for copy in own_copies(k):
            copy.start()

    def planes(k):
        if work[k][2]:
            return pl.ds(z, 1), pl.ds(0, 1), 1
        return pl.ds(0, 4), pl.ds(0, 4), 4

    def x1_copies(k):
        (s, _, xa, yb, *_), at, half = buffers(k)
        src, dst, _ = planes(k)
        left, right_half = pl.ds(0, half), pl.ds(half, half)
        return [
            send(s.at[at, src, xn, :, left], xa.at[at, 0, dst], x1s.at[k, 0], x1r.at[k, 0], right),
            send(s.at[at, src, dg, :, left], xa.at[at, 1, dst], x1s.at[k, 1], x1r.at[k, 1], right),
            send(s.at[at, src, yn, :, right_half], yb.at[at, 0, dst], x1s.at[k, 2], x1r.at[k, 2], up),
            send(s.at[at, src, dg, :, right_half], yb.at[at, 1, dst], x1s.at[k, 3], x1r.at[k, 3], up),
        ]

    def x2_copies(k):
        (s, _, _, _, xb, ya, *_), at, half = buffers(k)
        src, dst, _ = planes(k)
        left, right_half = pl.ds(0, half), pl.ds(half, half)
        return [
            send(s.at[at, src, yn, :, left], ya.at[at, dst], x2s.at[k, 0], x2r.at[k, 0], up),
            send(s.at[at, src, xn, :, right_half], xb.at[at, dst], x2s.at[k, 1], x2r.at[k, 1], right),
        ]

    def z_copies(k):
        (s, _, _, _, _, _, zb, *_), at, _ = buffers(k)
        if work[k][2]:
            zt = bufs[work[k][0]][8]
            return [
                send(s.at[at, zto[j]], zt.at[work[k][2] - 1, j], z_s.at[k, j], z_r.at[k, j], zpeer[j])
                for j in range(3)
            ]
        return [
            send(s.at[at, zto[j], g], zb.at[at, j], z_s.at[k, j], z_r.at[k, j], zpeer[j])
            for j in range(3)
        ]

    def out_at(k, q, part=None):
        index, cut = work[k][4:]
        if part is not None:
            cut = halves(cut)[part]
        return outs[index].at[q, cut[0], cut[1]]

    def ag_copies(k):
        (*_, fin, _), at, _ = buffers(k)
        return [
            send(fin.at[at], out_at(k, g), ags.at[k, 0], agr.at[k, 0], right),
            send(fin.at[at], out_at(k, g), ags.at[k, 1], agr.at[k, 1], up),
        ]

    def keep_copy(k):
        (*_, fin, _), at, _ = buffers(k)
        return pltpu.make_async_copy(fin.at[at], out_at(k, g), ls.at[k])

    def fwd_copies(k, of_x, of_y):
        return [
            send(out_at(k, of_x, 0), out_at(k, of_x, 0), ags.at[k, 2], agr.at[k, 2], up),
            send(out_at(k, of_y, 1), out_at(k, of_y, 1), ags.at[k, 3], agr.at[k, 3], right),
        ]

    def add_half(k, q, left, other):
        (s, *_), at, half = buffers(k)
        part = pl.ds(0 if left else half, half)
        if work[k][2]:
            s[at, z, q, :, part] = (s[at, z, q, :, part].astype(f32) + other[0].astype(f32)).astype(s.dtype)
            return

        @pl.loop(0, 4)
        def _(i):
            s[at, i, q, :, part] = (s[at, i, q, :, part].astype(f32) + other[i].astype(f32)).astype(s.dtype)

    def pair(k):
        (s, own, *_), at, _ = buffers(k)
        got(c_copies(k))
        for copy in own_copies(k):
            copy.wait()

        @pl.loop(0, 4)
        def _(i):
            for q in range(4):
                s[at, i, q] = (s[at, i, q].astype(f32) + own[at % slots, i, q].astype(f32)).astype(s.dtype)

    def first_half(k):
        (_, _, xa, yb, *_), at, _ = buffers(k)
        got(x1_copies(k))
        add_half(k, yn, True, xa.at[at, 1])
        add_half(k, xn, False, yb.at[at, 1])
        go(x2_copies(k))
        add_half(k, g, True, xa.at[at, 0])
        add_half(k, g, False, yb.at[at, 0])

    def second_half(k):
        (_, _, _, _, xb, ya, *_), at, _ = buffers(k)
        got(x2_copies(k))
        add_half(k, g, True, ya.at[at])
        add_half(k, g, False, xb.at[at])

    def finish(k, total):
        (*_, fin, _), at, _ = buffers(k)
        fin[at] = total.astype(fin.dtype)
        go(ag_copies(k))
        keep_copy(k).start()
        square = fin[at].astype(f32)
        square = square * square
        for i in range(square.shape[1] // ss.shape[1]):
            ss[...] += jnp.sum(
                square[:, i * ss.shape[1] : (i + 1) * ss.shape[1]], 0, keepdims=True
            )

    def collect(k):
        got(ag_copies(k))
        go(fwd_copies(k, xn, yn))

    def close(k):
        got(fwd_copies(k, dg, dg))

    def p1(k):
        pair(k)
        go(x1_copies(k))

    def p3(k):
        second_half(k)
        go(z_copies(k))

    def p4(k):
        (s, _, _, _, _, _, zb, *_), at, _ = buffers(k)
        got(z_copies(k))
        total = s[at, z, g].astype(f32)
        for j in range(3):
            total = total + zb[at, j].astype(f32)
        finish(k, total)

    def z1(k):
        pair(k)
        go(z_copies(k))

    def z2(k):
        (s, *_), at, _ = buffers(k)
        zt = bufs[work[k][0]][8]
        i = work[k][2] - 1
        got(z_copies(k))
        for q in range(4):
            total = s[at, z, q].astype(f32)
            for j in range(3):
                total = total + zt[i, j, q].astype(f32)
            s[at, z, q] = total.astype(s.dtype)
        go(x1_copies(k))

    def z4(k):
        (s, *_), at, _ = buffers(k)
        second_half(k)
        finish(k, s[at, z, g].astype(f32))

    plane_stages = [p1, first_half, p3, p4, collect, close]
    z_stages = [z1, z2, first_half, z4, collect, close]

    def share_rounds(value, sem_s, sem_r, store):
        def copy(i, slot, peer):
            return send(value.at[slot], value.at[4 + i], sem_s.at[i], sem_r.at[i], peer)

        def round_pair(i, peer, following):
            got([copy(i, i, peer)])
            value[i + 1] = value[i] + value[4 + i]
            go(following())

        def last():
            return [copy(3 + j, 3, zpeer[j]) for j in range(3)]

        def end():
            got(last())
            total = None
            for at in range(4):
                term = jnp.where(z == at, value[3], jnp.zeros_like(value[3]))
                for j in range(3):
                    term = term + jnp.where((z + 3 - j) % 4 == at, value[7 + j], jnp.zeros_like(value[3]))
                total = term if total is None else total + term
            store[...] = total

        return [
            lambda: go([copy(0, 0, sib)]),
            lambda: round_pair(0, sib, lambda: [copy(1, 1, right)]),
            lambda: round_pair(1, right, lambda: [copy(2, 2, up)]),
            lambda: round_pair(2, up, last),
            end,
        ]

    sm[0] = small_ref[...]
    ss[...] = jnp.zeros_like(ss)
    small_rounds = share_rounds(sm, sms, smr, small_out)
    small_rounds[0]()
    for k in range(min(ahead, steps)):
        begin(k)
    square_rounds = share_rounds(ssx, sss, ssr, ss_out)
    def at_time(k, i):
        return k + (z_offsets if work[k][2] else offsets)[i]

    last = max(at_time(k, 5) for k in range(steps))
    squared = max(at_time(k, 3) for k in range(steps))
    for t in range(last + 1):
        for k in range(steps) if newest_last else reversed(range(steps)):
            for i in range(6):
                if at_time(k, i) == t:
                    (z_stages if work[k][2] else plane_stages)[i](k)
                    if i == 0 and k + ahead < steps:
                        begin(k + ahead)
        if t < 4:
            small_rounds[t + 1]()
        if t == squared:
            ssx[0] = jnp.broadcast_to(jnp.sum(ss[...], keepdims=True).reshape(1, 1), ssx.shape[1:])
            square_rounds[0]()
        if squared < t < last and t - squared < 3:
            square_rounds[t - squared]()
        if t == last:
            for following in square_rounds[min(3, last - squared) :]:
                following()
    for copy in sent:
        copy.wait_send()
    for k in range(steps):
        keep_copy(k).wait()


def reduce_call(grads, small, kinds, work, out_shapes, ahead, offsets, z_offsets, newest_last, collective_id):
    steps = len(work)
    low, f32 = jnp.bfloat16, jnp.float32
    dma = pltpu.SemaphoreType.DMA
    hbm = pl.BlockSpec(memory_space=pl.ANY)
    vm = pl.BlockSpec(memory_space=pltpu.VMEM)
    vmem = pltpu.VMEM
    scratch = []
    for kind, (rows, columns, count) in enumerate(kinds):
        half = columns // 2
        z_first = max([1] + [w[2] for w in work if w[0] == kind])
        scratch += [
            vmem((count, 4, 4, rows, columns), low),
            vmem((min(count, ahead + 1), 4, 4, rows, columns), low),
            vmem((count, 2, 4, rows, half), low),
            vmem((count, 2, 4, rows, half), low),
            vmem((count, 4, rows, half), low),
            vmem((count, 4, rows, half), low),
            vmem((count, 3, rows, columns), low),
            vmem((count, rows, columns), low),
            vmem((z_first, 3, 4, rows, columns), low),
        ]
    return pl.pallas_call(
        functools.partial(reduce_kernel, len(grads), len(out_shapes), kinds, work, ahead, offsets, z_offsets, newest_last),
        out_shape=tuple(jax.ShapeDtypeStruct(shape, low) for shape in out_shapes)
        + (jax.ShapeDtypeStruct(small.shape, f32), jax.ShapeDtypeStruct((8, 128), f32)),
        in_specs=[hbm] * len(grads) + [vm],
        out_specs=tuple([hbm] * len(out_shapes) + [vm, vm]),
        scratch_shapes=scratch
        + [
            vmem((10,) + small.shape, f32),
            vmem((1, 512), f32),
            vmem((10, 8, 128), f32),
            dma((steps, 3)), dma((steps, 3)), dma((steps, 3)),
            dma((steps, 4)), dma((steps, 4)),
            dma((steps, 2)), dma((steps, 2)),
            dma((steps, 3)), dma((steps, 3)),
            dma((steps, 4)), dma((steps, 4)),
            dma((steps,)), dma((6,)), dma((6,)), dma((6,)), dma((6,)),
        ],
        compiler_params=pltpu.CompilerParams(
            collective_id=collective_id, has_side_effects=True, vmem_limit_bytes=62 * 1024 * 1024
        ),
    )(*grads, small)


def reduce_gradients(
    erows, ecols, dcols, drows, small, z_first=3, ahead=2, offsets=(0, 2, 4, 6, 8, 9),
    z_offsets=(0, 4, 6, 8, 10, 11), newest_last=False, collective_id=1,
):
    grads, shapes = [], []

    def add(array, z_count):
        grads.append(array.reshape(z_count, 2, 4, array.shape[0] // (8 * z_count), array.shape[1]))
        return len(grads) - 1

    chunks = [[], [], []]
    wide = 1024
    tall = erows.shape[0] // 32
    index = add(erows, 4)
    shapes.append((4, tall, wide))
    for k in range(tall // 32):
        cut = (slice(k * 32, (k + 1) * 32), slice(0, wide))
        chunks[0].append((0, ((index, 0, 4, cut),), 0, cut))
    index = add(ecols, 4)
    shapes.append((4, 32, ecols.shape[1]))
    for k in range(ecols.shape[1] // wide):
        cut = (slice(0, 32), slice(k * wide, (k + 1) * wide))
        chunks[0].append((0, ((index, 0, 4, cut),), 1, cut))
    index = add(dcols, 4)
    shapes.append((4, 16, dcols.shape[1]))
    for k in range(dcols.shape[1] // 2048):
        cut = (slice(0, 16), slice(k * 2048, (k + 1) * 2048))
        chunks[1].append((1, ((index, 0, 4, cut),), 2, cut))
    rows = sum(part.shape[0] for part in drows)
    z_rows = rows // 4
    parts = []
    at = 0
    for part in drows:
        count = part.shape[0] // z_rows
        parts.append((add(part, count), at, count))
        at += count
    tall = rows // 32
    shapes.append((4, tall, 512))
    for k in range(tall // 64):
        cut = (slice(k * 64, (k + 1) * 64), slice(0, 512))
        chunks[2].append((2, tuple((i, z0, nz, cut) for i, z0, nz in parts), 3, cut))
    numbered = [[(c[0], i) + c[1:] for i, c in enumerate(group)] for group in chunks]
    order = numbered[1] + numbered[2] + numbered[0]
    total = len(order)
    marks = {}
    if z_first:
        spots = [i for i in range(total) if order[i][0] == 0]
        every = max(1, len(spots) // z_first)
        for n in range(z_first):
            marks[spots[n * every]] = n + 1
    work = tuple(c[:2] + (marks.get(i, 0),) + c[2:] for i, c in enumerate(order))
    kinds = ((32, wide, len(chunks[0])), (16, 2048, len(chunks[1])), (64, 512, len(chunks[2])))
    out = reduce_call(tuple(grads), small, kinds, work, tuple(shapes), ahead, offsets, z_offsets, newest_last, collective_id)
    erows, ecols, dcols, drows = [o.reshape(-1, o.shape[-1]) for o in out[:4]]
    return ecols, erows, dcols, drows, out[4], out[5]


def adam_step(master, moment, square, grad, factor, fix_one, fix_two, decay, rate):
    clipped = grad * factor
    moment_new = beta_first * moment + (1.0 - beta_first) * clipped
    square_new = beta_second * square + (1.0 - beta_second) * clipped * clipped
    direction = moment_new / fix_one / (jnp.sqrt(square_new / fix_two) + adam_eps) + decay * master
    return (clipped, square_new, master - rate * direction)


def body(
    pixels,
    keep_index,
    band_group,
    gsd_index,
    gsd_table,
    group_items,
    step_count,
    enc_cols,
    enc_rows,
    dec_cols,
    dec_rows,
    enc_gains,
    dec_gains,
    moment_ecols,
    moment_erows,
    moment_dcols,
    moment_drows,
    moment_egains,
    moment_dgains,
    square_ecols,
    square_erows,
    square_dcols,
    square_drows,
    square_egains,
    square_dgains,
):
    n_grp = lax.axis_size("grp")
    grp_at = lax.axis_index("grp")

    def gather_rows(master):
        rows = master.shape[0]
        if rows % (16 * n_grp):
            return lax.all_gather(to_low(master), "dp", axis=0, tiled=True)
        part = rows // n_grp
        mine = lax.dynamic_slice_in_dim(master, grp_at * part, part, 0)
        return lax.all_gather(to_low(mine), ("dp", "grp"), axis=0, tiled=True)

    direct = (n_grp, lax.axis_size("dp")) == (4, 8)
    own_count = jnp.sum(group_items.astype(jnp.float32))
    if direct:
        (whole_rows, whole_cols), total_count = gather_call(
            [to_low(enc_rows), to_low(enc_cols)], own_count, (4, 4), 2, 0
        )
    else:
        total_count = lax.psum(own_count, "grp")
        whole_rows, whole_cols = gather_rows(enc_rows), gather_rows(enc_cols)
    masked = total_count * (L - K)
    copies = (whole_cols, whole_rows, gather_rows(dec_cols), gather_rows(dec_rows))
    dec_copy = copies[2]
    dec_down = copies[3][:DFF]
    dec_embed = copies[3][DFF : DFF + D]
    head_rows = copies[3][DFF + D :]
    keep_rows = keep_index[0]
    batch = keep_rows.shape[0]
    keep_column = keep_rows[..., None]
    band_row = band_group[0][:, None, :].astype(jnp.float32)
    gsd_row = gsd_index[0][:, None, :].astype(jnp.float32)
    latent, kept_pixels, kept_bands, *saved = encoder_call(
        pixels[0],
        keep_column,
        band_row,
        gsd_row,
        gsd_table[0],
        whole_rows,
        whole_cols,
        dec_embed,
        enc_gains,
        HEADS,
    )
    latent = latent.reshape(batch, K, -1)
    first_item = lax.axis_index("dp") * batch
    valid = (first_item + jnp.arange(batch, dtype=jnp.int32) < group_items[0]).astype(jnp.float32)
    scal = jnp.stack([valid / PIX, valid * (2.0 / PIX) / masked])
    grad_latent, grad_dcols, grad_ddown, grad_head, dec_sums, loss_local = decoder_call(
        scal,
        latent,
        keep_column,
        gsd_row,
        gsd_table[0],
        pixels[0],
        dec_copy,
        dec_down,
        head_rows,
        dec_gains,
        DHEADS,
    )
    loss_local = loss_local[0, 0]
    grad_erows, grad_ecols, grad_dembed, enc_sums = encoder_back_call(
        grad_latent.reshape(batch * K, -1),
        kept_pixels,
        kept_bands,
        saved,
        whole_rows,
        whole_cols,
        dec_embed,
        enc_gains,
        HEADS,
    )
    grad_egains = enc_sums[:6]

    def reduce_rows(pieces, axis):
        whole = jnp.concatenate([to_low(piece) for piece in pieces], axis)
        return lax.psum_scatter(whole, "dp", scatter_dimension=0, tiled=True)

    grad_dgains = dec_sums[:7]
    drows = (grad_ddown, grad_dembed, grad_head)
    if direct:
        flat = jnp.concatenate([grad_egains.reshape(-1), grad_dgains.reshape(-1), loss_local[None]])
        count_e, count_d = grad_egains.size, grad_dgains.size
        small = jnp.pad(flat, (0, 16 * D - flat.shape[0])).reshape(16, D)
        *shards, small, squares = reduce_gradients(grad_erows, grad_ecols, grad_dcols, drows, small)
        flat = small.reshape(-1)
        enc_sum = flat[:count_e].reshape(grad_egains.shape)
        dec_sum = flat[count_e : count_e + count_d].reshape(grad_dgains.shape)
        loss_sum = flat[count_e + count_d]
        shard_squares = squares[0, 0]
        shards = tuple(piece.astype(jnp.float32) for piece in shards)
    else:
        enc_sum, dec_sum, loss_sum = lax.psum((grad_egains, grad_dgains, loss_local), ("grp", "dp"))
        shards = tuple(
            lax.psum(reduce_rows(pieces, 0), "grp").astype(jnp.float32)
            for pieces in ((grad_ecols,), (grad_erows,), (grad_dcols,), drows)
        )
        shard_squares = lax.psum(sum((jnp.sum(piece * piece) for piece in shards)), "dp")
    loss = loss_sum / masked
    grad_norm = jnp.sqrt(shard_squares + jnp.sum(enc_sum * enc_sum) + jnp.sum(dec_sum * dec_sum))
    factor = clip_level / jnp.maximum(grad_norm, clip_level)
    count_steps = step_count[0].astype(jnp.float32)
    fix_one = 1.0 - beta_first**count_steps
    fix_two = 1.0 - beta_second**count_steps
    clipped_ecols, squares_ecols, updated_ecols = adam_step(
        enc_cols,
        moment_ecols,
        square_ecols,
        shards[0],
        factor,
        fix_one,
        fix_two,
        weight_decay,
        learn_rate,
    )
    clipped_erows, squares_erows, updated_erows = adam_step(
        enc_rows,
        moment_erows,
        square_erows,
        shards[1],
        factor,
        fix_one,
        fix_two,
        weight_decay,
        learn_rate,
    )
    clipped_dcols, squares_dcols, updated_dcols = adam_step(
        dec_cols,
        moment_dcols,
        square_dcols,
        shards[2],
        factor,
        fix_one,
        fix_two,
        weight_decay,
        learn_rate,
    )
    clipped_drows, squares_drows, updated_drows = adam_step(
        dec_rows,
        moment_drows,
        square_drows,
        shards[3],
        factor,
        fix_one,
        fix_two,
        weight_decay,
        learn_rate,
    )
    clipped_egains, squares_egains, updated_egains = adam_step(
        enc_gains, moment_egains, square_egains, enc_sum, factor, fix_one, fix_two, 0.0, gain_rate
    )
    clipped_dgains, squares_dgains, updated_dgains = adam_step(
        dec_gains, moment_dgains, square_dgains, dec_sum, factor, fix_one, fix_two, 0.0, gain_rate
    )
    return (
        clipped_ecols,
        squares_ecols,
        updated_ecols,
        clipped_erows,
        squares_erows,
        updated_erows,
        clipped_dcols,
        squares_dcols,
        updated_dcols,
        clipped_drows,
        squares_drows,
        updated_drows,
        clipped_egains,
        squares_egains,
        updated_egains,
        clipped_dgains,
        squares_dgains,
        updated_dgains,
        loss,
        grad_norm,
    )


def solution(mesh):
    return jax.shard_map(
        body,
        mesh=mesh,
        in_specs=(
            P("grp", "dp", None, None),
            P("grp", "dp", None),
            P("grp", "dp", None),
            P("grp", "dp", None),
            P("grp", None, None),
            P("grp"),
            P(),
            P("dp", None),
            P("dp", None),
            P("dp", None),
            P("dp", None),
            P(),
            P(),
            P("dp", None),
            P("dp", None),
            P("dp", None),
            P("dp", None),
            P(),
            P(),
            P("dp", None),
            P("dp", None),
            P("dp", None),
            P("dp", None),
            P(),
            P(),
        ),
        out_specs=(
            P("dp", None),
            P("dp", None),
            P("dp", None),
            P("dp", None),
            P("dp", None),
            P("dp", None),
            P("dp", None),
            P("dp", None),
            P("dp", None),
            P("dp", None),
            P("dp", None),
            P("dp", None),
            P(),
            P(),
            P(),
            P(),
            P(),
            P(),
            P(),
            P(),
        ),
        check_vma=False,
    )
```

time: 870 us -> 750 us (0.86)
  Pallas kernels: 520 us -> 666 us
  matrix products: 130 us -> 0 us
  local copies, waits for them, and re-layouts: 82.8 us -> 22.1 us
  waiting for transfers between devices: 29.7 us -> 0.06 us
  blocking collectives: 26.1 us -> 0 us
  other arithmetic: 52.5 us -> 29.9 us
    dot_general x29 -> x0, matrix products: 130 us -> none  [the longest x10 41.2 us: project(): jnp.einsum('...n,nm->...m', inputs, matrix, preferred_element_type=jnp.fl...]
    pallas_call x0 -> x2, Pallas kernels: none -> 128 us  [the longest x1 75.4 us: encoder_back_call(): pl.pallas_call(functools.partial(encoder_back_kernel, heads), grid=(12,),...]
    pallas_call x1, Pallas kernels: 205 us -> 244 us  [reduce_call(): pl.pallas_call(functools.partial(reduce_kernel, len(grads), len(out_shape...]
    reduce_scatter x2 -> x0, waiting for transfers between devices: 29.6 us -> none  [reduce_rows(): return lax.psum_scatter(whole, 'dp', scatter_dimension=0, tiled=True)]
    psum x2 -> x0, blocking collectives: 26.1 us -> none  [the longest x1 15 us: body(): lax.psum(sum((jnp.sum(piece * piece) for piece in shards)), 'dp')]
    pallas_call x1, Pallas kernels: 161 us -> 138 us  [decoder_call(): pl.pallas_call(functools.partial(decoder_kernel, items, heads), grid=(bat...]
    reshape x6 -> x0, local copies, waits for them, and re-layouts: 18 us -> none  [the longest x1 4.09 us: block_backward(): grad_key.reshape(flat_shape)]
    unnamed x152 -> x63, local copies, waits for them, and re-layouts: 24.3 us -> 7.36 us
  transfers between devices with their start and end apart: 5 -> 2, of which waited for: 1 -> 0; matrix products, arithmetic and copies ran while one was open for 25% -> 2% of each run, Pallas kernels for 42% -> 28%
where the time goes in v2:
time: 750 us; the launch traced here: 740 us
  Pallas kernels  666 us (89%)
  other arithmetic  29.9 us (4%)
  local copies, waits for them, and re-layouts  22.1 us (3%)
  between operations  22 us (3%)
    pallas_call x1, Pallas kernels, reduce_call(): pl.pallas_call(functools.partial(reduce_kernel, len(grads), len(out_shape...  244 us
    pallas_call x1, Pallas kernels, gather_call(): pl.pallas_call(functools.partial(gather_kernel, count, chunks, ahead), ou...  156 us
    pallas_call x1, Pallas kernels, decoder_call(): pl.pallas_call(functools.partial(decoder_kernel, items, heads), grid=(bat...  138 us
    pallas_call x1, Pallas kernels, encoder_back_call(): pl.pallas_call(functools.partial(encoder_back_kernel, heads), grid=(12,),...  75.4 us
    pallas_call x1, Pallas kernels, encoder_call(): pl.pallas_call(functools.partial(encoder_kernel, heads), grid=(12,), in_s...  53.1 us
    sub x6, other arithmetic, adam_step(): return (clipped, square_new, master - rate * direction)  17.4 us
  transfers between devices with their start and end apart: 2, of which 0 were waited for; matrix products, arithmetic and copies ran while one was open for 2% of the time, Pallas kernels for 28%

profile of v2, /device:TPU:0, one launch (start us, length us, event | category | flops | bytes accessed | tf_op | source)
XLA Modules:
  0.0 740.4 jit_solution(17976637174996699328)
XLA Ops:
  7.2 0.0 all-gather.3.cloned.1.call-start
  7.2 1.6 dynamic-slice_convert_fusion.1
  8.9 0.0 all-gather.3.cloned.1.call-update
  8.9 0.0 all-gather.5.cloned.1.call-start
  8.9 1.6 dynamic-slice_convert_fusion
  11.4 4.0 convert_element_type.49
  15.4 1.6 convert_element_type.50
  17.0 0.9 copy.49.keep_ref
  17.9 0.6 copy.56
  18.5 0.6 copy.57
  19.1 0.6 broadcast_in_dim.3.refs_2_
  19.7 156.0 %shard_map.392 = (bf16[4,2,4,256,1024]{4,3,2,1,0:T(8,128)(2,1)}, bf16[4,2,4,32,8192]{4,3,2,1,0:T(8,128)(2,1)}, f32[8,128]{1,0:T(8,128)}) custom-call(bf16[4,256,1024]{2,1,0:T(8,128)(2,1)} %bitcast.45, bf16[4,32,8192]{2,1,0:T(8,128)(2,1)} %bitcast.46, f32[8,128]{1,0:T(8,128)} %broadcast_in_dim.3.refs_2_), custom_call_target="tpu_custom_call" | custom-call | tf_op jit(solution)/shard_map/pallas_call | solution.py:835
  175.7 1.2 slice.34
  178.2 0.6 pad_maximum_fusion.scal_ref
  178.8 3.3 slice.46.down_ref
  182.0 1.4 fusion.37
  183.5 53.1 %shard_map.393 = (f32[512,512]{1,0:T(8,128)}, bf16[512,1024]{1,0:T(8,128)(2,1)}, s32[512,1]{1,0:T(8,128)}, f32[512,1024]{1,0:T(8,128)}, bf16[512,3072]{1,0:T(8,1...) custom-call(bf16[8,256,1024]{2,1,0:T(8,128)(2,1)} %bitcast.65, ...), custom_call_target="tpu_custom_call" | custom-call | flops 20000000000 | bytes 70000000 | tf_op jit(solution)/shard_map/pallas_call | solution.py:507
  236.6 0.0 all-gather.5.cloned.1.call-done.cols_ref
  236.6 137.8 %shard_map.394 = (bf16[8,64,512]{2,1,0:T(8,128)(2,1)}, bf16[512,4096]{1,0:T(8,128)(2,1)}, bf16[2048,512]{1,0:T(8,128)(2,1)}, bf16[1024,512]{1,0:T(8,128)(2,1)}, f32[8,512]{1,0:T(8,128)}, /*index=5*/f32[1,1]{1,0:T(1,128)}) custom-call(f32[2,8]{1,0:T(2,128)} %pad_maximum_fusion.scal_ref, f32[8,64,512]{2,1,0:T(8,128)} %bitcast.69, s32[8,64,1]{2,1,0:T(8,128)} %copy.49.keep_ref, ...), custom_call_target="tpu_custom_call" | custom-call | flops 70000001024 | bytes 40000000 | tf_op jit(solution)/shard_map/pallas_call | solution.py:332
  374.5 75.4 %shard_map.395 = (bf16[8192,1024]{1,0:T(8,128)(2,1)}, bf16[1024,8192]{1,0:T(8,128)(2,1)}, bf16[1024,512]{1,0:T(8,128)(2,1)}, f32[8,1024]{1,0:T(8,128)}) custom-call(bf16[512,512]{1,0:T(8,128)(2,1)} %bitcast.70, bf16[512,1024]{1,0:T(8,128)(2,1)} %get-tuple-element.56.pix_ref, s32[512,1]{1,0:T(8,128)} %get-tuple-element.57.band_ref, ...), custom_call_target="tpu_custom_call" | custom-call | flops 40000000000 | bytes 110000000 | tf_op jit(solution)/shard_map/pallas_call | solution.py:654
  449.9 0.8 reshape.176
  450.6 0.7 select_maximum_fusion
  451.3 0.6 reshape.178.refs_6_
  452.0 244.1 %shard_map.396 = (bf16[4,256,1024]{2,1,0:T(8,128)(2,1)}, bf16[4,32,8192]{2,1,0:T(8,128)(2,1)}, bf16[4,16,4096]{2,1,0:T(8,128)(2,1)}, bf16[4,128,512]{2,1,0:T(8,1...) custom-call(bf16[4,2,4,256,1024]{4,3,2,1,0:T(8,128)(2,1)} %bitcast.41, bf16[4,2,4,32,8192]{4,3,2,1,0:T(8,128)(2,1)} %bitcast.42, ...), custom_call_target="tpu_custom_call" | custom-call | tf_op jit(solution)/shard_map/pallas_call | solution.py:1159
  696.0 1.0 slice.42
  697.0 1.4 multiply_reduce_fusion
  698.4 0.9 copy.51
  699.3 0.5 slice.49
  700.4 0.6 multiply_reduce_fusion.1
  701.1 1.2 slice.40
  704.3 1.2 convert_multiply_fusion.2
  705.5 1.5 convert_multiply_fusion.3
  707.0 0.6 convert_multiply_fusion
  707.8 0.4 convert_multiply_fusion.1
  708.3 0.1 copy-done.23
  708.4 0.1 copy-done.24
  708.4 0.0 copy-done.25
  708.5 0.6 fusion.29
  709.1 0.7 fusion.24
  709.8 0.3 copy-done.13
  710.1 1.1 copy-done.15
  711.2 1.1 copy-done.16
  712.2 2.1 fusion.19
  714.3 2.1 fusion.14
  716.4 1.3 copy-done.9
  717.6 1.2 copy-done
  718.9 5.5 fusion.9
  724.4 6.5 fusion.4
  (58 shorter events, 0.2 us)
Async XLA Ops:
  7.2 171.6 %all-gather.3.cloned.1.call-start = ((), (), s32[]{:S(2)}) async-start(), calls=%async_computation | async-start | bytes 4325376 | tf_op jit(solution)/shard_map/all_gather | solution.py:1284
  8.9 227.7 %all-gather.5.cloned.1.call-start = ((), (), s32[]{:S(2)}) async-start(), calls=%async_computation.1 | async-start | bytes 4325376 | tf_op jit(solution)/shard_map/all_gather | solution.py:1284
  10.6 4.8 copy-start.1
  15.4 1.6 copy-start.29
  15.4 2.5 copy-start.27
  15.4 3.1 copy-start.28
  178.8 3.3 copy-start.7
  374.5 76.2 %copy-start.26 = (f32[8,512]{1,0:T(8,128)S(1)}, f32[8,512]{1,0:T(8,128)}, u32[]{:S(2)}) copy-start(f32[8,512]{1,0:T(8,128)} %get-tuple-element.74) | copy-start | bytes 49156
  696.0 11.0 %copy-start.12 = (bf16[4,256,1024]{2,1,0:T(8,128)(2,1)S(1)}, bf16[4,256,1024]{2,1,0:T(8,128)(2,1)}, u32[]{:S(2)}) copy-start(bf16[4,256,1024]{2,1,0:T(8,128)(2,1)} %get-tuple-element.79) | copy-start | bytes 6291460
  705.5 4.3 copy-start.5
  705.5 2.3 copy-start.11
  707.0 7.3 copy-start.6
  707.6 8.8 %copy-start.3 = (f32[4,256,1024]{2,1,0:T(8,128)}, f32[4,256,1024]{2,1,0:T(8,128)S(1)}, u32[]{:S(2)}) copy-start(f32[4,256,1024]{2,1,0:T(8,128)S(1)} %convert_multiply_fusion) | copy-start | bytes 12582916
  707.6 0.7 copy-start.23
  707.6 0.8 copy-start.24
  707.7 0.8 copy-start.25
  707.7 1.5 copy-start.19
  707.7 1.4 copy-start.20
  707.7 1.4 copy-start.21
  707.7 1.4 copy-start.22
  707.7 2.4 copy-start.13
  707.7 3.4 copy-start.15
  707.7 4.5 copy-start.16
  707.8 6.5 copy-start.14
  707.8 6.5 copy-start.17
  707.8 6.5 copy-start.18
  708.3 16.1 %copy-start.4 = (f32[4,32,8192]{2,1,0:T(8,128)}, f32[4,32,8192]{2,1,0:T(8,128)S(1)}, u32[]{:S(2)}) copy-start(f32[4,32,8192]{2,1,0:T(8,128)S(1)} %convert_multiply_fusion.1) | copy-start | bytes 12582916
  712.2 4.2 copy-start.8
  712.2 5.4 copy-start.9
  714.3 4.6 copy-start
  718.9 5.5 copy-start.2
  718.9 5.5 copy-start.10
Sparse Core Ops, SparseCore 0:
  11.5 84.6 all-gather.2
  99.6 78.4 all-gather.4

commit v3 on v2

--- a/solution.py
+++ b/solution.py
@@ -105,7 +105,7 @@
     o_s[rs, qa] = out.astype(o_s.dtype)
 
 
-def attend_back(n, groups, tokens, width, ee, scale, qkv_s, s_s, ds_s, p_s, inv_s, oo_s, do_s, dqkv_s):
+def attend_back(n, slot, groups, tokens, width, ee, scale, qkv_s, s_s, ds_s, p_s, inv_s, oo_s, do_s, dqkv_s):
     low = dqkv_s.dtype
     item = n // groups
     g = n % groups
@@ -114,8 +114,8 @@
     ka = pl.ds(pl.multiple_of(width + g * LANES, LANES), LANES)
     va = pl.ds(pl.multiple_of(2 * width + g * LANES, LANES), LANES)
     heads = range(LANES // ee)
-    do = do_s[rs, qa].astype(jnp.float32) * inv_s[n]
-    rest = (-do * oo_s[n]).astype(low)
+    do = do_s[rs, qa].astype(jnp.float32) * inv_s[slot]
+    rest = (-do * oo_s[slot]).astype(low)
     do_t = do.T.astype(low)
     do = do.astype(low)
     v = qkv_s[rs, va]
@@ -125,8 +125,8 @@
     )
     for h in heads:
         at = slice(h * tokens, (h + 1) * tokens)
-        ds_s[:, at] = (p_s[n, :, at].astype(jnp.float32) * s_s[at, :]).astype(low)
-    e_rows = jnp.concatenate([p_s[n, :, h * tokens : (h + 1) * tokens] for h in heads], 0)
+        ds_s[:, at] = (p_s[slot, :, at].astype(jnp.float32) * s_s[at, :]).astype(low)
+    e_rows = jnp.concatenate([p_s[slot, :, h * tokens : (h + 1) * tokens] for h in heads], 0)
     ds_rows = jnp.concatenate([ds_s[:, h * tokens : (h + 1) * tokens] for h in heads], 0)
     dv_t = dot_nn(stack_lanes(do_t, ee), e_rows)
     dk_t = dot_nn(stack_lanes(qkv_s[rs, qa].T, ee), ds_rows)
@@ -277,7 +277,7 @@
 
     @pl.loop(0, items * groups)
     def _(n):
-        attend_back(n, groups, tokens, width, ee, scale, qkv_s, s_s, ds_s, p_s, inv_s, oo_s, o_s, dqkv_s)
+        attend_back(n, n, groups, tokens, width, ee, scale, qkv_s, s_s, ds_s, p_s, inv_s, oo_s, o_s, dqkv_s)
 
     acc_s[...] = jnp.zeros_like(acc_s)
 
@@ -393,8 +393,8 @@
 
 def encoder_kernel(
     heads, pixels_ref, keep_ref, bands_ref, gsd_ref, table_ref, rows_ref, cols_ref, de_ref, gains_ref,
-    z_ref, pix_ref, band_ref, x_ref, qkv_ref, p_ref, inv_ref, oo_ref, x1_ref, a_ref, gp_ref, x2_ref,
-    h_s, s_s, o_s, high_s, low_s,
+    z_ref, pix_ref, band_ref, x_ref, qkv_ref, p_ref, inv_ref, oo_ref, x1_ref, a_ref, gp_ref, x2_ref, o_s,
+    h_s, s_s, high_s, low_s,
 ):
     low = jnp.bfloat16
     step = pl.program_id(0)
@@ -503,6 +503,7 @@
         (jax.ShapeDtypeStruct(ff, low), pl.BlockSpec((tokens, width), hidden_block)),
         (jax.ShapeDtypeStruct(ff, low), pl.BlockSpec((tokens, width), hidden_block)),
         hold((tokens, width)),
+        hold((tokens, width), low),
     ]
     return pl.pallas_call(
         functools.partial(encoder_kernel, heads),
@@ -523,7 +524,6 @@
         scratch_shapes=[
             pltpu.VMEM((tokens, width), low),
             pltpu.VMEM((wide, RUN), f32),
-            pltpu.VMEM((tokens, width), low),
             pltpu.VMEM((table.shape[0], width), low),
             pltpu.VMEM((table.shape[0], width), low),
         ],
@@ -595,7 +595,7 @@
         @pl.loop(0, runs * groups)
         def _(n):
             attend_back(
-                n, groups, RUN, width, ee, ee ** (-0.5), qkv_ref, s_s, ds_s, p_ref, inv_ref, oo_ref, do_s,
+                n, n, groups, RUN, width, ee, ee ** (-0.5), qkv_ref, s_s, ds_s, p_ref, inv_ref, oo_ref, do_s,
                 dqkv_s,
             )
 
@@ -621,7 +621,7 @@
 
 
 def encoder_back_call(dz, pixel, band, saved, rows, cols, de, gains, heads):
-    x, qkv, p, inv, oo, x1, a, gp, x2 = saved
+    x, qkv, p, inv, oo, x1, a, gp, x2, _ = saved
     tokens, width = x.shape
     low, f32 = jnp.bfloat16, jnp.float32
     wide = p.shape[2]
@@ -846,15 +846,15 @@
     return [o.reshape(-1, o.shape[-1]) for o in outs], total[0, 0]
 
 
-def reduce_kernel(n_in, n_out, kinds, work, ahead, offsets, z_offsets, newest_last, *refs):
-    ins = refs[:n_in]
-    small_ref = refs[n_in]
-    outs = refs[n_in + 1 : n_in + 1 + n_out]
-    small_out, ss_out = refs[n_in + 1 + n_out : n_in + 3 + n_out]
-    rest = refs[n_in + 3 + n_out :]
-    bufs = [rest[9 * i : 9 * i + 9] for i in range(len(kinds))]
-    (sm, ss, ssx, cs, cr, os, x1s, x1r, x2s, x2r, z_s, z_r, ags, agr, ls, sms, smr, sss, ssr) = rest[
-        9 * len(kinds) :
+def back_reduce_kernel(heads, kinds, work, pieces, refs_in, refs_out, *refs):
+    low, f32 = jnp.bfloat16, jnp.float32
+    ref = dict(zip(refs_in + refs_out, refs))
+    rest = refs[len(refs_in) + len(refs_out) :]
+    per = 9
+    bufs = [rest[per * i : per * i + per] for i in range(len(kinds))]
+    (sm, ss, ssx, dx, acc, xin, h, dy, wide, wt, wu, out_r, out_c, out_e, p_t, inv_t, oo_t, s_s, ds_s, gsum,
+     cs, cr, ls, os, x1s, x1r, x2s, x2r, z_s, z_r, ags, agr, ks, sms, smr, sss, ssr, dma, att_sem) = rest[
+        per * len(kinds) :
     ]
     g, z, c, xn, yn = place()
     dg = (xn + 2) % 4
@@ -866,8 +866,7 @@
     greet([sib, right, up] + zpeer)
     steps = len(work)
     sent = []
-    f32 = jnp.float32
-    slots = ahead + 1
+    from_slot = [[] for _ in range(steps)]
 
     def send(src, dst, send_sem, recv_sem, peer):
         return pltpu.make_async_remote_copy(
@@ -875,97 +874,103 @@
             device_id=peer, device_id_type=MESH_ID,
         )
 
-    def go(copies):
-        for copy in copies:
-            copy.start()
-            sent.append(copy)
+    def guarded(test, action):
+        if test is None:
+            action()
+        else:
+            pl.when(test)(action)
+
+    def go(copies, keep=None, tests=None):
+        for i, copy in enumerate(copies):
+            test = tests[i] if tests else None
+            guarded(test, copy.start)
+            (sent if keep is None else keep).append((test, copy))
+
+    def left(entries):
+        for test, copy in entries:
+            guarded(test, copy.wait_send)
 
     def got(copies):
         for copy in copies:
             copy.wait_recv()
 
+    def mine(k, at=None):
+        base = work[k][2]
+        at = z if at is None else at
+        return None if base is None else ((at >= base) & (at < base + 2))
+
     def buffers(k):
         kind, at = work[k][:2]
-        return bufs[kind], at, kinds[kind][1] // 2
+        return bufs[kind], at, at % kinds[kind][4], kinds[kind][2] // 2
 
     def c_copies(k):
-        (s, *_), at, _ = buffers(k)
+        (_, crecv, *_), at, _, _ = buffers(k)
         return [
             send(
-                ins[array].at[:, 1 - c, :, cut[0], cut[1]], s.at[at, pl.ds(z0, nz)],
+                ref[array].at[:, 1 - c, :, cut[0], cut[1]], crecv.at[at, pl.ds(z0, nz)],
                 cs.at[k, i], cr.at[k, i], sib,
             )
             for i, (array, z0, nz, cut) in enumerate(work[k][3])
         ]
 
     def own_copies(k):
-        (_, own, *_), at, _ = buffers(k)
+        (s, *_), _, slot, _ = buffers(k)
         return [
             pltpu.make_async_copy(
-                ins[array].at[:, c, :, cut[0], cut[1]], own.at[at % slots, pl.ds(z0, nz)], os.at[k, i]
+                ref[array].at[:, c, :, cut[0], cut[1]], s.at[slot, pl.ds(z0, nz)], os.at[k, i]
             )
             for i, (array, z0, nz, cut) in enumerate(work[k][3])
         ]
 
-    def begin(k):
-        go(c_copies(k))
-        for copy in own_copies(k):
-            copy.start()
-
-    def planes(k):
-        if work[k][2]:
-            return pl.ds(z, 1), pl.ds(0, 1), 1
-        return pl.ds(0, 4), pl.ds(0, 4), 4
+    def recv_load(k, i):
+        (_, crecv, tmp, *_), at, _, _ = buffers(k)
+        return pltpu.make_async_copy(crecv.at[at, i], tmp.at[i % 2], ls.at[k, i])
 
     def x1_copies(k):
-        (s, _, xa, yb, *_), at, half = buffers(k)
-        src, dst, _ = planes(k)
-        left, right_half = pl.ds(0, half), pl.ds(half, half)
+        (s, _, _, xa, yb, *_), at, slot, half = buffers(k)
+        lo, hi = pl.ds(0, half), pl.ds(half, half)
         return [
-            send(s.at[at, src, xn, :, left], xa.at[at, 0, dst], x1s.at[k, 0], x1r.at[k, 0], right),
-            send(s.at[at, src, dg, :, left], xa.at[at, 1, dst], x1s.at[k, 1], x1r.at[k, 1], right),
-            send(s.at[at, src, yn, :, right_half], yb.at[at, 0, dst], x1s.at[k, 2], x1r.at[k, 2], up),
-            send(s.at[at, src, dg, :, right_half], yb.at[at, 1, dst], x1s.at[k, 3], x1r.at[k, 3], up),
+            send(s.at[slot, :, xn, :, lo], xa.at[at, 0], x1s.at[k, 0], x1r.at[k, 0], right),
+            send(s.at[slot, :, dg, :, lo], xa.at[at, 1], x1s.at[k, 1], x1r.at[k, 1], right),
+            send(s.at[slot, :, yn, :, hi], yb.at[at, 0], x1s.at[k, 2], x1r.at[k, 2], up),
+            send(s.at[slot, :, dg, :, hi], yb.at[at, 1], x1s.at[k, 3], x1r.at[k, 3], up),
         ]
 
     def x2_copies(k):
-        (s, _, _, _, xb, ya, *_), at, half = buffers(k)
-        src, dst, _ = planes(k)
-        left, right_half = pl.ds(0, half), pl.ds(half, half)
+        (s, _, _, _, _, xb, ya, *_), at, slot, half = buffers(k)
+        lo, hi = pl.ds(0, half), pl.ds(half, half)
         return [
-            send(s.at[at, src, yn, :, left], ya.at[at, dst], x2s.at[k, 0], x2r.at[k, 0], up),
-            send(s.at[at, src, xn, :, right_half], xb.at[at, dst], x2s.at[k, 1], x2r.at[k, 1], right),
+            send(s.at[slot, :, yn, :, lo], ya.at[at], x2s.at[k, 0], x2r.at[k, 0], up),
+            send(s.at[slot, :, xn, :, hi], xb.at[at], x2s.at[k, 1], x2r.at[k, 1], right),
         ]
 
     def z_copies(k):
-        (s, _, _, _, _, _, zb, *_), at, _ = buffers(k)
-        if work[k][2]:
-            zt = bufs[work[k][0]][8]
-            return [
-                send(s.at[at, zto[j]], zt.at[work[k][2] - 1, j], z_s.at[k, j], z_r.at[k, j], zpeer[j])
-                for j in range(3)
-            ]
+        (s, *_, zb, _), at, slot, _ = buffers(k)
+        base = work[k][2] or 0
         return [
-            send(s.at[at, zto[j], g], zb.at[at, j], z_s.at[k, j], z_r.at[k, j], zpeer[j])
+            send(
+                s.at[slot, (zto[j] - base) % kinds[work[k][0]][0], g], zb.at[at, j],
+                z_s.at[k, j], z_r.at[k, j], zpeer[j],
+            )
             for j in range(3)
         ]
 
     def out_at(k, q, part=None):
-        index, cut = work[k][4:]
+        name, cut = work[k][4:6]
         if part is not None:
             cut = halves(cut)[part]
-        return outs[index].at[q, cut[0], cut[1]]
+        return ref[name].at[q, cut[0], cut[1]]
 
     def ag_copies(k):
-        (*_, fin, _), at, _ = buffers(k)
+        (*_, fin), at, _, _ = buffers(k)
         return [
             send(fin.at[at], out_at(k, g), ags.at[k, 0], agr.at[k, 0], right),
             send(fin.at[at], out_at(k, g), ags.at[k, 1], agr.at[k, 1], up),
         ]
 
     def keep_copy(k):
-        (*_, fin, _), at, _ = buffers(k)
-        return pltpu.make_async_copy(fin.at[at], out_at(k, g), ls.at[k])
+        (*_, fin), at, _, _ = buffers(k)
+        return pltpu.make_async_copy(fin.at[at], out_at(k, g), ks.at[k])
 
     def fwd_copies(k, of_x, of_y):
         return [
@@ -973,101 +978,87 @@
             send(out_at(k, of_y, 1), out_at(k, of_y, 1), ags.at[k, 3], agr.at[k, 3], right),
         ]
 
-    def add_half(k, q, left, other):
-        (s, *_), at, half = buffers(k)
-        part = pl.ds(0 if left else half, half)
-        if work[k][2]:
-            s[at, z, q, :, part] = (s[at, z, q, :, part].astype(f32) + other[0].astype(f32)).astype(s.dtype)
-            return
-
-        @pl.loop(0, 4)
+    def add_half(k, q, first, other):
+        (s, *_), _, slot, half = buffers(k)
+        part = pl.ds(0 if first else half, half)
+
+        @pl.loop(0, kinds[work[k][0]][0])
         def _(i):
-            s[at, i, q, :, part] = (s[at, i, q, :, part].astype(f32) + other[i].astype(f32)).astype(s.dtype)
+            s[slot, i, q, :, part] = (s[slot, i, q, :, part].astype(f32) + other[i].astype(f32)).astype(low)
+
+    def load(k):
+        kind, at = work[k][:2]
+        slots = kinds[kind][4]
+        if at >= slots:
+            before = [j for j in range(steps) if work[j][:2] == (kind, at - slots)][0]
+            left(from_slot[before])
+            from_slot[before].clear()
+        for copy in own_copies(k):
+            copy.start()
 
     def pair(k):
-        (s, own, *_), at, _ = buffers(k)
+        (s, _, tmp, *_), _, slot, _ = buffers(k)
+        count = kinds[work[k][0]][0]
         got(c_copies(k))
+        for i in range(2):
+            recv_load(k, i).start()
         for copy in own_copies(k):
             copy.wait()
-
-        @pl.loop(0, 4)
-        def _(i):
-            for q in range(4):
-                s[at, i, q] = (s[at, i, q].astype(f32) + own[at % slots, i, q].astype(f32)).astype(s.dtype)
+        for i in range(count):
+            recv_load(k, i).wait()
+
+            @pl.loop(0, 4)
+            def _(q):
+                s[slot, i, q] = (s[slot, i, q].astype(f32) + tmp[i % 2, q].astype(f32)).astype(low)
+
+            if i + 2 < count:
+                recv_load(k, i + 2).start()
+        go(x1_copies(k), from_slot[k])
 
     def first_half(k):
-        (_, _, xa, yb, *_), at, _ = buffers(k)
+        (_, _, _, xa, yb, *_), at, _, _ = buffers(k)
         got(x1_copies(k))
         add_half(k, yn, True, xa.at[at, 1])
         add_half(k, xn, False, yb.at[at, 1])
-        go(x2_copies(k))
+        go(x2_copies(k), from_slot[k])
         add_half(k, g, True, xa.at[at, 0])
         add_half(k, g, False, yb.at[at, 0])
 
     def second_half(k):
-        (_, _, _, _, xb, ya, *_), at, _ = buffers(k)
+        (_, _, _, _, _, xb, ya, *_), at, _, _ = buffers(k)
         got(x2_copies(k))
         add_half(k, g, True, ya.at[at])
         add_half(k, g, False, xb.at[at])
-
-    def finish(k, total):
-        (*_, fin, _), at, _ = buffers(k)
-        fin[at] = total.astype(fin.dtype)
-        go(ag_copies(k))
-        keep_copy(k).start()
-        square = fin[at].astype(f32)
-        square = square * square
-        for i in range(square.shape[1] // ss.shape[1]):
-            ss[...] += jnp.sum(
-                square[:, i * ss.shape[1] : (i + 1) * ss.shape[1]], 0, keepdims=True
-            )
+        go(z_copies(k), from_slot[k], [mine(k, t) for t in zto])
+
+    def finish(k):
+        def act():
+            (s, *_, zb, fin), at, slot, _ = buffers(k)
+            got(z_copies(k))
+            base = work[k][2] or 0
+            total = s[slot, (z - base) % kinds[work[k][0]][0], g].astype(f32)
+            for j in range(3):
+                total = total + zb[at, j].astype(f32)
+            fin[at] = total.astype(low)
+            keep_copy(k).start()
+            square = fin[at].astype(f32)
+            square = square * square
+            for i in range(square.shape[1] // ss.shape[1]):
+                ss[...] += jnp.sum(
+                    square[:, i * ss.shape[1] : (i + 1) * ss.shape[1]], 0, keepdims=True
+                )
+
+        guarded(mine(k), act)
+        go(ag_copies(k), None, [mine(k)] * 2)
 
     def collect(k):
-        got(ag_copies(k))
-        go(fwd_copies(k, xn, yn))
+        guarded(mine(k), lambda: got(ag_copies(k)))
+        go(fwd_copies(k, xn, yn), None, [mine(k)] * 2)
 
     def close(k):
-        got(fwd_copies(k, dg, dg))
-
-    def p1(k):
-        pair(k)
-        go(x1_copies(k))
-
-    def p3(k):
-        second_half(k)
-        go(z_copies(k))
-
-    def p4(k):
-        (s, _, _, _, _, _, zb, *_), at, _ = buffers(k)
-        got(z_copies(k))
-        total = s[at, z, g].astype(f32)
-        for j in range(3):
-            total = total + zb[at, j].astype(f32)
-        finish(k, total)
-
-    def z1(k):
-        pair(k)
-        go(z_copies(k))
-
-    def z2(k):
-        (s, *_), at, _ = buffers(k)
-        zt = bufs[work[k][0]][8]
-        i = work[k][2] - 1
-        got(z_copies(k))
-        for q in range(4):
-            total = s[at, z, q].astype(f32)
-            for j in range(3):
-                total = total + zt[i, j, q].astype(f32)
-            s[at, z, q] = total.astype(s.dtype)
-        go(x1_copies(k))
-
-    def z4(k):
-        (s, *_), at, _ = buffers(k)
-        second_half(k)
-        finish(k, s[at, z, g].astype(f32))
-
-    plane_stages = [p1, first_half, p3, p4, collect, close]
-    z_stages = [z1, z2, first_half, z4, collect, close]
+        guarded(mine(k), lambda: got(fwd_copies(k, dg, dg)))
+
+    stages = [load, pair, first_half, second_half, finish, collect, close]
 
     def share_rounds(value, sem_s, sem_r, store):
         def copy(i, slot, peer):
@@ -1099,142 +1090,328 @@
             end,
         ]
 
-    sm[0] = small_ref[...]
+    tokens, width = dx.shape
+    ee = width // heads
+    groups = width // LANES
+    runs = tokens // RUN
+    gains = ref["gains"]
+
+    moving = {}
+
+    def move(name, src, dst):
+        copy = pltpu.make_async_copy(src, dst, dma.at[lanes_of.index(name)])
+        copy.start()
+        moving[name] = copy
+
+    def done(*names):
+        for name in names:
+            if name in moving:
+                moving.pop(name).wait()
+
+    lanes_of = (
+        "a", "gp", "rows", "cols", "x", "dz", "de", "o", "qkv", "pix", "out_r", "out_c", "out_e",
+    )
+
+    def tile(i):
+        return pl.ds(i * width, width)
+
+    def gain(i):
+        return gains[i : i + 1, :]
+
+    def back(grads, at):
+        hat, scaled = unit_rows(xin[...])
+        gsum[at : at + 1, :] = jnp.sum(grads * hat, 0, keepdims=True)
+        gsum[at + 1 : at + 2, :] = jnp.sum(grads, 0, keepdims=True)
+        return unit_back(grads, hat, scaled, gain(at))
+
+    def normed(at):
+        hat, _ = unit_rows(xin[...])
+        h[...] = (hat * gain(at) + gain(at + 1)).astype(low)
+
+    def column_grads(block, source):
+        done("out_c")
+        for d in range(8):
+            value = dot_tn(h[:, d * 128 : (d + 1) * 128], source()).astype(low)
+            out_c[d // 2, d % 2] = value.reshape(out_c.shape[2:])
+        move("out_c", out_c, ref["g_cols"].at[:, :, :, :, tile(block)])
+
+    def load_hidden(s):
+        move("a", ref["a"].at[:, tile(s)], wide.at[:, tile(0)])
+        move("gp", ref["gp"].at[:, tile(s)], wide.at[:, tile(1)])
+        move("rows", ref["rows"].at[tile(s)], wt)
+
+    def load_columns(block):
+        move("cols", ref["cols"].at[:, tile(block)], wu)
+
+    narrow = ref["dz"].shape[1]
+
+    def first_loads():
+        move("x", ref["x2"], xin)
+        move("dz", ref["dz"], wide.at[:, pl.ds(2 * width, narrow)])
+        move("de", ref["de"], wt.at[:, pl.ds(0, narrow)])
+        move("a", ref["a"].at[:, tile(0)], wide.at[:, tile(0)])
+        move("gp", ref["gp"].at[:, tile(0)], wide.at[:, tile(1)])
+        load_columns(4)
+
+    def head_piece(_):
+        done("x", "dz", "de")
+        dz = wide[:, 2 * width : 2 * width + narrow]
+        normed(4)
+        for d in range(8):
+            out_e[0, d // 4, d % 4] = dot_tn(h[:, d * 128 : (d + 1) * 128], dz).astype(low)
+        move("out_e", out_e, ref["g_de"])
+        dx[...] = back(dot_nt(dz, wt[:, :narrow]), 4)
+        move("rows", ref["rows"].at[tile(0)], wt)
+        move("x", ref["x1"], xin)
+        dy[...] = dx[...].astype(low)
+        done("x")
+        normed(2)
+        acc[...] = jnp.zeros_like(acc)
+
+    def hidden_piece(s):
+        done("a", "gp", "rows", "out_r")
+        wide[:, 2 * width :] = (dot_nt(dy[...], wt[...]) * wide[:, width : 2 * width].astype(f32)).astype(low)
+        for q in range(4):
+            out_r[q] = dot_tn(wide[:, q * 256 : (q + 1) * 256], dy[...]).astype(low)
+        move("out_r", out_r, ref["g_down"].at[s // 2, s % 2])
+        if s < 3:
+            load_hidden(s + 1)
+        column_grads(4 + s, lambda: wide[:, 2 * width :])
+        done("cols")
+        acc[...] += dot_nt(wide[:, 2 * width :], wu[...])
+        load_columns(5 + s if s < 3 else 3)
+        if s == 3:
+            move("o", ref["o"], h)
+            move("qkv", ref["qkv"], wide)
+
+    def middle_piece(_):
+        dx[...] += back(acc[...], 2)
+        dy[...] = dx[...].astype(low)
+        move("x", ref["x"], xin)
+        done("o")
+        column_grads(3, lambda: dy[...])
+        done("cols")
+        h[...] = dot_nt(dy[...], wu[...]).astype(low)
+        load_columns(0)
+        done("qkv")
+
+    def attention_loads(n):
+        slot = n % 2
+        return [
+            pltpu.make_async_copy(ref[name].at[n], buf.at[slot], att_sem.at[slot, i])
+            for i, (name, buf) in enumerate((("p", p_t), ("inv", inv_t), ("oo", oo_t)))
+        ]
+
+    def attention_piece(part):
+        count = runs * groups // 4
+        first = part * count
+        for copy in attention_loads(first):
+            copy.start()
+
+        @pl.loop(0, count)
+        def _(i):
+            n = first + i
+            for copy in attention_loads(n):
+                copy.wait()
+
+            @pl.when(i + 1 < count)
+            def _():
+                for copy in attention_loads(n + 1):
+                    copy.start()
+
+            attend_back(
+                n, n % 2, groups, RUN, width, ee, ee ** (-0.5), wide, s_s, ds_s, p_t, inv_t, oo_t, h, wide
+            )
+
+    def input_piece(t):
+        if t == 0:
+            done("x")
+            normed(0)
+            acc[...] = jnp.zeros_like(acc)
+        column_grads(t, lambda: wide[:, t * width : (t + 1) * width])
+        done("cols")
+        acc[...] += dot_nt(wide[:, t * width : (t + 1) * width], wu[...])
+        if t < 2:
+            load_columns(t + 1)
+        else:
+            move("pix", ref["pix"], h)
+
+    def first_piece(_):
+        dx[...] += back(acc[...], 0)
+        dy[...] = dx[...].astype(low)
+        sm[0] = ref["small"][...]
+        sm[0, 0:6, :] = gsum[0:6, :]
+
+    def embed_piece(b):
+        done("pix", "out_r")
+        for q in range(4):
+            part = h[:, q * 256 : (q + 1) * 256]
+            part = jnp.where(ref["band"][...] == b, part, jnp.zeros_like(part))
+            out_r[q] = dot_tn(part, dy[...]).astype(low)
+        move("out_r", out_r, ref["g_emb"].at[b // 2, b % 2])
+
+    action = {
+        "head": head_piece, "hidden": hidden_piece, "middle": middle_piece, "attention": attention_piece,
+        "input": input_piece, "first": first_piece, "embed": embed_piece,
+    }
+
     ss[...] = jnp.zeros_like(ss)
-    small_rounds = share_rounds(sm, sms, smr, small_out)
-    small_rounds[0]()
-    for k in range(min(ahead, steps)):
-        begin(k)
-    square_rounds = share_rounds(ssx, sss, ssr, ss_out)
-    def at_time(k, i):
-        return k + (z_offsets if work[k][2] else offsets)[i]
-
-    last = max(at_time(k, 5) for k in range(steps))
-    squared = max(at_time(k, 3) for k in range(steps))
+    gsum[...] = jnp.zeros_like(gsum)
+    small_rounds = share_rounds(sm, sms, smr, ref["small_out"])
+    square_rounds = share_rounds(ssx, sss, ssr, ref["ss_out"])
+    ends = [w[6] + 6 for w in work]
+    last = max(ends)
+    squared = max(w[6] + 4 for w in work)
+    compute_end = max(t for t, _, _ in pieces)
     for t in range(last + 1):
-        for k in range(steps) if newest_last else reversed(range(steps)):
-            for i in range(6):
-                if at_time(k, i) == t:
-                    (z_stages if work[k][2] else plane_stages)[i](k)
-                    if i == 0 and k + ahead < steps:
-                        begin(k + ahead)
-        if t < 4:
-            small_rounds[t + 1]()
+        for i in (1, 6, 5, 4, 3, 2, 0):
+            for k in range(steps):
+                if work[k][6] + i == t:
+                    stages[i](k)
+        if t == 0:
+            first_loads()
+        done("out_r", "out_c", "out_e")
+        for k in range(steps):
+            if work[k][7] == t:
+                go(c_copies(k))
+        for at, name, argument in pieces:
+            if at == t:
+                action[name](argument)
+        if compute_end < t <= compute_end + 5:
+            small_rounds[t - compute_end - 1]()
         if t == squared:
             ssx[0] = jnp.broadcast_to(jnp.sum(ss[...], keepdims=True).reshape(1, 1), ssx.shape[1:])
             square_rounds[0]()
-        if squared < t < last and t - squared < 3:
+        if squared < t < last:
             square_rounds[t - squared]()
         if t == last:
-            for following in square_rounds[min(3, last - squared) :]:
+            for following in square_rounds[last - squared :]:
                 following()
-    for copy in sent:
-        copy.wait_send()
     for k in range(steps):
-        keep_copy(k).wait()
-
-
-def reduce_call(grads, small, kinds, work, out_shapes, ahead, offsets, z_offsets, newest_last, collective_id):
+        left(from_slot[k])
+    left(sent)
+    for k in range(steps):
+        guarded(mine(k), keep_copy(k).wait)
+
+
+def back_reduce_call(dz, pix, band, saved, rows, cols, de, gains, dcols, ddown, dhead, small, heads):
+    x, qkv, p, inv, oo, x1, a, gp, x2, o = saved
+    tokens, width = x.shape
+    low, f32 = jnp.bfloat16, jnp.float32
+    narrow = de.shape[1]
+    ins = dict(
+        dz=dz, pix=pix, band=band, x=x, x1=x1, x2=x2, qkv=qkv, p=p, inv=inv, oo=oo, o=o, a=a, gp=gp,
+        rows=rows, cols=cols, de=de, gains=gains, small=small,
+        d_cols=dcols.reshape(4, 2, 4, 16, dcols.shape[1]),
+        d_down=ddown.reshape(2, 2, 4, 128, narrow),
+        d_head=dhead.reshape(1, 2, 4, 128, narrow),
+    )
+    outs = dict(
+        erows=((4, 256, width), low), ecols=((4, 32, cols.shape[1]), low),
+        dcols=((4, 16, dcols.shape[1]), low), drows=((4, 128, narrow), low),
+        small_out=(small.shape, f32), ss_out=((8, 128), f32),
+        g_down=((2, 2, 4, 256, width), low), g_emb=((2, 2, 4, 256, width), low),
+        g_cols=((4, 2, 4, 32, cols.shape[1]), low), g_de=((1, 2, 4, 128, narrow), low),
+    )
+    kinds = ((4, 32, 1024, 16, 6), (4, 16, 2048, 2, 2), (4, 64, 512, 2, 2))
+
+    def column_chunk(at, block):
+        cut = (slice(0, 32), slice(block * 1024, (block + 1) * 1024))
+        return (0, at, None, (("g_cols", 0, 4, cut),), "ecols", cut)
+
+    def row_chunk(at, i):
+        cut = (slice(i * 32, (i + 1) * 32), slice(0, width))
+        return (0, at, None, (("g_down", 0, 2, cut), ("g_emb", 2, 2, cut)), "erows", cut)
+
+    chunks = []
+    for i in range(2):
+        cut = (slice(0, 16), slice(i * 2048, (i + 1) * 2048))
+        chunks.append((1, i, None, (("d_cols", 0, 4, cut),), "dcols", cut))
+    for i in range(2):
+        cut = (slice(i * 64, (i + 1) * 64), slice(0, narrow))
+        sources = (("d_down", 0, 2, cut), ("g_de", 2, 1, cut), ("d_head", 3, 1, cut))
+        chunks.append((2, i, None, sources, "drows", cut))
+    chunks += [column_chunk(i, 4 + i) for i in range(4)]
+    chunks += [column_chunk(4 + i, block) for i, block in enumerate((3, 0, 1, 2))]
+    chunks += [row_chunk(8 + i, i) for i in range(8)]
+    starts = (0, 1, 3, 4, 5, 6, 7, 8, 9, 11, 12, 13) + tuple(range(14, 22))
+    begins = (0, 0, 2, 2, 3, 4, 5, 6, 7, 10, 10, 11) + tuple(range(13, 21))
+    work = tuple(chunk + (starts[i], begins[i]) for i, chunk in enumerate(chunks))
+    pieces = [(1, "head", 0)] + [(2 + s, "hidden", s) for s in range(4)] + [(6, "middle", 0)]
+    pieces += [(7 + i // 2, "attention", i) for i in range(4)]
+    pieces += [(9, "input", 0), (9, "input", 1), (10, "input", 2), (10, "first", 0)]
+    pieces += [(11 + i // 2, "embed", i) for i in range(4)]
     steps = len(work)
-    low, f32 = jnp.bfloat16, jnp.float32
-    dma = pltpu.SemaphoreType.DMA
     hbm = pl.BlockSpec(memory_space=pl.ANY)
     vm = pl.BlockSpec(memory_space=pltpu.VMEM)
-    vmem = pltpu.VMEM
-    scratch = []
-    for kind, (rows, columns, count) in enumerate(kinds):
-        half = columns // 2
-        z_first = max([1] + [w[2] for w in work if w[0] == kind])
+    vmem, sems = pltpu.VMEM, pltpu.SemaphoreType.DMA
+    scratch, landing = [], {}
+    for i, (nz, r, col, count, slots) in enumerate(kinds):
+        landing[f"land{i}"] = ((count, nz, 4, r, col), low)
+        half = col // 2
         scratch += [
-            vmem((count, 4, 4, rows, columns), low),
-            vmem((min(count, ahead + 1), 4, 4, rows, columns), low),
-            vmem((count, 2, 4, rows, half), low),
-            vmem((count, 2, 4, rows, half), low),
-            vmem((count, 4, rows, half), low),
-            vmem((count, 4, rows, half), low),
-            vmem((count, 3, rows, columns), low),
-            vmem((count, rows, columns), low),
-            vmem((z_first, 3, 4, rows, columns), low),
+            vmem((slots, nz, 4, r, col), low),
+            None,
+            vmem((2, 4, r, col), low),
+            vmem((count, 2, nz, r, half), low),
+            vmem((count, 2, nz, r, half), low),
+            vmem((count, nz, r, half), low),
+            vmem((count, nz, r, half), low),
+            vmem((count, 3, r, col), low),
+            vmem((count, r, col), low),
         ]
-    return pl.pallas_call(
-        functools.partial(reduce_kernel, len(grads), len(out_shapes), kinds, work, ahead, offsets, z_offsets, newest_last),
-        out_shape=tuple(jax.ShapeDtypeStruct(shape, low) for shape in out_shapes)
-        + (jax.ShapeDtypeStruct(small.shape, f32), jax.ShapeDtypeStruct((8, 128), f32)),
-        in_specs=[hbm] * len(grads) + [vm],
-        out_specs=tuple([hbm] * len(out_shapes) + [vm, vm]),
-        scratch_shapes=scratch
+    outs.update(landing)
+    in_names, out_names = tuple(ins), tuple(outs)
+
+    def kernel(*refs):
+        n = len(in_names) + len(out_names)
+        ref = dict(zip(in_names + out_names, refs))
+        kept = list(refs[n:])
+        for i in range(len(kinds)):
+            kept.insert(9 * i + 1, ref[f"land{i}"])
+        back_reduce_kernel(heads, kinds, work, pieces, in_names, out_names, *refs[:n], *kept)
+
+    result = pl.pallas_call(
+        kernel,
+        out_shape=tuple(jax.ShapeDtypeStruct(*outs[name]) for name in out_names),
+        in_specs=[vm if name in ("band", "gains", "small") else hbm for name in in_names],
+        out_specs=tuple(vm if name in ("small_out", "ss_out") else hbm for name in out_names),
+        scratch_shapes=[s for s in scratch if s is not None]
         + [
             vmem((10,) + small.shape, f32),
             vmem((1, 512), f32),
             vmem((10, 8, 128), f32),
-            dma((steps, 3)), dma((steps, 3)), dma((steps, 3)),
-            dma((steps, 4)), dma((steps, 4)),
-            dma((steps, 2)), dma((steps, 2)),
-            dma((steps, 3)), dma((steps, 3)),
-            dma((steps, 4)), dma((steps, 4)),
-            dma((steps,)), dma((6,)), dma((6,)), dma((6,)), dma((6,)),
+            vmem((tokens, width), f32),
+            vmem((tokens, width), f32),
+            vmem((tokens, width), f32),
+            vmem((tokens, width), low),
+            vmem((tokens, width), low),
+            vmem((tokens, 3 * width), low),
+            vmem((width, width), low),
+            vmem((width, width), low),
+            vmem((4, 256, width), low),
+            vmem((4, 2, 4, 32, width), low),
+            vmem((1, 2, 4, 128, narrow), low),
+            vmem((2,) + p.shape[1:], low),
+            vmem((2,) + inv.shape[1:], f32),
+            vmem((2,) + oo.shape[1:], f32),
+            vmem((p.shape[2], RUN), f32),
+            vmem((RUN, p.shape[2]), low),
+            vmem((8, width), f32),
+            sems((steps, 3)), sems((steps, 3)), sems((steps, 4)), sems((steps, 3)),
+            sems((steps, 4)), sems((steps, 4)),
+            sems((steps, 2)), sems((steps, 2)),
+            sems((steps, 3)), sems((steps, 3)),
+            sems((steps, 4)), sems((steps, 4)),
+            sems((steps,)), sems((6,)), sems((6,)), sems((6,)), sems((6,)), sems((13,)), sems((2, 3)),
         ],
         compiler_params=pltpu.CompilerParams(
-            collective_id=collective_id, has_side_effects=True, vmem_limit_bytes=62 * 1024 * 1024
+            collective_id=1, has_side_effects=True, vmem_limit_bytes=63 * 1024 * 1024
         ),
-    )(*grads, small)
-
-
-def reduce_gradients(
-    erows, ecols, dcols, drows, small, z_first=3, ahead=2, offsets=(0, 2, 4, 6, 8, 9),
-    z_offsets=(0, 4, 6, 8, 10, 11), newest_last=False, collective_id=1,
-):
-    grads, shapes = [], []
-
-    def add(array, z_count):
-        grads.append(array.reshape(z_count, 2, 4, array.shape[0] // (8 * z_count), array.shape[1]))
-        return len(grads) - 1
-
-    chunks = [[], [], []]
-    wide = 1024
-    tall = erows.shape[0] // 32
-    index = add(erows, 4)
-    shapes.append((4, tall, wide))
-    for k in range(tall // 32):
-        cut = (slice(k * 32, (k + 1) * 32), slice(0, wide))
-        chunks[0].append((0, ((index, 0, 4, cut),), 0, cut))
-    index = add(ecols, 4)
-    shapes.append((4, 32, ecols.shape[1]))
-    for k in range(ecols.shape[1] // wide):
-        cut = (slice(0, 32), slice(k * wide, (k + 1) * wide))
-        chunks[0].append((0, ((index, 0, 4, cut),), 1, cut))
-    index = add(dcols, 4)
-    shapes.append((4, 16, dcols.shape[1]))
-    for k in range(dcols.shape[1] // 2048):
-        cut = (slice(0, 16), slice(k * 2048, (k + 1) * 2048))
-        chunks[1].append((1, ((index, 0, 4, cut),), 2, cut))
-    rows = sum(part.shape[0] for part in drows)
-    z_rows = rows // 4
-    parts = []
-    at = 0
-    for part in drows:
-        count = part.shape[0] // z_rows
-        parts.append((add(part, count), at, count))
-        at += count
-    tall = rows // 32
-    shapes.append((4, tall, 512))
-    for k in range(tall // 64):
-        cut = (slice(k * 64, (k + 1) * 64), slice(0, 512))
-        chunks[2].append((2, tuple((i, z0, nz, cut) for i, z0, nz in parts), 3, cut))
-    numbered = [[(c[0], i) + c[1:] for i, c in enumerate(group)] for group in chunks]
-    order = numbered[1] + numbered[2] + numbered[0]
-    total = len(order)
-    marks = {}
-    if z_first:
-        spots = [i for i in range(total) if order[i][0] == 0]
-        every = max(1, len(spots) // z_first)
-        for n in range(z_first):
-            marks[spots[n * every]] = n + 1
-    work = tuple(c[:2] + (marks.get(i, 0),) + c[2:] for i, c in enumerate(order))
-    kinds = ((32, wide, len(chunks[0])), (16, 2048, len(chunks[1])), (64, 512, len(chunks[2])))
-    out = reduce_call(tuple(grads), small, kinds, work, tuple(shapes), ahead, offsets, z_offsets, newest_last, collective_id)
-    erows, ecols, dcols, drows = [o.reshape(-1, o.shape[-1]) for o in out[:4]]
-    return ecols, erows, dcols, drows, out[4], out[5]
+    )(*ins.values())
+    got = dict(zip(out_names, result))
+    shards = [got[name].reshape(-1, got[name].shape[-1]) for name in ("ecols", "erows", "dcols", "drows")]
+    return shards, got["small_out"], got["ss_out"]
 
 
 def adam_step(master, moment, square, grad, factor, fix_one, fix_two, decay, rate):
@@ -1333,37 +1510,52 @@
         DHEADS,
     )
     loss_local = loss_local[0, 0]
-    grad_erows, grad_ecols, grad_dembed, enc_sums = encoder_back_call(
-        grad_latent.reshape(batch * K, -1),
-        kept_pixels,
-        kept_bands,
-        saved,
-        whole_rows,
-        whole_cols,
-        dec_embed,
-        enc_gains,
-        HEADS,
-    )
-    grad_egains = enc_sums[:6]
+    grad_latent = grad_latent.reshape(batch * K, -1)
+    grad_dgains = dec_sums[:7]
 
     def reduce_rows(pieces, axis):
         whole = jnp.concatenate([to_low(piece) for piece in pieces], axis)
         return lax.psum_scatter(whole, "dp", scatter_dimension=0, tiled=True)
 
-    grad_dgains = dec_sums[:7]
-    drows = (grad_ddown, grad_dembed, grad_head)
     if direct:
-        flat = jnp.concatenate([grad_egains.reshape(-1), grad_dgains.reshape(-1), loss_local[None]])
-        count_e, count_d = grad_egains.size, grad_dgains.size
-        small = jnp.pad(flat, (0, 16 * D - flat.shape[0])).reshape(16, D)
-        *shards, small, squares = reduce_gradients(grad_erows, grad_ecols, grad_dcols, drows, small)
+        count_e, count_d = enc_gains.size, grad_dgains.size
+        flat = jnp.concatenate([grad_dgains.reshape(-1), loss_local[None]])
+        small = jnp.pad(flat, (count_e, 16 * D - count_e - flat.shape[0])).reshape(16, D)
+        shards, small, squares = back_reduce_call(
+            grad_latent,
+            kept_pixels,
+            kept_bands,
+            saved,
+            whole_rows,
+            whole_cols,
+            dec_embed,
+            enc_gains,
+            grad_dcols,
+            grad_ddown,
+            grad_head,
+            small,
+            HEADS,
+        )
         flat = small.reshape(-1)
-        enc_sum = flat[:count_e].reshape(grad_egains.shape)
+        enc_sum = flat[:count_e].reshape(enc_gains.shape)
         dec_sum = flat[count_e : count_e + count_d].reshape(grad_dgains.shape)
         loss_sum = flat[count_e + count_d]
         shard_squares = squares[0, 0]
         shards = tuple(piece.astype(jnp.float32) for piece in shards)
     else:
+        grad_erows, grad_ecols, grad_dembed, enc_sums = encoder_back_call(
+            grad_latent,
+            kept_pixels,
+            kept_bands,
+            saved,
+            whole_rows,
+            whole_cols,
+            dec_embed,
+            enc_gains,
+            HEADS,
+        )
+        grad_egains = enc_sums[:6]
+        drows = (grad_ddown, grad_dembed, grad_head)
         enc_sum, dec_sum, loss_sum = lax.psum((grad_egains, grad_dgains, loss_local), ("grp", "dp"))
         shards = tuple(
             lax.psum(reduce_rows(pieces, 0), "grp").astype(jnp.float32)

time: 750 us -> 711 us (0.948)
  Pallas kernels: 666 us -> 627 us
    pallas_call x2 -> x1, Pallas kernels: 319 us -> 280 us  [back_reduce_call(): pl.pallas_call(kernel, out_shape=tuple((jax.ShapeDtypeStruct(*outs[name])...]
  transfers between devices with their start and end apart: 2 -> 2, of which waited for: 0 -> 0; matrix products, arithmetic and copies ran while one was open for 2% -> 2% of each run, Pallas kernels for 28% -> 30%
where the time goes in v3:
time: 711 us; the launch traced here: 701 us
  Pallas kernels  627 us (88%)
  other arithmetic  29.9 us (4%)
  local copies, waits for them, and re-layouts  22 us (3%)
  between operations  21.9 us (3%)
    pallas_call x1, Pallas kernels, back_reduce_call(): pl.pallas_call(kernel, out_shape=tuple((jax.ShapeDtypeStruct(*outs[name])...  280 us
    pallas_call x1, Pallas kernels, gather_call(): pl.pallas_call(functools.partial(gather_kernel, count, chunks, ahead), ou...  155 us
    pallas_call x1, Pallas kernels, decoder_call(): pl.pallas_call(functools.partial(decoder_kernel, items, heads), grid=(bat...  138 us
    pallas_call x1, Pallas kernels, encoder_call(): pl.pallas_call(functools.partial(encoder_kernel, heads), grid=(12,), in_s...  53.4 us
    sub x6, other arithmetic, adam_step(): return (clipped, square_new, master - rate * direction)  17.4 us
  transfers between devices with their start and end apart: 2, of which 0 were waited for; matrix products, arithmetic and copies ran while one was open for 2% of the time, Pallas kernels for 30%

profile of v3, /device:TPU:0, one launch (start us, length us, event | category | flops | bytes accessed | tf_op | source)
XLA Modules:
  0.0 700.9 jit_solution(17478472156282748893)
XLA Ops:
  7.2 0.0 all-gather.3.cloned.1.call-start
  7.2 1.6 dynamic-slice_convert_fusion.1
  8.9 0.0 all-gather.3.cloned.1.call-update
  8.9 0.0 all-gather.5.cloned.1.call-start
  8.9 1.6 dynamic-slice_convert_fusion
  10.6 0.0 all-gather.5.cloned.1.call-update
  11.4 4.0 convert_element_type.49
  15.4 1.6 convert_element_type.50
  17.0 0.9 copy.49.keep_ref
  17.9 0.6 copy.56
  18.5 0.6 copy.57
  19.1 0.6 broadcast_in_dim.3.refs_2_
  19.7 155.5 %shard_map.392 = (bf16[4,2,4,256,1024]{4,3,2,1,0:T(8,128)(2,1)}, bf16[4,2,4,32,8192]{4,3,2,1,0:T(8,128)(2,1)}, f32[8,128]{1,0:T(8,128)}) custom-call(bf16[4,256,1024]{2,1,0:T(8,128)(2,1)} %bitcast.43, bf16[4,32,8192]{2,1,0:T(8,128)(2,1)} %bitcast.44, f32[8,128]{1,0:T(8,128)} %broadcast_in_dim.3.refs_2_), custom_call_target="tpu_custom_call" | custom-call | tf_op jit(solution)/shard_map/pallas_call | solution.py:835
  175.2 1.2 slice.31
  177.7 0.6 pad_maximum_fusion.scal_ref
  178.3 3.2 slice.42.down_ref
  181.5 1.4 fusion.38
  183.0 53.4 %shard_map.393 = (f32[512,512]{1,0:T(8,128)}, bf16[512,1024]{1,0:T(8,128)(2,1)}, s32[512,1]{1,0:T(8,128)}, f32[512,1024]{1,0:T(8,128)}, bf16[512,3072]{1,0:T(8,1...) custom-call(bf16[8,256,1024]{2,1,0:T(8,128)(2,1)} %bitcast.58, ...), custom_call_target="tpu_custom_call" | custom-call | flops 20000000000 | bytes 70000000 | tf_op jit(solution)/shard_map/pallas_call | solution.py:508
  236.4 0.0 all-gather.5.cloned.1.call-done.cols_ref
  236.5 138.2 %shard_map.394 = (bf16[8,64,512]{2,1,0:T(8,128)(2,1)}, bf16[512,4096]{1,0:T(8,128)(2,1)}, bf16[2048,512]{1,0:T(8,128)(2,1)}, bf16[1024,512]{1,0:T(8,128)(2,1)}, f32[8,512]{1,0:T(8,128)}, /*index=5*/f32[1,1]{1,0:T(1,128)}) custom-call(f32[2,8]{1,0:T(2,128)} %pad_maximum_fusion.scal_ref, f32[8,64,512]{2,1,0:T(8,128)} %bitcast.62, s32[8,64,1]{2,1,0:T(8,128)} %copy.49.keep_ref, ...), custom_call_target="tpu_custom_call" | custom-call | flops 70000001024 | bytes 40000000 | tf_op jit(solution)/shard_map/pallas_call | solution.py:332
  374.7 0.7 reshape.158
  375.4 0.7 select_maximum_fusion
  376.1 0.6 reshape.159.refs_17_
  376.7 279.8 %shard_map.395 = (bf16[4,256,1024]{2,1,0:T(8,128)(2,1)}, bf16[4,32,8192]{2,1,0:T(8,128)(2,1)}, bf16[4,16,4096]{2,1,0:T(8,128)(2,1)}, bf16[4,128,512]{2,1,0:T(8,1...) custom-call(bf16[512,512]{1,0:T(8,128)(2,1)} %bitcast.51, ...), custom_call_target="tpu_custom_call" | custom-call | tf_op jit(solution)/shard_map/pallas_call | solution.py:1374
  656.5 1.0 slice.38
  657.5 1.4 multiply_reduce_fusion
  658.9 0.9 copy.51
  659.7 0.5 slice.45
  660.9 0.6 multiply_reduce_fusion.1
  661.5 1.2 slice.36
  664.7 1.2 convert_multiply_fusion.2
  665.9 1.5 convert_multiply_fusion.3
  667.5 0.6 convert_multiply_fusion
  668.2 0.4 convert_multiply_fusion.1
  668.7 0.1 copy-done.23
  668.8 0.1 copy-done.24
  668.9 0.0 copy-done.25
  668.9 0.6 fusion.30
  669.6 0.7 fusion.25
  670.2 0.3 copy-done.13
  670.5 1.1 copy-done.15
  671.6 1.1 copy-done.16
  672.7 2.1 fusion.19
  674.8 2.1 fusion.14
  676.8 1.3 copy-done.9
  678.1 1.2 copy-done
  679.3 5.5 fusion.9
  684.8 6.5 fusion.4
  (54 shorter events, 0.2 us)
Async XLA Ops:
  7.2 171.1 %all-gather.3.cloned.1.call-start = ((), (), s32[]{:S(2)}) async-start(), calls=%async_computation | async-start | bytes 4325376 | tf_op jit(solution)/shard_map/all_gather | solution.py:1461
  8.9 227.6 %all-gather.5.cloned.1.call-start = ((), (), s32[]{:S(2)}) async-start(), calls=%async_computation.1 | async-start | bytes 4325376 | tf_op jit(solution)/shard_map/all_gather | solution.py:1461
  10.6 4.8 copy-start.1
  15.4 1.6 copy-start.28
  15.4 2.5 copy-start.26
  15.4 3.1 copy-start.27
  178.3 3.2 copy-start.7
  656.5 11.0 %copy-start.12 = (bf16[4,256,1024]{2,1,0:T(8,128)(2,1)S(1)}, bf16[4,256,1024]{2,1,0:T(8,128)(2,1)}, u32[]{:S(2)}) copy-start(bf16[4,256,1024]{2,1,0:T(8,128)(2,1)} %get-tuple-element.73) | copy-start | bytes 6291460
  665.9 4.3 copy-start.5
  665.9 2.3 copy-start.11
  667.4 7.3 %copy-start.6 = (f32[4,16,4096]{2,1,0:T(8,128)}, f32[4,16,4096]{2,1,0:T(8,128)S(1)}, u32[]{:S(2)}) copy-start(f32[4,16,4096]{2,1,0:T(8,128)S(1)} %convert_multiply_fusion.3) | copy-start | bytes 3145732
  668.1 8.8 %copy-start.3 = (f32[4,256,1024]{2,1,0:T(8,128)}, f32[4,256,1024]{2,1,0:T(8,128)S(1)}, u32[]{:S(2)}) copy-start(f32[4,256,1024]{2,1,0:T(8,128)S(1)} %convert_multiply_fusion) | copy-start | bytes 12582916
  668.1 0.7 copy-start.23
  668.1 0.8 copy-start.24
  668.1 0.8 copy-start.25
  668.1 1.5 copy-start.19
  668.1 1.4 copy-start.20
  668.1 1.4 copy-start.21
  668.1 1.4 copy-start.22
  668.2 2.4 copy-start.13
  668.2 3.4 copy-start.15
  668.2 4.5 copy-start.16
  668.2 6.5 copy-start.14
  668.2 6.5 copy-start.17
  668.2 6.5 copy-start.18
  668.7 16.1 %copy-start.4 = (f32[4,32,8192]{2,1,0:T(8,128)}, f32[4,32,8192]{2,1,0:T(8,128)S(1)}, u32[]{:S(2)}) copy-start(f32[4,32,8192]{2,1,0:T(8,128)S(1)} %convert_multiply_fusion.1) | copy-start | bytes 12582916
  672.7 4.2 copy-start.8
  672.7 5.4 copy-start.9
  674.7 4.6 copy-start
  679.3 5.5 copy-start.2
  679.3 5.5 copy-start.10
Sparse Core Ops, SparseCore 0:
  11.5 83.5 all-gather.2
  98.5 79.5 all-gather.4

commit v4 on v3

--- a/solution.py
+++ b/solution.py
@@ -304,17 +304,20 @@
         ghead_out[...] = ghead[...].astype(low)
 
 
-def decoder_call(scal, latent, keep, gsd, table, pixels, cols, down, head, gains, heads):
+def decoder_call(scal, latent, keep, gsd, table, pixels, cols, rows, gains, heads):
     batch, tokens, pixel_count = pixels.shape
     width = cols.shape[0]
+    down = jax.ShapeDtypeStruct((cols.shape[1] - 4 * width, width), rows.dtype)
+    head = jax.ShapeDtypeStruct((pixel_count, width), rows.dtype)
+    last = rows.shape[0] // pixel_count - 1
     items = 2
-    rows = items * tokens
+    run = items * tokens
     hide = tokens - K
     low = jnp.bfloat16
     full = pl.Buffered(1)
 
     def whole(array):
-        return pl.BlockSpec(array.shape, lambda s: (0,) * array.ndim, pipeline_mode=full)
+        return pl.BlockSpec(array.shape, lambda s: (0,) * len(array.shape), pipeline_mode=full)
 
     def by_item(shape):
         return pl.BlockSpec((items,) + shape, lambda s: (s, 0, 0))
@@ -341,27 +344,27 @@
             by_item((tokens, pixel_count)),
             whole(cols),
             whole(down),
-            whole(head),
+            pl.BlockSpec(head.shape, lambda s: (last, 0), pipeline_mode=full),
             whole(gains),
         ],
         out_specs=(by_item((K, width)),) + tuple(whole(out) for out in outs[1:]),
         out_shape=outs,
         scratch_shapes=[
-            vmem((rows, width), f32),
-            vmem((rows, width), low),
-            vmem((rows, 3 * width), low),
+            vmem((run, width), f32),
+            vmem((run, width), low),
+            vmem((run, 3 * width), low),
             vmem((items * width // 128, tokens, 4 * tokens), low),
-            vmem((rows, width), low),
-            vmem((rows, width), f32),
-            vmem((rows, width), low),
-            vmem((rows, down.shape[0]), low),
-            vmem((rows, down.shape[0]), low),
-            vmem((rows, width), f32),
-            vmem((rows, width), low),
-            vmem((rows, width), f32),
-            vmem((rows, width), low),
-            vmem((rows, width), f32),
-            vmem((rows, 3 * width), low),
+            vmem((run, width), low),
+            vmem((run, width), f32),
+            vmem((run, width), low),
+            vmem((run, down.shape[0]), low),
+            vmem((run, down.shape[0]), low),
+            vmem((run, width), f32),
+            vmem((run, width), low),
+            vmem((run, width), f32),
+            vmem((run, width), low),
+            vmem((run, width), f32),
+            vmem((run, 3 * width), low),
             vmem((items * width // 128, tokens, 128), f32),
             vmem((items * width // 128, tokens, 128), f32),
             vmem((4 * tokens, tokens), f32),
@@ -379,7 +382,211 @@
         cost_estimate=pl.CostEstimate(
             flops=70_000_000_000, bytes_accessed=40_000_000, transcendentals=20_000_000
         ),
-    )(scal, latent, keep, gsd, table, pixels, cols, down, head, gains)
+    )(scal, latent, keep, gsd, table, pixels, cols, rows, rows, gains)
+
+
+MESH_ID = pl.DeviceIdType.MESH
+
+
+def place():
+    g = lax.axis_index("grp")
+    d = lax.axis_index("dp")
+    z, c = d // 2, d % 2
+    xn = g + 1 - 2 * (g % 2)
+    yn = (g + 2) % 4
+    return g, z, c, xn, yn
+
+
+def pieces(shape, parts):
+    rows, columns = shape
+    if rows // parts >= 32:
+        n = rows // parts
+        cut = [(slice(i * n, (i + 1) * n), slice(0, columns)) for i in range(parts)]
+    else:
+        n = columns // parts
+        cut = [(slice(0, rows), slice(i * n, (i + 1) * n)) for i in range(parts)]
+    return cut
+
+
+def halves(cut):
+    rows, columns = cut
+    mid = (columns.start + columns.stop) // 2
+    return (rows, slice(columns.start, mid)), (rows, slice(mid, columns.stop))
+
+
+def greet(peers):
+    barrier = pltpu.get_barrier_semaphore()
+    for peer in peers:
+        pl.semaphore_signal(barrier, inc=1, device_id=peer, device_id_type=MESH_ID)
+    pl.semaphore_wait(barrier, len(peers))
+
+
+GATHER_SEMS = 14
+
+
+def gather_events(count, chunks, ahead, ins, outs, sems):
+    zs, zr, xs, xr, ys, yr, fs, fr, gs, gr, cs, os, cr, ls = sems
+    g, z, c, xn, yn = place()
+    dg = (xn + 2) % 4
+    here = 2 * z + c
+    other = 1 - c
+    sib = (g, 2 * z + 1 - c)
+    right, up = (xn, here), (yn, here)
+    zpeer = [(g, 2 * ((z + j) % 4) + c) for j in (1, 2, 3)]
+    zfrom = [(z + 4 - j) % 4 for j in (1, 2, 3)]
+    peers = [sib, right, up] + zpeer
+    work = []
+    for array in range(count):
+        for cut in pieces(ins[array].shape[1:], chunks[array]):
+            work.append((array, cut))
+    steps = len(work)
+    sent = []
+
+    def send(src, dst, send_sem, recv_sem, peer):
+        return pltpu.make_async_remote_copy(
+            src_ref=src, dst_ref=dst, send_sem=send_sem, recv_sem=recv_sem,
+            device_id=peer, device_id_type=MESH_ID,
+        )
+
+    def go(make):
+        make().start()
+        sent.append(make)
+
+    def block(array, z_at, q, cut):
+        return outs[array].at[z_at, c, q, cut[0], cut[1]]
+
+    def zcopy(k, j):
+        array, cut = work[k]
+        return send(
+            ins[array].at[g, cut[0], cut[1]], block(array, z, g, cut), zs.at[k, j], zr.at[k, j], zpeer[j]
+        )
+
+    def relay(k, j, q, cut, ssem, rsem, peer):
+        at = block(work[k][0], zfrom[j], q, cut)
+        return send(at, at, ssem, rsem, peer)
+
+    def to_x(k, j):
+        return relay(k, j, g, work[k][1], xs.at[k, j], xr.at[k, j], right)
+
+    def to_y(k, j):
+        return relay(k, j, g, work[k][1], ys.at[k, j], yr.at[k, j], up)
+
+    def to_core(k, j, i, q):
+        return relay(k, j, q, work[k][1], cs.at[k, j, i], cr.at[work[k][0]], sib)
+
+    def on_y(k, j, q):
+        return relay(k, j, q, halves(work[k][1])[0], fs.at[k, j], fr.at[k, j], up)
+
+    def on_x(k, j, q):
+        return relay(k, j, q, halves(work[k][1])[1], gs.at[k, j], gr.at[k, j], right)
+
+    def own(array):
+        return pltpu.make_async_copy(ins[array], outs[array].at[z, c], ls.at[array])
+
+    def own_to_core(array):
+        return send(ins[array], outs[array].at[z, c], os.at[array], cr.at[array], sib)
+
+    def begin():
+        for array in range(count):
+            own(array).start()
+        for k in range(min(ahead, steps)):
+            for j in range(3):
+                go(functools.partial(zcopy, k, j))
+        for array in range(count):
+            go(functools.partial(own_to_core, array))
+
+    def event(t):
+        if t < steps:
+            for j in range(3):
+                zcopy(t, j).wait_recv()
+                go(functools.partial(to_x, t, j))
+                go(functools.partial(to_y, t, j))
+                go(functools.partial(to_core, t, j, 0, g))
+            if t + ahead < steps:
+                for j in range(3):
+                    go(functools.partial(zcopy, t + ahead, j))
+        if 1 <= t <= steps:
+            k = t - 1
+            for j in range(3):
+                relay(k, j, xn, work[k][1], xs.at[k, j], xr.at[k, j], right).wait_recv()
+                go(functools.partial(on_y, k, j, xn))
+                go(functools.partial(to_core, k, j, 1, xn))
+                relay(k, j, yn, work[k][1], ys.at[k, j], yr.at[k, j], up).wait_recv()
+                go(functools.partial(on_x, k, j, yn))
+                go(functools.partial(to_core, k, j, 2, yn))
+        if 2 <= t:
+            k = t - 2
+            for j in range(3):
+                on_y(k, j, dg).wait_recv()
+                on_x(k, j, dg).wait_recv()
+                go(functools.partial(to_core, k, j, 3, dg))
+
+    def finish():
+        for make in sent:
+            make().wait_send()
+        for array in range(count):
+            whole = outs[array].at[:, other]
+            send(whole, whole, os.at[array], cr.at[array], sib).wait_recv()
+            own(array).wait()
+
+    return peers, begin, [functools.partial(event, t) for t in range(steps + 2)], finish
+
+
+def gather_scratch(count, steps):
+    dma = pltpu.SemaphoreType.DMA
+    return [dma((steps, 3))] * 10 + [dma((steps, 3, 4)), dma((count,)), dma((count,)), dma((count,))]
+
+
+def gather_kernel(count, chunks, ahead, *refs):
+    ins, items_ref = refs[:count], refs[count]
+    outs, items_out = refs[count + 1 : 2 * count + 1], refs[2 * count + 1]
+    sems = refs[2 * count + 2 :]
+    it, its, itr = sems[GATHER_SEMS:]
+    peers, begin, events, finish = gather_events(count, chunks, ahead, ins, outs, sems[:GATHER_SEMS])
+    greet(peers)
+    _, right, up = peers[:3]
+
+    def items_copy(i, peer):
+        return pltpu.make_async_remote_copy(
+            src_ref=it.at[2 * i], dst_ref=it.at[2 * i + 1], send_sem=its.at[i], recv_sem=itr.at[i],
+            device_id=peer, device_id_type=MESH_ID,
+        )
+
+    it[0] = items_ref[...]
+    items_copy(0, right).start()
+    begin()
+    for t, event in enumerate(events):
+        event()
+        if t == 0:
+            items_copy(0, right).wait_recv()
+            it[2] = it[0] + it[1]
+            items_copy(1, up).start()
+        if t == 1:
+            items_copy(1, up).wait_recv()
+            items_out[...] = it[2] + it[3]
+    finish()
+    items_copy(0, right).wait_send()
+    items_copy(1, up).wait_send()
+
+
+def gather_call(shards, items, chunks, ahead=2, collective_id=0):
+    count = len(shards)
+    steps = sum(chunks)
+    views = [s.reshape(4, s.shape[0] // 4, s.shape[1]) for s in shards]
+    dma = pltpu.SemaphoreType.DMA
+    hbm = pl.BlockSpec(memory_space=pl.ANY)
+    vm = pl.BlockSpec(memory_space=pltpu.VMEM)
+    *outs, total = pl.pallas_call(
+        functools.partial(gather_kernel, count, chunks, ahead),
+        out_shape=tuple(jax.ShapeDtypeStruct((4, 2) + v.shape, v.dtype) for v in views)
+        + (jax.ShapeDtypeStruct((8, 128), jnp.float32),),
+        in_specs=[hbm] * count + [vm],
+        out_specs=tuple([hbm] * count + [vm]),
+        scratch_shapes=gather_scratch(count, steps)
+        + [pltpu.VMEM((4, 8, 128), jnp.float32), dma((2,)), dma((2,))],
+        compiler_params=pltpu.CompilerParams(collective_id=collective_id, has_side_effects=True),
+    )(*views, jnp.broadcast_to(items, (8, 128)))
+    return [o.reshape(-1, o.shape[-1]) for o in outs], total[0, 0]
 
 
 RUN = 256
@@ -391,20 +598,52 @@
     return row == column
 
 
-def encoder_kernel(
-    heads, pixels_ref, keep_ref, bands_ref, gsd_ref, table_ref, rows_ref, cols_ref, de_ref, gains_ref,
-    z_ref, pix_ref, band_ref, x_ref, qkv_ref, p_ref, inv_ref, oo_ref, x1_ref, a_ref, gp_ref, x2_ref, o_s,
-    h_s, s_s, high_s, low_s,
-):
+def encoder_kernel(heads, chunks, *refs):
+    count = 2 if chunks else 0
+    (pixels_ref, keep_ref, bands_ref, gsd_ref, table_ref, rows_ref, cols_ref, de_ref, gains_ref) = refs[:9]
+    shards = refs[9 : 9 + count]
+    outs = refs[9 + count :]
+    z_ref, band_ref, a_ref, gp_ref, x2_ref = outs[:5]
+    stored = outs[5:13]
+    gathered = outs[13 : 13 + count]
+    rest = outs[13 + count :]
+    pix_ref, x_ref, qkv_ref, p_ref, inv_ref, oo_ref, x1_ref, o_s = rest[:8]
+    h_s, s_s, high_s, low_s, de_s, store_sem, de_sem = rest[8:15]
     low = jnp.bfloat16
     step = pl.program_id(0)
     width = x_ref.shape[1]
     ee = width // heads
     groups = width // LANES
     expo = ee ** (-0.5) * 1.4426950408889634
+    if chunks:
+        peers, begin, events, finish = gather_events(
+            count, chunks, 2, shards, gathered, rest[15 : 15 + GATHER_SEMS]
+        )
 
     def gain(i):
         return gains_ref[i : i + 1, :]
+
+    def store(i):
+        return pltpu.make_async_copy(rest[i], stored[i], store_sem.at[i])
+
+    def load_de():
+        return pltpu.make_async_copy(gathered[1].at[2] if chunks else de_ref, de_s, de_sem)
+
+    if chunks:
+
+        @pl.when(step == 0)
+        def _():
+            greet(peers)
+            begin()
+
+        for at, event in zip((3, 6, 7, 8, 9, 10), events):
+            pl.when(step == at)(event)
+
+    @pl.when(step == 11)
+    def _():
+        if chunks:
+            finish()
+        load_de().start()
 
     @pl.when(step == 0)
     def _():
@@ -418,6 +657,8 @@
             band_ref[at, :] = jnp.sum(hot * bands_ref[i], -1, keepdims=True).astype(jnp.int32)
             x_ref[at, :] = look_up(hot, gsd_ref[i], high_s, low_s)
 
+        store(0).start()
+
     @pl.when(step < 4)
     def _():
         pixel = pix_ref[...]
@@ -425,6 +666,7 @@
 
     @pl.when(step == 4)
     def _():
+        store(1).start()
         hat, _ = unit_rows(x_ref[...])
         h_s[...] = (hat * gain(0) + gain(1)).astype(low)
 
@@ -435,13 +677,17 @@
 
     @pl.when(step == 7)
     def _():
+        store(2).start()
         same = same_item()
 
         @pl.loop(0, x_ref.shape[0] // RUN * groups)
         def _(n):
             attend(n, groups, RUN, width, ee, expo, same, qkv_ref, s_s, p_ref, inv_ref, oo_ref, o_s)
 
+        for i in (3, 4, 5, 7):
+            store(i).start()
         x1_ref[...] = x_ref[...] + dot_nn(o_s[...], cols_ref[...])
+        store(6).start()
         hat, _ = unit_rows(x1_ref[...])
         h_s[...] = (hat * gain(2) + gain(3)).astype(low)
         x2_ref[...] = x1_ref[...]
@@ -463,16 +709,28 @@
     def _():
         hat, _ = unit_rows(x2_ref[...])
         h_s[...] = (hat * gain(4) + gain(5)).astype(low)
-        z_ref[...] = dot_nn(h_s[...], de_ref[...])
-
-
-def encoder_call(pixels, keep, bands, gsd, table, rows, cols, de, gains, heads):
+        load_de().wait()
+        z_ref[...] = dot_nn(h_s[...], de_s[...].reshape(width, z_ref.shape[1]))
+        for i in range(8):
+            store(i).wait()
+
+
+def encoder_call(pixels, keep, bands, gsd, table, rows, cols, de, gains, heads, shards=()):
     width = cols.shape[0]
     tokens = keep.shape[0] * K
     low, f32 = jnp.bfloat16, jnp.float32
     runs = tokens // RUN * (width // LANES)
     wide = LANES // (width // heads) * RUN
     one = pl.Buffered(1)
+    hbm = pl.BlockSpec(memory_space=pl.ANY)
+    vmem = pltpu.VMEM
+    chunks = (2, 2) if shards else ()
+    views = [s.reshape(4, s.shape[0] // 4, s.shape[1]) for s in shards]
+    if shards:
+        narrow = shards[1].shape[1]
+        de, de_shape = jnp.zeros((8, 128), low), (2, 4, 128, narrow)
+    else:
+        narrow, de_shape = de.shape[1], de.shape
 
     def whole(shape):
         return pl.BlockSpec(shape, lambda s: (0,) * len(shape), pipeline_mode=one)
@@ -486,27 +744,27 @@
     def hidden_block(s):
         return (0, jnp.where(s < 8, 0, s - 8))
 
-    def hold(shape, dtype=f32):
-        return jax.ShapeDtypeStruct(shape, dtype), whole(shape)
-
-    ff = (tokens, 4 * width)
-    outs = [
-        hold((tokens, de.shape[1])),
-        hold((tokens, pixels.shape[2]), low),
-        hold((tokens, 1), jnp.int32),
-        hold((tokens, width)),
-        hold((tokens, 3 * width), low),
-        hold((runs, RUN, wide), low),
-        hold((runs, RUN, LANES)),
-        hold((runs, RUN, LANES)),
-        hold((tokens, width)),
-        (jax.ShapeDtypeStruct(ff, low), pl.BlockSpec((tokens, width), hidden_block)),
-        (jax.ShapeDtypeStruct(ff, low), pl.BlockSpec((tokens, width), hidden_block)),
-        hold((tokens, width)),
-        hold((tokens, width), low),
+    hidden = pl.BlockSpec((tokens, width), hidden_block)
+    blocks = [
+        ((tokens, narrow), f32, whole((tokens, narrow))),
+        ((tokens, 1), jnp.int32, whole((tokens, 1))),
+        ((tokens, 4 * width), low, hidden),
+        ((tokens, 4 * width), low, hidden),
+        ((tokens, width), f32, whole((tokens, width))),
     ]
-    return pl.pallas_call(
-        functools.partial(encoder_kernel, heads),
+    held = [
+        ((tokens, pixels.shape[2]), low),
+        ((tokens, width), f32),
+        ((tokens, 3 * width), low),
+        ((runs, RUN, wide), low),
+        ((runs, RUN, LANES), f32),
+        ((runs, RUN, LANES), f32),
+        ((tokens, width), f32),
+        ((tokens, width), low),
+    ]
+    struct = jax.ShapeDtypeStruct
+    out = pl.pallas_call(
+        functools.partial(encoder_kernel, heads, chunks),
         grid=(12,),
         in_specs=[
             whole(pixels.shape),
@@ -516,24 +774,39 @@
             pl.BlockSpec((table.shape[0], width), lambda s: (0, 0), pipeline_mode=one),
             pl.BlockSpec((width, width), row_block),
             pl.BlockSpec((width, width), column_block),
-            whole(de.shape),
+            hbm,
             whole(gains.shape),
-        ],
-        out_specs=tuple(o[1] for o in outs),
-        out_shape=tuple(o[0] for o in outs),
-        scratch_shapes=[
-            pltpu.VMEM((tokens, width), low),
-            pltpu.VMEM((wide, RUN), f32),
-            pltpu.VMEM((table.shape[0], width), low),
-            pltpu.VMEM((table.shape[0], width), low),
-        ],
+        ]
+        + [hbm] * len(views),
+        out_specs=tuple(b[2] for b in blocks) + (hbm,) * (len(held) + len(views)),
+        out_shape=tuple(struct(b[0], b[1]) for b in blocks)
+        + tuple(struct(*h) for h in held)
+        + tuple(struct((4, 2) + v.shape, low) for v in views),
+        scratch_shapes=[vmem(*h) for h in held]
+        + [
+            vmem((tokens, width), low),
+            vmem((wide, RUN), f32),
+            vmem((table.shape[0], width), low),
+            vmem((table.shape[0], width), low),
+            vmem(de_shape, low),
+            pltpu.SemaphoreType.DMA((8,)),
+            pltpu.SemaphoreType.DMA,
+        ]
+        + (gather_scratch(2, sum(chunks)) if shards else []),
         compiler_params=pltpu.CompilerParams(
-            dimension_semantics=("arbitrary",), vmem_limit_bytes=60 * 1024 * 1024
+            dimension_semantics=("arbitrary",),
+            vmem_limit_bytes=60 * 1024 * 1024,
+            collective_id=2 if shards else None,
+            has_side_effects=bool(shards),
         ),
         cost_estimate=pl.CostEstimate(
             flops=20_000_000_000, bytes_accessed=70_000_000, transcendentals=8_000_000
         ),
-    )(pixels, keep, bands, gsd, table, rows, cols, de, gains)
+    )(pixels, keep, bands, gsd, table, rows, cols, de, gains, *views)
+    z, band, a, gp, x2 = out[:5]
+    pix, x, qkv, p, inv, oo, x1, o = out[5:13]
+    saved = (x, qkv, p, inv, oo, x1, a, gp, x2, o)
+    return z, pix, band, saved, [w.reshape(-1, w.shape[-1]) for w in out[13:]]
 
 
 def encoder_back_kernel(
@@ -686,166 +959,6 @@
     )(dz, pixel, band, x, qkv, p, inv, oo, x1, a, gp, x2, rows, cols, de, gains)
 
 
-MESH_ID = pl.DeviceIdType.MESH
-
-
-def place():
-    g = lax.axis_index("grp")
-    d = lax.axis_index("dp")
-    z, c = d // 2, d % 2
-    xn = g + 1 - 2 * (g % 2)
-    yn = (g + 2) % 4
-    return g, z, c, xn, yn
-
-
-def pieces(shape, parts):
-    rows, columns = shape
-    if rows // parts >= 32:
-        n = rows // parts
-        cut = [(slice(i * n, (i + 1) * n), slice(0, columns)) for i in range(parts)]
-    else:
-        n = columns // parts
-        cut = [(slice(0, rows), slice(i * n, (i + 1) * n)) for i in range(parts)]
-    return cut
-
-
-def halves(cut):
-    rows, columns = cut
-    mid = (columns.start + columns.stop) // 2
-    return (rows, slice(columns.start, mid)), (rows, slice(mid, columns.stop))
-
-
-def greet(peers):
-    barrier = pltpu.get_barrier_semaphore()
-    for peer in peers:
-        pl.semaphore_signal(barrier, inc=1, device_id=peer, device_id_type=MESH_ID)
-    pl.semaphore_wait(barrier, len(peers))
-
-
-def gather_kernel(count, chunks, ahead, *refs):
-    ins, items_ref = refs[:count], refs[count]
-    outs, items_out = refs[count + 1 : 2 * count + 1], refs[2 * count + 1]
-    (zs, zr, xs, xr, ys, yr, fs, fr, gs, gr, cs, os, cr, ls, it, its, itr) = refs[2 * count + 2 :]
-    g, z, c, xn, yn = place()
-    dg = (xn + 2) % 4
-    here = 2 * z + c
-    sib = (g, 2 * z + 1 - c)
-    zpeer = [(g, 2 * ((z + j) % 4) + c) for j in (1, 2, 3)]
-    zfrom = [(z + 4 - j) % 4 for j in (1, 2, 3)]
-    greet([sib, (xn, here), (yn, here)] + zpeer)
-
-    def send(src, dst, send_sem, recv_sem, peer):
-        return pltpu.make_async_remote_copy(
-            src_ref=src, dst_ref=dst, send_sem=send_sem, recv_sem=recv_sem,
-            device_id=peer, device_id_type=MESH_ID,
-        )
-
-    def block(array, z_at, q, cut, core=None):
-        return outs[array].at[z_at, c if core is None else core, q, cut[0], cut[1]]
-
-    work = []
-    for array in range(count):
-        for cut in pieces(ins[array].shape[1:], chunks[array]):
-            work.append((array, cut))
-    steps = len(work)
-    sent = []
-
-    def go(copy):
-        copy.start()
-        sent.append(copy)
-
-    def items_copy(i, peer):
-        return send(it.at[2 * i], it.at[2 * i + 1], its.at[i], itr.at[i], peer)
-
-    def zcopy(k, j):
-        array, cut = work[k]
-        return send(
-            ins[array].at[g, cut[0], cut[1]], block(array, z, g, cut), zs.at[k, j], zr.at[k, j], zpeer[j]
-        )
-
-    def relay(k, j, q, cut, ssem, rsem, peer):
-        at = block(work[k][0], zfrom[j], q, cut)
-        return send(at, at, ssem, rsem, peer)
-
-    it[0] = items_ref[...]
-    go(items_copy(0, (xn, here)))
-    local = []
-    for array in range(count):
-        copy = pltpu.make_async_copy(ins[array], outs[array].at[z, c], ls.at[array])
-        copy.start()
-        local.append(copy)
-    for k in range(min(ahead, steps)):
-        for j in range(3):
-            go(zcopy(k, j))
-    for array in range(count):
-        go(send(ins[array], outs[array].at[z, c], os.at[array], cr.at[array], sib))
-
-    for t in range(steps + 2):
-        if t < steps:
-            array, cut = work[t]
-            for j in range(3):
-                zcopy(t, j).wait_recv()
-                go(relay(t, j, g, cut, xs.at[t, j], xr.at[t, j], (xn, here)))
-                go(relay(t, j, g, cut, ys.at[t, j], yr.at[t, j], (yn, here)))
-                go(relay(t, j, g, cut, cs.at[t, j, 0], cr.at[array], sib))
-            if t + ahead < steps:
-                for j in range(3):
-                    go(zcopy(t + ahead, j))
-        if t == 0:
-            items_copy(0, (xn, here)).wait_recv()
-            it[2] = it[0] + it[1]
-            go(items_copy(1, (yn, here)))
-        if t == 1:
-            items_copy(1, (yn, here)).wait_recv()
-            items_out[...] = it[2] + it[3]
-        if 1 <= t <= steps:
-            k = t - 1
-            array, cut = work[k]
-            left, right = halves(cut)
-            for j in range(3):
-                relay(k, j, xn, cut, xs.at[k, j], xr.at[k, j], (xn, here)).wait_recv()
-                go(relay(k, j, xn, left, fs.at[k, j], fr.at[k, j], (yn, here)))
-                go(relay(k, j, xn, cut, cs.at[k, j, 1], cr.at[array], sib))
-                relay(k, j, yn, cut, ys.at[k, j], yr.at[k, j], (yn, here)).wait_recv()
-                go(relay(k, j, yn, right, gs.at[k, j], gr.at[k, j], (xn, here)))
-                go(relay(k, j, yn, cut, cs.at[k, j, 2], cr.at[array], sib))
-        if 2 <= t:
-            k = t - 2
-            array, cut = work[k]
-            left, right = halves(cut)
-            for j in range(3):
-                relay(k, j, dg, left, fs.at[k, j], fr.at[k, j], (yn, here)).wait_recv()
-                relay(k, j, dg, right, gs.at[k, j], gr.at[k, j], (xn, here)).wait_recv()
-                go(relay(k, j, dg, cut, cs.at[k, j, 3], cr.at[array], sib))
-    for copy in sent:
-        copy.wait_send()
-    for array in range(count):
-        whole = outs[array].at[:, 1 - c]
-        send(whole, whole, os.at[array], cr.at[array], sib).wait_recv()
-        local[array].wait()
-
-
-def gather_call(shards, items, chunks, ahead=2, collective_id=0):
-    count = len(shards)
-    steps = sum(chunks)
-    views = [s.reshape(4, s.shape[0] // 4, s.shape[1]) for s in shards]
-    dma = pltpu.SemaphoreType.DMA
-    hbm = pl.BlockSpec(memory_space=pl.ANY)
-    vm = pl.BlockSpec(memory_space=pltpu.VMEM)
-    *outs, total = pl.pallas_call(
-        functools.partial(gather_kernel, count, chunks, ahead),
-        out_shape=tuple(jax.ShapeDtypeStruct((4, 2) + v.shape, v.dtype) for v in views)
-        + (jax.ShapeDtypeStruct((8, 128), jnp.float32),),
-        in_specs=[hbm] * count + [vm],
-        out_specs=tuple([hbm] * count + [vm]),
-        scratch_shapes=[dma((steps, 3))] * 10
-        + [dma((steps, 3, 4)), dma((count,)), dma((count,)), dma((count,))]
-        + [pltpu.VMEM((4, 8, 128), jnp.float32), dma((2,)), dma((2,))],
-        compiler_params=pltpu.CompilerParams(collective_id=collective_id, has_side_effects=True),
-    )(*views, jnp.broadcast_to(items, (8, 128)))
-    return [o.reshape(-1, o.shape[-1]) for o in outs], total[0, 0]
-
-
 def back_reduce_kernel(heads, kinds, work, pieces, refs_in, refs_out, *refs):
     low, f32 = jnp.bfloat16, jnp.float32
     ref = dict(zip(refs_in + refs_out, refs))
@@ -1148,7 +1261,7 @@
     def first_loads():
         move("x", ref["x2"], xin)
         move("dz", ref["dz"], wide.at[:, pl.ds(2 * width, narrow)])
-        move("de", ref["de"], wt.at[:, pl.ds(0, narrow)])
+        move("de", ref["dec_rows"].at[pl.ds(2 * width, width)], wt.at[:, pl.ds(0, narrow)])
         move("a", ref["a"].at[:, tile(0)], wide.at[:, tile(0)])
         move("gp", ref["gp"].at[:, tile(0)], wide.at[:, tile(1)])
         load_columns(4)
@@ -1294,14 +1407,14 @@
         guarded(mine(k), keep_copy(k).wait)
 
 
-def back_reduce_call(dz, pix, band, saved, rows, cols, de, gains, dcols, ddown, dhead, small, heads):
+def back_reduce_call(dz, pix, band, saved, rows, cols, dec_rows, gains, dcols, ddown, dhead, small, heads):
     x, qkv, p, inv, oo, x1, a, gp, x2, o = saved
     tokens, width = x.shape
     low, f32 = jnp.bfloat16, jnp.float32
-    narrow = de.shape[1]
+    narrow = dec_rows.shape[1]
     ins = dict(
         dz=dz, pix=pix, band=band, x=x, x1=x1, x2=x2, qkv=qkv, p=p, inv=inv, oo=oo, o=o, a=a, gp=gp,
-        rows=rows, cols=cols, de=de, gains=gains, small=small,
+        rows=rows, cols=cols, dec_rows=dec_rows, gains=gains, small=small,
         d_cols=dcols.reshape(4, 2, 4, 16, dcols.shape[1]),
         d_down=ddown.reshape(2, 2, 4, 128, narrow),
         d_head=dhead.reshape(1, 2, 4, 128, narrow),
@@ -1422,6 +1535,88 @@
     return (clipped, square_new, master - rate * direction)
 
 
+def adam_kernel(count_e, count_d, *refs):
+    scal_ref, small_ref, ss_ref = refs[:3]
+    ins, outs = refs[3:25], refs[25:]
+    small = small_ref[...]
+    width = small.shape[1]
+    flat = lax.broadcasted_iota(jnp.int32, small.shape, 0) * width + lax.broadcasted_iota(
+        jnp.int32, small.shape, 1
+    )
+    gains = jnp.where(flat < count_e + count_d, small, 0.0)
+    norm = jnp.sqrt(ss_ref[0:1, 0:1] + jnp.sum(gains * gains, keepdims=True).reshape(1, 1))
+    factor = clip_level / jnp.maximum(norm, clip_level)
+    masked, fix_one, fix_two = scal_ref[0, 0], scal_ref[0, 1], scal_ref[0, 2]
+
+    def update(grad, master, moment, square, decay, rate):
+        return adam_step(master, moment, square, grad, factor, fix_one, fix_two, decay, rate)
+
+    for i in range(4):
+        grad, master, moment, square = ins[4 * i : 4 * i + 4]
+        got = update(
+            grad[...].astype(jnp.float32), master[...], moment[...], square[...], weight_decay, learn_rate
+        )
+        for target, value in zip(outs[3 * i : 3 * i + 3], got):
+            target[...] = value
+
+    @pl.when(pl.program_id(0) == 0)
+    def _():
+        at = 0
+        for i in range(2):
+            master, moment, square = ins[16 + 3 * i : 19 + 3 * i]
+            rows, columns = master.shape
+            for r in range(rows):
+                row, lane = at // width, at % width
+                grad = small[row : row + 1, lane : lane + columns]
+                one = slice(r, r + 1)
+                got = update(grad, master[one, :], moment[one, :], square[one, :], 0.0, gain_rate)
+                for target, value in zip(outs[12 + 3 * i : 15 + 3 * i], got):
+                    target[one, :] = value
+                at += columns
+        outs[18][...] = small[at // width : at // width + 1, at % width : at % width + 1] / masked
+        outs[19][...] = norm
+
+
+def adam_call(scal, small, squares, matrices, gains):
+    steps = 4
+
+    def block(array):
+        rows, columns = array.shape
+        if rows // steps % 16 == 0:
+            return pl.BlockSpec((rows // steps, columns), lambda s: (s, 0))
+        return pl.BlockSpec((rows, columns // steps), lambda s: (0, s))
+
+    def whole(array):
+        return pl.BlockSpec(array.shape, lambda s: (0, 0))
+
+    struct = jax.ShapeDtypeStruct
+    f32 = jnp.float32
+    ins, in_specs, outs, out_specs = [], [], [], []
+    for group in matrices:
+        ins += group
+        in_specs += [block(array) for array in group]
+        outs += [struct(group[1].shape, f32)] * 3
+        out_specs += [block(group[1])] * 3
+    for group in gains:
+        ins += group
+        in_specs += [whole(array) for array in group]
+        outs += [struct(group[0].shape, f32)] * 3
+        out_specs += [whole(group[0])] * 3
+    outs += [struct((1, 1), f32)] * 2
+    out_specs += [pl.BlockSpec((1, 1), lambda s: (0, 0))] * 2
+    out = pl.pallas_call(
+        functools.partial(adam_kernel, gains[0][0].size, gains[1][0].size),
+        grid=(steps,),
+        in_specs=[pl.BlockSpec(memory_space=pltpu.SMEM), whole(small), whole(squares)] + in_specs,
+        out_specs=tuple(out_specs),
+        out_shape=tuple(outs),
+        compiler_params=pltpu.CompilerParams(
+            dimension_semantics=("arbitrary",), vmem_limit_bytes=56 * 1024 * 1024
+        ),
+    )(scal, small, squares, *ins)
+    return tuple(out[:18]) + (out[18][0, 0], out[19][0, 0])
+
+
 def body(
     pixels,
     keep_index,
@@ -1470,17 +1665,20 @@
         total_count = lax.psum(own_count, "grp")
         whole_rows, whole_cols = gather_rows(enc_rows), gather_rows(enc_cols)
     masked = total_count * (L - K)
-    copies = (whole_cols, whole_rows, gather_rows(dec_cols), gather_rows(dec_rows))
-    dec_copy = copies[2]
-    dec_down = copies[3][:DFF]
-    dec_embed = copies[3][DFF : DFF + D]
-    head_rows = copies[3][DFF + D :]
+    count_steps = step_count[0].astype(jnp.float32)
+    fix_one = 1.0 - beta_first**count_steps
+    fix_two = 1.0 - beta_second**count_steps
     keep_rows = keep_index[0]
     batch = keep_rows.shape[0]
     keep_column = keep_rows[..., None]
     band_row = band_group[0][:, None, :].astype(jnp.float32)
     gsd_row = gsd_index[0][:, None, :].astype(jnp.float32)
-    latent, kept_pixels, kept_bands, *saved = encoder_call(
+    if direct:
+        shards, dec_embed = (to_low(dec_cols), to_low(dec_rows)), None
+    else:
+        dec_copy, dec_whole = gather_rows(dec_cols), gather_rows(dec_rows)
+        shards, dec_embed = (), dec_whole[DFF : DFF + D]
+    latent, kept_pixels, kept_bands, saved, gathered = encoder_call(
         pixels[0],
         keep_column,
         band_row,
@@ -1491,7 +1689,10 @@
         dec_embed,
         enc_gains,
         HEADS,
-    )
+        shards,
+    )
+    if direct:
+        dec_copy, dec_whole = gathered
     latent = latent.reshape(batch, K, -1)
     first_item = lax.axis_index("dp") * batch
     valid = (first_item + jnp.arange(batch, dtype=jnp.int32) < group_items[0]).astype(jnp.float32)
@@ -1504,8 +1705,7 @@
         gsd_table[0],
         pixels[0],
         dec_copy,
-        dec_down,
-        head_rows,
+        dec_whole,
         dec_gains,
         DHEADS,
     )
@@ -1528,7 +1728,7 @@
             saved,
             whole_rows,
             whole_cols,
-            dec_embed,
+            dec_whole,
             enc_gains,
             grad_dcols,
             grad_ddown,
@@ -1536,12 +1736,16 @@
             small,
             HEADS,
         )
-        flat = small.reshape(-1)
-        enc_sum = flat[:count_e].reshape(enc_gains.shape)
-        dec_sum = flat[count_e : count_e + count_d].reshape(grad_dgains.shape)
-        loss_sum = flat[count_e + count_d]
-        shard_squares = squares[0, 0]
-        shards = tuple(piece.astype(jnp.float32) for piece in shards)
+        matrices = (
+            [shards[0], enc_cols, moment_ecols, square_ecols],
+            [shards[1], enc_rows, moment_erows, square_erows],
+            [shards[2], dec_cols, moment_dcols, square_dcols],
+            [shards[3], dec_rows, moment_drows, square_drows],
+        )
+        gains = ([enc_gains, moment_egains, square_egains], [dec_gains, moment_dgains, square_dgains])
+        return adam_call(
+            jnp.stack([masked, fix_one, fix_two]).reshape(1, 3), small, squares, matrices, gains
+        )
     else:
         grad_erows, grad_ecols, grad_dembed, enc_sums = encoder_back_call(
             grad_latent,
@@ -1565,9 +1769,6 @@
     loss = loss_sum / masked
     grad_norm = jnp.sqrt(shard_squares + jnp.sum(enc_sum * enc_sum) + jnp.sum(dec_sum * dec_sum))
     factor = clip_level / jnp.maximum(grad_norm, clip_level)
-    count_steps = step_count[0].astype(jnp.float32)
-    fix_one = 1.0 - beta_first**count_steps
-    fix_two = 1.0 - beta_second**count_steps
     clipped_ecols, squares_ecols, updated_ecols = adam_step(
         enc_cols,
         moment_ecols,

time: 711 us -> 665 us (0.935)
  between operations: 21.9 us -> 2.95 us
  other arithmetic: 29.9 us -> 13 us
  local copies, waits for them, and re-layouts: 22 us -> 5.89 us
  Pallas kernels: 627 us -> 636 us
    pallas_call x1 -> x2, Pallas kernels: 53.4 us -> 94.2 us  [the longest x1 66.5 us: encoder_call(): pl.pallas_call(functools.partial(encoder_kernel, heads, chunks), grid=(12...]
    pallas_call x1, Pallas kernels: 155 us -> 138 us  [gather_call(): pl.pallas_call(functools.partial(gather_kernel, count, chunks, ahead), ou...]
    sub x6 -> x0, other arithmetic: 17.4 us -> none  [adam_step(): return (clipped, square_new, master - rate * direction)]
    pallas_call x1, Pallas kernels: 280 us -> 266 us  [back_reduce_call(): pl.pallas_call(kernel, out_shape=tuple((jax.ShapeDtypeStruct(*outs[name])...]
    slice x5 -> x0, local copies, waits for them, and re-layouts: 7.38 us -> none  [the longest x1 3.24 us: body(): dec_down = copies[3][:DFF]]
    unnamed x61 -> x2, local copies, waits for them, and re-layouts: 7.35 us -> 0.01 us
  transfers between devices with their start and end apart: 2 -> 0, of which waited for: 0 -> 0; matrix products, arithmetic and copies ran while one was open for 2% -> 0% of each run, Pallas kernels for 30% -> 0%
where the time goes in v4:
time: 665 us; the launch traced here: 658 us
  Pallas kernels  636 us (96%)
  other arithmetic  13 us (2%)
    pallas_call x1, Pallas kernels, back_reduce_call(): pl.pallas_call(kernel, out_shape=tuple((jax.ShapeDtypeStruct(*outs[name])...  266 us
    pallas_call x1, Pallas kernels, decoder_call(): pl.pallas_call(functools.partial(decoder_kernel, items, heads), grid=(bat...  138 us
    pallas_call x1, Pallas kernels, gather_call(): pl.pallas_call(functools.partial(gather_kernel, count, chunks, ahead), ou...  138 us
    pallas_call x1, Pallas kernels, encoder_call(): pl.pallas_call(functools.partial(encoder_kernel, heads, chunks), grid=(12...  66.5 us
    pallas_call x1, Pallas kernels, adam_call(): pl.pallas_call(functools.partial(adam_kernel, gains[0][0].size, gains[1][...  27.8 us

profile of v4, /device:TPU:0, one launch (start us, length us, event | category | flops | bytes accessed | tf_op | source)
XLA Modules:
  0.0 658.1 jit_solution(17005588600292697185)
XLA Ops:
  2.0 0.6 broadcast_in_dim.6.refs_2_
  2.6 0.7 convert_element_type.43
  3.3 0.7 convert_element_type.44
  4.0 0.6 copy_bitcast_fusion
  4.6 1.5 copy.49.refs_1_.keep_ref
  6.1 2.1 convert_element_type.41
  8.2 0.0 copy-start
  8.2 2.2 convert_element_type.42
  10.5 3.8 convert_element_type.34
  14.2 0.0 copy-done
  14.2 1.6 convert_element_type.33
  15.9 137.6 %shard_map.392 = (bf16[4,2,4,256,1024]{4,3,2,1,0:T(8,128)(2,1)}, bf16[4,2,4,32,8192]{4,3,2,1,0:T(8,128)(2,1)}, f32[8,128]{1,0:T(8,128)}) custom-call(bf16[4,256,1024]{2,1,0:T(8,128)(2,1)} %bitcast.40, bf16[4,32,8192]{2,1,0:T(8,128)(2,1)} %bitcast.39, f32[8,128]{1,0:T(8,128)} %broadcast_in_dim.6.refs_2_), custom_call_target="tpu_custom_call" | custom-call | tf_op jit(solution)/shard_map/pallas_call | solution.py:579
  153.4 1.2 slice.6
  155.3 0.6 maximum_bitcast_fusion.refs_0_
  155.9 0.6 pad_maximum_fusion.scal_ref
  156.5 0.6 broadcast_in_dim.7.refs_7_
  157.1 66.5 %shard_map.393 = (f32[512,512]{1,0:T(8,128)}, s32[512,1]{1,0:T(8,128)}, bf16[512,4096]{1,0:T(8,128)(2,1)}, bf16[512,4096]{1,0:T(8,128)(2,1)}, f32[512,1024]{1,0:...) custom-call(bf16[8,256,1024]{2,1,0:T(8,128)(2,1)} %bitcast.56, ...), custom_call_target="tpu_custom_call" | custom-call | flops 20000000000 | bytes 70000000 | tf_op jit(solution)/shard_map/pallas_call | solution.py:766
  223.6 138.3 %shard_map.394 = (bf16[8,64,512]{2,1,0:T(8,128)(2,1)}, bf16[512,4096]{1,0:T(8,128)(2,1)}, bf16[2048,512]{1,0:T(8,128)(2,1)}, bf16[1024,512]{1,0:T(8,128)(2,1)}, f32[8,512]{1,0:T(8,128)}, /*index=5*/f32[1,1]{1,0:T(1,128)}) custom-call(f32[2,8]{1,0:T(2,128)} %pad_maximum_fusion.scal_ref, f32[8,64,512]{2,1,0:T(8,128)} %bitcast.61, ...), custom_call_target="tpu_custom_call" | custom-call | flops 70000001024 | bytes 40000000 | tf_op jit(solution)/shard_map/pallas_call | solution.py:335
  361.8 0.7 reshape.167
  362.6 0.7 select_maximum_fusion
  363.2 0.6 reshape.168.refs_17_
  363.9 266.2 %shard_map.395 = (bf16[4,256,1024]{2,1,0:T(8,128)(2,1)}, bf16[4,32,8192]{2,1,0:T(8,128)(2,1)}, bf16[4,16,4096]{2,1,0:T(8,128)(2,1)}, bf16[4,128,512]{2,1,0:T(8,1...) custom-call(bf16[512,512]{1,0:T(8,128)(2,1)} %bitcast.51, ...), custom_call_target="tpu_custom_call" | custom-call | tf_op jit(solution)/shard_map/pallas_call | solution.py:1487
  630.0 27.8 %shard_map.396 = (f32[128,8192]{1,0:T(8,128)}, f32[128,8192]{1,0:T(8,128)}, f32[128,8192]{1,0:T(8,128)}, f32[1024,1024]{1,0:T(8,128)}, f32[1024,1024]{1,0:T(8,12...) custom-call(f32[1,3]{1,0:T(1,128)} %maximum_bitcast_fusion.refs_0_, ...), custom_call_target="tpu_custom_call" | custom-call | tf_op jit(solution)/shard_map/pallas_call | solution.py:1607
  (1 shorter events, 0.0 us)
Async XLA Ops:
  8.2 6.0 copy-start

commit v5 on v4

--- a/solution.py
+++ b/solution.py
@@ -79,14 +79,18 @@
     )
 
 
+def span(at, size):
+    return slice(at * size, (at + 1) * size)
+
+
 def attend(n, groups, tokens, width, ee, expo, same, qkv_s, s_s, p_s, inv_s, oo_s, o_s):
     item = n // groups
     g = n % groups
-    rs = pl.ds(pl.multiple_of(item * tokens, tokens), tokens)
-    qa = pl.ds(pl.multiple_of(g * LANES, LANES), LANES)
+    rs = span(item, tokens)
+    qa = span(g, LANES)
     q = qkv_s[rs, qa]
-    k = qkv_s[rs, pl.ds(pl.multiple_of(width + g * LANES, LANES), LANES)]
-    v = qkv_s[rs, pl.ds(pl.multiple_of(2 * width + g * LANES, LANES), LANES)]
+    k = qkv_s[rs, span(width // LANES + g, LANES)]
+    v = qkv_s[rs, span(2 * width // LANES + g, LANES)]
     s_s[...] = dot_nt(stack_rows(q, ee), k)
     for h in range(LANES // ee):
         at = slice(h * tokens, (h + 1) * tokens)
@@ -109,10 +113,10 @@
     low = dqkv_s.dtype
     item = n // groups
     g = n % groups
-    rs = pl.ds(pl.multiple_of(item * tokens, tokens), tokens)
-    qa = pl.ds(pl.multiple_of(g * LANES, LANES), LANES)
-    ka = pl.ds(pl.multiple_of(width + g * LANES, LANES), LANES)
-    va = pl.ds(pl.multiple_of(2 * width + g * LANES, LANES), LANES)
+    rs = span(item, tokens)
+    qa = span(g, LANES)
+    ka = span(width // LANES + g, LANES)
+    va = span(2 * width // LANES + g, LANES)
     heads = range(LANES // ee)
     do = do_s[rs, qa].astype(jnp.float32) * inv_s[slot]
     rest = (-do * oo_s[slot]).astype(low)
@@ -201,26 +205,23 @@
     hat, _ = unit_rows(x_s[...])
     h1_s[...] = (hat * gain(0) + gain(1)).astype(low)
 
-    @pl.loop(0, 3)
-    def _(t):
-        at = pl.ds(pl.multiple_of(t * width, width), width)
+    for t in range(3):
+        at = slice(t * width, (t + 1) * width)
         qkv_s[:, at] = dot_nn(h1_s[...], cols_ref[:, at]).astype(low)
 
     groups = width // LANES
 
-    @pl.loop(0, items * groups)
-    def _(n):
-        attend(n, groups, tokens, width, ee, expo, None, qkv_s, s_s, p_s, inv_s, oo_s, o_s)
+    for n in range(items * groups):
+        attend(n, groups, tokens, width, ee, expo, None, qkv_s, s_s.at[n % 2], p_s, inv_s, oo_s, o_s)
 
     x1_s[...] = x_s[...] + dot_nn(o_s[...], cols_ref[:, 3 * width : 4 * width])
     hat, _ = unit_rows(x1_s[...])
     h2_s[...] = (hat * gain(2) + gain(3)).astype(low)
     x2_s[...] = x1_s[...]
 
-    @pl.loop(0, down_ref.shape[0] // tile)
-    def _(t):
-        at = pl.ds(pl.multiple_of(t * tile, tile), tile)
-        up = pl.ds(pl.multiple_of(4 * width + t * tile, tile), tile)
+    for t in range(down_ref.shape[0] // tile):
+        at = slice(t * tile, (t + 1) * tile)
+        up = slice(4 * width + t * tile, 4 * width + (t + 1) * tile)
         u = dot_nn(h2_s[...], cols_ref[:, up])
         cumul = 0.5 * (1.0 + lax.erf(u * 0.7071067811865476))
         act = (u * cumul).astype(low)
@@ -257,10 +258,9 @@
 
     acc_s[...] = jnp.zeros_like(acc_s)
 
-    @pl.loop(0, down_ref.shape[0] // tile)
-    def _(t):
-        at = pl.ds(pl.multiple_of(t * tile, tile), tile)
-        up = pl.ds(pl.multiple_of(4 * width + t * tile, tile), tile)
+    for t in range(down_ref.shape[0] // tile):
+        at = slice(t * tile, (t + 1) * tile)
+        up = slice(4 * width + t * tile, 4 * width + (t + 1) * tile)
         gdown[at, :] += dot_tn(a_s[:, at], dy_s[...])
         du = (dot_nt(dy_s[...], down_ref[at, :]) * gp_s[:, at].astype(jnp.float32)).astype(low)
         gcols[:, up] += dot_tn(h2_s[...], du)
@@ -275,15 +275,16 @@
     gcols[:, 3 * width : 4 * width] += dot_tn(o_s[...], dy_s[...])
     o_s[...] = dot_nt(dy_s[...], cols_ref[:, 3 * width : 4 * width]).astype(low)
 
-    @pl.loop(0, items * groups)
-    def _(n):
-        attend_back(n, n, groups, tokens, width, ee, scale, qkv_s, s_s, ds_s, p_s, inv_s, oo_s, o_s, dqkv_s)
+    for n in range(items * groups):
+        attend_back(
+            n, n, groups, tokens, width, ee, scale, qkv_s, s_s.at[n % 2], ds_s.at[n % 2], p_s, inv_s, oo_s, o_s,
+            dqkv_s,
+        )
 
     acc_s[...] = jnp.zeros_like(acc_s)
 
-    @pl.loop(0, 3)
-    def _(t):
-        at = pl.ds(pl.multiple_of(t * width, width), width)
+    for t in range(3):
+        at = slice(t * width, (t + 1) * width)
         gcols[:, at] += dot_tn(h1_s[...], dqkv_s[:, at])
         acc_s[...] += dot_nt(dqkv_s[:, at], cols_ref[:, at])
 
@@ -367,8 +368,8 @@
             vmem((run, 3 * width), low),
             vmem((items * width // 128, tokens, 128), f32),
             vmem((items * width // 128, tokens, 128), f32),
-            vmem((4 * tokens, tokens), f32),
-            vmem((tokens, 4 * tokens), low),
+            vmem((2, 4 * tokens, tokens), f32),
+            vmem((2, tokens, 4 * tokens), low),
             vmem((table.shape[0], width), low),
             vmem((table.shape[0], width), low),
             vmem((items, hide, pixel_count), low),
@@ -377,7 +378,7 @@
             vmem(head.shape, f32),
         ],
         compiler_params=pltpu.CompilerParams(
-            dimension_semantics=("arbitrary",), vmem_limit_bytes=62 * 1024 * 1024
+            dimension_semantics=("arbitrary",), vmem_limit_bytes=63 * 1024 * 1024
         ),
         cost_estimate=pl.CostEstimate(
             flops=70_000_000_000, bytes_accessed=40_000_000, transcendentals=20_000_000
@@ -680,9 +681,8 @@
         store(2).start()
         same = same_item()
 
-        @pl.loop(0, x_ref.shape[0] // RUN * groups)
-        def _(n):
-            attend(n, groups, RUN, width, ee, expo, same, qkv_ref, s_s, p_ref, inv_ref, oo_ref, o_s)
+        for n in range(x_ref.shape[0] // RUN * groups):
+            attend(n, groups, RUN, width, ee, expo, same, qkv_ref, s_s.at[n % 2], p_ref, inv_ref, oo_ref, o_s)
 
         for i in (3, 4, 5, 7):
             store(i).start()
@@ -694,10 +694,9 @@
 
     @pl.when(step >= 8)
     def _():
-        @pl.loop(0, 2)
-        def _(t):
-            half = width // 2
-            at = pl.ds(pl.multiple_of(t * half, half), half)
+        half = width // 2
+        for t in range(2):
+            at = slice(t * half, (t + 1) * half)
             u = dot_nn(h_s[...], cols_ref[:, at])
             cumul = 0.5 * (1.0 + lax.erf(u * 0.7071067811865476))
             a_ref[:, at] = (u * cumul).astype(low)
@@ -785,7 +784,7 @@
         scratch_shapes=[vmem(*h) for h in held]
         + [
             vmem((tokens, width), low),
-            vmem((wide, RUN), f32),
+            vmem((2, wide, RUN), f32),
             vmem((table.shape[0], width), low),
             vmem((table.shape[0], width), low),
             vmem(de_shape, low),
@@ -865,8 +864,7 @@
         gcols_ref[...] = dot_tn(h_s[...], dy_s[...]).astype(low)
         do_s[...] = dot_nt(dy_s[...], cols_ref[...]).astype(low)
 
-        @pl.loop(0, runs * groups)
-        def _(n):
+        for n in range(runs * groups):
             attend_back(
                 n, n, groups, RUN, width, ee, ee ** (-0.5), qkv_ref, s_s, ds_s, p_ref, inv_ref, oo_ref, do_s,
                 dqkv_s,
@@ -1321,19 +1319,15 @@
         for copy in attention_loads(first):
             copy.start()
 
-        @pl.loop(0, count)
-        def _(i):
-            n = first + i
+        for n in range(first, first + count):
             for copy in attention_loads(n):
                 copy.wait()
-
-            @pl.when(i + 1 < count)
-            def _():
+            if n + 1 < first + count:
                 for copy in attention_loads(n + 1):
                     copy.start()
-
             attend_back(
-                n, n % 2, groups, RUN, width, ee, ee ** (-0.5), wide, s_s, ds_s, p_t, inv_t, oo_t, h, wide
+                n, n % 2, groups, RUN, width, ee, ee ** (-0.5), wide, s_s.at[n % 2], ds_s.at[n % 2], p_t, inv_t,
+                oo_t, h, wide,
             )
 
     def input_piece(t):
@@ -1508,8 +1502,8 @@
             vmem((2,) + p.shape[1:], low),
             vmem((2,) + inv.shape[1:], f32),
             vmem((2,) + oo.shape[1:], f32),
-            vmem((p.shape[2], RUN), f32),
-            vmem((RUN, p.shape[2]), low),
+            vmem((2, p.shape[2], RUN), f32),
+            vmem((2, RUN, p.shape[2]), low),
             vmem((8, width), f32),
             sems((steps, 3)), sems((steps, 3)), sems((steps, 4)), sems((steps, 3)),
             sems((steps, 4)), sems((steps, 4)),

time: 665 us -> 620 us (0.932)
  Pallas kernels: 636 us -> 593 us
    pallas_call x1, Pallas kernels: 138 us -> 99.9 us  [decoder_call(): pl.pallas_call(functools.partial(decoder_kernel, items, heads), grid=(bat...]
where the time goes in v5:
time: 620 us; the launch traced here: 615 us
  Pallas kernels  593 us (96%)
  other arithmetic  13 us (2%)
    pallas_call x1, Pallas kernels, back_reduce_call(): pl.pallas_call(kernel, out_shape=tuple((jax.ShapeDtypeStruct(*outs[name])...  268 us
    pallas_call x1, Pallas kernels, gather_call(): pl.pallas_call(functools.partial(gather_kernel, count, chunks, ahead), ou...  138 us
    pallas_call x1, Pallas kernels, decoder_call(): pl.pallas_call(functools.partial(decoder_kernel, items, heads), grid=(bat...  99.9 us
    pallas_call x1, Pallas kernels, encoder_call(): pl.pallas_call(functools.partial(encoder_kernel, heads, chunks), grid=(12...  60.4 us
    pallas_call x1, Pallas kernels, adam_call(): pl.pallas_call(functools.partial(adam_kernel, gains[0][0].size, gains[1][...  27.8 us

profile of v5, /device:TPU:0, one launch (start us, length us, event | category | flops | bytes accessed | tf_op | source)
XLA Modules:
  0.0 615.1 jit_solution(18440822692163797902)
XLA Ops:
  2.0 0.6 broadcast_in_dim.6.refs_2_
  2.6 0.7 convert_element_type.43
  3.3 0.7 convert_element_type.44
  4.0 0.6 copy_bitcast_fusion
  4.6 1.5 copy.49.refs_1_.keep_ref
  6.1 2.1 convert_element_type.41
  8.2 0.0 copy-start
  8.2 2.2 convert_element_type.42
  10.5 3.8 convert_element_type.34
  14.2 0.0 copy-done
  14.2 1.6 convert_element_type.33
  15.9 137.6 %shard_map.392 = (bf16[4,2,4,256,1024]{4,3,2,1,0:T(8,128)(2,1)}, bf16[4,2,4,32,8192]{4,3,2,1,0:T(8,128)(2,1)}, f32[8,128]{1,0:T(8,128)}) custom-call(bf16[4,256,1024]{2,1,0:T(8,128)(2,1)} %bitcast.40, bf16[4,32,8192]{2,1,0:T(8,128)(2,1)} %bitcast.39, f32[8,128]{1,0:T(8,128)} %broadcast_in_dim.6.refs_2_), custom_call_target="tpu_custom_call" | custom-call | tf_op jit(solution)/shard_map/pallas_call | solution.py:580
  153.4 1.2 slice.6
  155.3 0.6 maximum_bitcast_fusion.refs_0_
  155.9 0.6 pad_maximum_fusion.scal_ref
  156.5 0.6 broadcast_in_dim.7.refs_7_
  157.1 60.4 %shard_map.393 = (f32[512,512]{1,0:T(8,128)}, s32[512,1]{1,0:T(8,128)}, bf16[512,4096]{1,0:T(8,128)(2,1)}, bf16[512,4096]{1,0:T(8,128)(2,1)}, f32[512,1024]{1,0:...) custom-call(bf16[8,256,1024]{2,1,0:T(8,128)(2,1)} %bitcast.56, ...), custom_call_target="tpu_custom_call" | custom-call | flops 20000000000 | bytes 70000000 | tf_op jit(solution)/shard_map/pallas_call | solution.py:765
  217.5 99.9 %shard_map.394 = (bf16[8,64,512]{2,1,0:T(8,128)(2,1)}, bf16[512,4096]{1,0:T(8,128)(2,1)}, bf16[2048,512]{1,0:T(8,128)(2,1)}, bf16[1024,512]{1,0:T(8,128)(2,1)}, f32[8,512]{1,0:T(8,128)}, /*index=5*/f32[1,1]{1,0:T(1,128)}) custom-call(f32[2,8]{1,0:T(2,128)} %pad_maximum_fusion.scal_ref, f32[8,64,512]{2,1,0:T(8,128)} %bitcast.61, ...), custom_call_target="tpu_custom_call" | custom-call | flops 70000001024 | bytes 40000000 | tf_op jit(solution)/shard_map/pallas_call | solution.py:336
  317.4 0.7 reshape.167
  318.1 0.7 select_maximum_fusion
  318.8 0.6 reshape.168.refs_17_
  319.4 267.6 %shard_map.395 = (bf16[4,256,1024]{2,1,0:T(8,128)(2,1)}, bf16[4,32,8192]{2,1,0:T(8,128)(2,1)}, bf16[4,16,4096]{2,1,0:T(8,128)(2,1)}, bf16[4,128,512]{2,1,0:T(8,1...) custom-call(bf16[512,512]{1,0:T(8,128)(2,1)} %bitcast.51, ...), custom_call_target="tpu_custom_call" | custom-call | tf_op jit(solution)/shard_map/pallas_call | solution.py:1481
  587.0 27.8 %shard_map.396 = (f32[128,8192]{1,0:T(8,128)}, f32[128,8192]{1,0:T(8,128)}, f32[128,8192]{1,0:T(8,128)}, f32[1024,1024]{1,0:T(8,128)}, f32[1024,1024]{1,0:T(8,12...) custom-call(f32[1,3]{1,0:T(1,128)} %maximum_bitcast_fusion.refs_0_, ...), custom_call_target="tpu_custom_call" | custom-call | tf_op jit(solution)/shard_map/pallas_call | solution.py:1601
  (1 shorter events, 0.0 us)
Async XLA Ops:
  8.2 6.0 copy-start

commit v6 on v5

--- a/solution.py
+++ b/solution.py
@@ -198,7 +198,7 @@
         rank = dot_nn(jnp.broadcast_to(1.0 - shown, (8, tokens)).astype(low), before)[:1]
         slot = lax.broadcasted_iota(jnp.int32, (hide, tokens), 0).astype(f32) + 1.0
         hide_hot = jnp.where(slot == rank, 1.0 - shown, 0.0)
-        position = look_up(jnp.concatenate([keep_hot, hide_hot], 0), gsd_ref[i], high_s, low_s)
+        position = look_up(jnp.concatenate([keep_hot, hide_hot], 0), gsd_ref[i].astype(f32), high_s, low_s)
         x_s[base : base + K, :] = position[:K] + z_ref[i]
         x_s[base + K : base + tokens, :] = position[K:] + gain(6)
         pixel_s[i] = dot_nn(hide_hot.astype(low), pix_ref[i]).astype(low)
@@ -488,11 +488,13 @@
         return send(ins[array], outs[array].at[z, c], os.at[array], cr.at[array], sib)
 
     def begin():
-        for array in range(count):
-            own(array).start()
         for k in range(min(ahead, steps)):
             for j in range(3):
                 go(functools.partial(zcopy, k, j))
+
+    def begin_own():
+        for array in range(count):
+            own(array).start()
         for array in range(count):
             go(functools.partial(own_to_core, array))
 
@@ -530,7 +532,7 @@
             send(whole, whole, os.at[array], cr.at[array], sib).wait_recv()
             own(array).wait()
 
-    return peers, begin, [functools.partial(event, t) for t in range(steps + 2)], finish
+    return peers, begin, begin_own, [functools.partial(event, t) for t in range(steps + 2)], finish
 
 
 def gather_scratch(count, steps):
@@ -542,8 +544,27 @@
     ins, items_ref = refs[:count], refs[count]
     outs, items_out = refs[count + 1 : 2 * count + 1], refs[2 * count + 1]
     sems = refs[2 * count + 2 :]
-    it, its, itr = sems[GATHER_SEMS:]
-    peers, begin, events, finish = gather_events(count, chunks, ahead, ins, outs, sems[:GATHER_SEMS])
+    it, its, itr, load_sem = sems[GATHER_SEMS : GATHER_SEMS + 4]
+    wide = sems[GATHER_SEMS + 4 : GATHER_SEMS + 4 + count]
+    masters, ins = ins, sems[GATHER_SEMS + 4 + count :]
+    parts = [(array, cut) for array in range(count) for cut in pieces(ins[array].shape[1:], chunks[array])]
+    loads = [
+        pltpu.make_async_copy(
+            masters[array].at[:, cut[0], cut[1]], wide[array].at[:, cut[0], cut[1]], load_sem.at[i]
+        )
+        for i, (array, cut) in enumerate(parts)
+    ]
+    for load in loads:
+        load.start()
+    peers, begin, begin_own, events, finish = gather_events(
+        count, chunks, ahead, ins, outs, sems[:GATHER_SEMS]
+    )
+
+    def narrow(i):
+        array, cut = parts[i]
+        loads[i].wait()
+        ins[array][:, cut[0], cut[1]] = wide[array][:, cut[0], cut[1]].astype(ins[array].dtype)
+
     greet(peers)
     _, right, up = peers[:3]
 
@@ -555,7 +576,12 @@
 
     it[0] = items_ref[...]
     items_copy(0, right).start()
+    for i in range(ahead):
+        narrow(i)
     begin()
+    for i in range(ahead, len(parts)):
+        narrow(i)
+    begin_own()
     for t, event in enumerate(events):
         event()
         if t == 0:
@@ -579,13 +605,17 @@
     vm = pl.BlockSpec(memory_space=pltpu.VMEM)
     *outs, total = pl.pallas_call(
         functools.partial(gather_kernel, count, chunks, ahead),
-        out_shape=tuple(jax.ShapeDtypeStruct((4, 2) + v.shape, v.dtype) for v in views)
+        out_shape=tuple(jax.ShapeDtypeStruct((4, 2) + v.shape, jnp.bfloat16) for v in views)
         + (jax.ShapeDtypeStruct((8, 128), jnp.float32),),
         in_specs=[hbm] * count + [vm],
         out_specs=tuple([hbm] * count + [vm]),
         scratch_shapes=gather_scratch(count, steps)
-        + [pltpu.VMEM((4, 8, 128), jnp.float32), dma((2,)), dma((2,))],
-        compiler_params=pltpu.CompilerParams(collective_id=collective_id, has_side_effects=True),
+        + [pltpu.VMEM((4, 8, 128), jnp.float32), dma((2,)), dma((2,)), dma((steps,))]
+        + [pltpu.VMEM(v.shape, jnp.float32) for v in views]
+        + [pltpu.VMEM(v.shape, jnp.bfloat16) for v in views],
+        compiler_params=pltpu.CompilerParams(
+            collective_id=collective_id, has_side_effects=True, vmem_limit_bytes=60 * 1024 * 1024
+        ),
     )(*views, jnp.broadcast_to(items, (8, 128)))
     return [o.reshape(-1, o.shape[-1]) for o in outs], total[0, 0]
 
@@ -617,8 +647,11 @@
     groups = width // LANES
     expo = ee ** (-0.5) * 1.4426950408889634
     if chunks:
-        peers, begin, events, finish = gather_events(
-            count, chunks, 2, shards, gathered, rest[15 : 15 + GATHER_SEMS]
+        low_shards = rest[15 + GATHER_SEMS : 17 + GATHER_SEMS]
+        wide_shards = rest[17 + GATHER_SEMS : 19 + GATHER_SEMS]
+        shard_sem = rest[19 + GATHER_SEMS]
+        peers, begin, begin_own, events, finish = gather_events(
+            count, chunks, 2, low_shards, gathered, rest[15 : 15 + GATHER_SEMS]
         )
 
     def gain(i):
@@ -634,8 +667,17 @@
 
         @pl.when(step == 0)
         def _():
+            loads = [
+                pltpu.make_async_copy(shards[i], wide_shards[i], shard_sem.at[i]) for i in range(count)
+            ]
+            for load in loads:
+                load.start()
             greet(peers)
+            for i in range(count):
+                loads[i].wait()
+                low_shards[i][...] = wide_shards[i][...].astype(low)
             begin()
+            begin_own()
 
         for at, event in zip((3, 6, 7, 8, 9, 10), events):
             pl.when(step == at)(event)
@@ -655,8 +697,8 @@
             at = pl.ds(pl.multiple_of(i * K, K), K)
             hot = one_hot(keep_ref[i], pixels_ref.shape[1])
             pix_ref[at, :] = dot_nn(hot.astype(low), pixels_ref[i]).astype(low)
-            band_ref[at, :] = jnp.sum(hot * bands_ref[i], -1, keepdims=True).astype(jnp.int32)
-            x_ref[at, :] = look_up(hot, gsd_ref[i], high_s, low_s)
+            band_ref[at, :] = jnp.sum(hot * bands_ref[i].astype(jnp.float32), -1, keepdims=True).astype(jnp.int32)
+            x_ref[at, :] = look_up(hot, gsd_ref[i].astype(jnp.float32), high_s, low_s)
 
         store(0).start()
 
@@ -791,7 +833,10 @@
             pltpu.SemaphoreType.DMA((8,)),
             pltpu.SemaphoreType.DMA,
         ]
-        + (gather_scratch(2, sum(chunks)) if shards else []),
+        + (gather_scratch(2, sum(chunks)) if shards else [])
+        + [vmem(v.shape, low) for v in views]
+        + [vmem(v.shape, f32) for v in views]
+        + ([pltpu.SemaphoreType.DMA((2,))] if shards else []),
         compiler_params=pltpu.CompilerParams(
             dimension_semantics=("arbitrary",),
             vmem_limit_bytes=60 * 1024 * 1024,
@@ -1653,7 +1698,7 @@
     own_count = jnp.sum(group_items.astype(jnp.float32))
     if direct:
         (whole_rows, whole_cols), total_count = gather_call(
-            [to_low(enc_rows), to_low(enc_cols)], own_count, (4, 4), 2, 0
+            [enc_rows, enc_cols], own_count, (4, 4), 2, 0
         )
     else:
         total_count = lax.psum(own_count, "grp")
@@ -1665,10 +1710,10 @@
     keep_rows = keep_index[0]
     batch = keep_rows.shape[0]
     keep_column = keep_rows[..., None]
-    band_row = band_group[0][:, None, :].astype(jnp.float32)
-    gsd_row = gsd_index[0][:, None, :].astype(jnp.float32)
+    band_row = band_group[0][:, None, :]
+    gsd_row = gsd_index[0][:, None, :]
     if direct:
-        shards, dec_embed = (to_low(dec_cols), to_low(dec_rows)), None
+        shards, dec_embed = (dec_cols, dec_rows), None
     else:
         dec_copy, dec_whole = gather_rows(dec_cols), gather_rows(dec_rows)
         shards, dec_embed = (), dec_whole[DFF : DFF + D]

time: 620 us -> 611 us (0.985)
  other arithmetic: 13 us -> 1.85 us
    convert_element_type x6 -> x0, other arithmetic: 11.1 us -> none  [the longest x4 9.71 us: to_low(): return value.astype(jnp.bfloat16)]
    pallas_call x1, Pallas kernels: 60.4 us -> 71.3 us  [encoder_call(): pl.pallas_call(functools.partial(encoder_kernel, heads, chunks), grid=(12...]
    pallas_call x1, Pallas kernels: 138 us -> 127 us  [gather_call(): pl.pallas_call(functools.partial(gather_kernel, count, chunks, ahead), ou...]
where the time goes in v6:
time: 611 us; the launch traced here: 606 us
  Pallas kernels  594 us (97%)
  local copies, waits for them, and re-layouts  7.87 us (1%)
    pallas_call x1, Pallas kernels, back_reduce_call(): pl.pallas_call(kernel, out_shape=tuple((jax.ShapeDtypeStruct(*outs[name])...  267 us
    pallas_call x1, Pallas kernels, gather_call(): pl.pallas_call(functools.partial(gather_kernel, count, chunks, ahead), ou...  127 us
    pallas_call x1, Pallas kernels, decoder_call(): pl.pallas_call(functools.partial(decoder_kernel, items, heads), grid=(bat...  99.8 us
    pallas_call x1, Pallas kernels, encoder_call(): pl.pallas_call(functools.partial(encoder_kernel, heads, chunks), grid=(12...  71.3 us
    pallas_call x1, Pallas kernels, adam_call(): pl.pallas_call(functools.partial(adam_kernel, gains[0][0].size, gains[1][...  27.8 us

profile of v6, /device:TPU:0, one launch (start us, length us, event | category | flops | bytes accessed | tf_op | source)
XLA Modules:
  0.0 606.2 jit_solution(13198018545896292717)
XLA Ops:
  2.0 0.6 broadcast_in_dim.6.refs_2_
  2.6 1.3 broadcast_in_dim_squeeze.14.refs_3_.gsd_ref
  3.9 1.3 broadcast_in_dim_squeeze.13.refs_2_
  5.2 1.5 copy.45.refs_1_.keep_ref
  6.7 127.2 %shard_map.392 = (bf16[4,2,4,256,1024]{4,3,2,1,0:T(8,128)(2,1)}, bf16[4,2,4,32,8192]{4,3,2,1,0:T(8,128)(2,1)}, f32[8,128]{1,0:T(8,128)}) custom-call(f32[4,256,1024]{2,1,0:T(8,128)} %bitcast.35, f32[4,32,8192]{2,1,0:T(8,128)} %bitcast.36, f32[8,128]{1,0:T(8,128)} %broadcast_in_dim.6.refs_2_), custom_call_target="tpu_custom_call" | custom-call | tf_op jit(solution)/shard_map/pallas_call | solution.py:606
  134.0 1.2 slice.6
  135.8 0.6 maximum_bitcast_fusion.refs_0_
  136.4 0.6 pad_maximum_fusion.scal_ref
  137.0 0.6 broadcast_in_dim.7.refs_7_
  137.6 71.3 %shard_map.393 = (f32[512,512]{1,0:T(8,128)}, s32[512,1]{1,0:T(8,128)}, bf16[512,4096]{1,0:T(8,128)(2,1)}, bf16[512,4096]{1,0:T(8,128)(2,1)}, f32[512,1024]{1,0:...) custom-call(bf16[8,256,1024]{2,1,0:T(8,128)(2,1)} %bitcast.52, ...), custom_call_target="tpu_custom_call" | custom-call | flops 20000000000 | bytes 70000000 | tf_op jit(solution)/shard_map/pallas_call | solution.py:807
  208.9 99.8 %shard_map.394 = (bf16[8,64,512]{2,1,0:T(8,128)(2,1)}, bf16[512,4096]{1,0:T(8,128)(2,1)}, bf16[2048,512]{1,0:T(8,128)(2,1)}, bf16[1024,512]{1,0:T(8,128)(2,1)}, f32[8,512]{1,0:T(8,128)}, /*index=5*/f32[1,1]{1,0:T(1,128)}) custom-call(f32[2,8]{1,0:T(2,128)} %pad_maximum_fusion.scal_ref, f32[8,64,512]{2,1,0:T(8,128)} %bitcast.57, ...), custom_call_target="tpu_custom_call" | custom-call | flops 70000001024 | bytes 40000000 | tf_op jit(solution)/shard_map/pallas_call | solution.py:336
  308.7 0.7 reshape.141
  309.4 0.7 select_maximum_fusion
  310.1 0.6 reshape.142.refs_17_
  310.7 267.4 %shard_map.395 = (bf16[4,256,1024]{2,1,0:T(8,128)(2,1)}, bf16[4,32,8192]{2,1,0:T(8,128)(2,1)}, bf16[4,16,4096]{2,1,0:T(8,128)(2,1)}, bf16[4,128,512]{2,1,0:T(8,1...) custom-call(bf16[512,512]{1,0:T(8,128)(2,1)} %bitcast.49, ...), custom_call_target="tpu_custom_call" | custom-call | tf_op jit(solution)/shard_map/pallas_call | solution.py:1526
  578.1 27.8 %shard_map.396 = (f32[128,8192]{1,0:T(8,128)}, f32[128,8192]{1,0:T(8,128)}, f32[128,8192]{1,0:T(8,128)}, f32[1024,1024]{1,0:T(8,128)}, f32[1024,1024]{1,0:T(8,12...) custom-call(f32[1,3]{1,0:T(1,128)} %maximum_bitcast_fusion.refs_0_, ...), custom_call_target="tpu_custom_call" | custom-call | tf_op jit(solution)/shard_map/pallas_call | solution.py:1646
  (1 shorter events, 0.0 us)

commit v7 on v6

--- a/solution.py
+++ b/solution.py
@@ -679,7 +679,7 @@
             begin()
             begin_own()
 
-        for at, event in zip((3, 6, 7, 8, 9, 10), events):
+        for at, event in zip((3, 5, 7, 8, 9, 10), events):
             pl.when(step == at)(event)
 
     @pl.when(step == 11)
@@ -1416,13 +1416,13 @@
     squared = max(w[6] + 4 for w in work)
     compute_end = max(t for t, _, _ in pieces)
     for t in range(last + 1):
+        done("out_r", "out_c", "out_e")
         for i in (1, 6, 5, 4, 3, 2, 0):
             for k in range(steps):
                 if work[k][6] + i == t:
                     stages[i](k)
         if t == 0:
             first_loads()
-        done("out_r", "out_c", "out_e")
         for k in range(steps):
             if work[k][7] == t:
                 go(c_copies(k))
@@ -1486,8 +1486,8 @@
     chunks += [column_chunk(i, 4 + i) for i in range(4)]
     chunks += [column_chunk(4 + i, block) for i, block in enumerate((3, 0, 1, 2))]
     chunks += [row_chunk(8 + i, i) for i in range(8)]
-    starts = (0, 1, 3, 4, 5, 6, 7, 8, 9, 11, 12, 13) + tuple(range(14, 22))
-    begins = (0, 0, 2, 2, 3, 4, 5, 6, 7, 10, 10, 11) + tuple(range(13, 21))
+    starts = (0, 1, 2, 3, 4, 5, 6, 7, 8, 10, 11, 12) + tuple(range(13, 21))
+    begins = (0, 0, 2, 2, 3, 4, 5, 6, 7, 10, 10, 11) + (13,) + tuple(range(13, 20))
     work = tuple(chunk + (starts[i], begins[i]) for i, chunk in enumerate(chunks))
     pieces = [(1, "head", 0)] + [(2 + s, "hidden", s) for s in range(4)] + [(6, "middle", 0)]
     pieces += [(7 + i // 2, "attention", i) for i in range(4)]

time: 611 us -> 602 us (0.985)
  Pallas kernels: 594 us -> 584 us
    pallas_call x1, Pallas kernels: 267 us -> 260 us  [back_reduce_call(): pl.pallas_call(kernel, out_shape=tuple((jax.ShapeDtypeStruct(*outs[name])...]
where the time goes in v7:
time: 602 us; the launch traced here: 597 us
  Pallas kernels  584 us (97%)
  local copies, waits for them, and re-layouts  7.87 us (1%)
    pallas_call x1, Pallas kernels, back_reduce_call(): pl.pallas_call(kernel, out_shape=tuple((jax.ShapeDtypeStruct(*outs[name])...  260 us
    pallas_call x1, Pallas kernels, gather_call(): pl.pallas_call(functools.partial(gather_kernel, count, chunks, ahead), ou...  127 us
    pallas_call x1, Pallas kernels, decoder_call(): pl.pallas_call(functools.partial(decoder_kernel, items, heads), grid=(bat...  99.8 us
    pallas_call x1, Pallas kernels, encoder_call(): pl.pallas_call(functools.partial(encoder_kernel, heads, chunks), grid=(12...  69.7 us
    pallas_call x1, Pallas kernels, adam_call(): pl.pallas_call(functools.partial(adam_kernel, gains[0][0].size, gains[1][...  27.8 us

profile of v7, /device:TPU:0, one launch (start us, length us, event | category | flops | bytes accessed | tf_op | source)
XLA Modules:
  0.0 596.8 jit_solution(4862669278481035467)
XLA Ops:
  2.0 0.6 broadcast_in_dim.6.refs_2_
  2.6 1.3 broadcast_in_dim_squeeze.14.refs_3_.gsd_ref
  3.9 1.3 broadcast_in_dim_squeeze.13.refs_2_
  5.2 1.5 copy.45.refs_1_.keep_ref
  6.7 127.2 %shard_map.392 = (bf16[4,2,4,256,1024]{4,3,2,1,0:T(8,128)(2,1)}, bf16[4,2,4,32,8192]{4,3,2,1,0:T(8,128)(2,1)}, f32[8,128]{1,0:T(8,128)}) custom-call(f32[4,256,1024]{2,1,0:T(8,128)} %bitcast.35, f32[4,32,8192]{2,1,0:T(8,128)} %bitcast.36, f32[8,128]{1,0:T(8,128)} %broadcast_in_dim.6.refs_2_), custom_call_target="tpu_custom_call" | custom-call | tf_op jit(solution)/shard_map/pallas_call | solution.py:606
  134.0 1.2 slice.6
  135.8 0.6 maximum_bitcast_fusion.refs_0_
  136.4 0.6 pad_maximum_fusion.scal_ref
  137.0 0.6 broadcast_in_dim.7.refs_7_
  137.6 69.7 %shard_map.393 = (f32[512,512]{1,0:T(8,128)}, s32[512,1]{1,0:T(8,128)}, bf16[512,4096]{1,0:T(8,128)(2,1)}, bf16[512,4096]{1,0:T(8,128)(2,1)}, f32[512,1024]{1,0:...) custom-call(bf16[8,256,1024]{2,1,0:T(8,128)(2,1)} %bitcast.52, ...), custom_call_target="tpu_custom_call" | custom-call | flops 20000000000 | bytes 70000000 | tf_op jit(solution)/shard_map/pallas_call | solution.py:807
  207.3 99.8 %shard_map.394 = (bf16[8,64,512]{2,1,0:T(8,128)(2,1)}, bf16[512,4096]{1,0:T(8,128)(2,1)}, bf16[2048,512]{1,0:T(8,128)(2,1)}, bf16[1024,512]{1,0:T(8,128)(2,1)}, f32[8,512]{1,0:T(8,128)}, /*index=5*/f32[1,1]{1,0:T(1,128)}) custom-call(f32[2,8]{1,0:T(2,128)} %pad_maximum_fusion.scal_ref, f32[8,64,512]{2,1,0:T(8,128)} %bitcast.57, ...), custom_call_target="tpu_custom_call" | custom-call | flops 70000001024 | bytes 40000000 | tf_op jit(solution)/shard_map/pallas_call | solution.py:336
  307.1 0.7 reshape.141
  307.8 0.7 select_maximum_fusion
  308.5 0.6 reshape.142.refs_17_
  309.1 259.5 %shard_map.395 = (bf16[4,256,1024]{2,1,0:T(8,128)(2,1)}, bf16[4,32,8192]{2,1,0:T(8,128)(2,1)}, bf16[4,16,4096]{2,1,0:T(8,128)(2,1)}, bf16[4,128,512]{2,1,0:T(8,1...) custom-call(bf16[512,512]{1,0:T(8,128)(2,1)} %bitcast.49, ...), custom_call_target="tpu_custom_call" | custom-call | tf_op jit(solution)/shard_map/pallas_call | solution.py:1526
  568.7 27.8 %shard_map.396 = (f32[128,8192]{1,0:T(8,128)}, f32[128,8192]{1,0:T(8,128)}, f32[128,8192]{1,0:T(8,128)}, f32[1024,1024]{1,0:T(8,128)}, f32[1024,1024]{1,0:T(8,12...) custom-call(f32[1,3]{1,0:T(1,128)} %maximum_bitcast_fusion.refs_0_, ...), custom_call_target="tpu_custom_call" | custom-call | tf_op jit(solution)/shard_map/pallas_call | solution.py:1646
  (1 shorter events, 0.0 us)
